TPU v7x, 32 devices: a whole 2x2x4 slice. The times are simulated.
32 devices in a mesh: win: 4 (over x, core), src: 8 (over z, y).
Axes of the slice: x: 2, y: 2, z: 4, core: 2. Of those that a mesh axis runs over, the one named last changes fastest.
Arguments:
- strain: bfloat16 [6144, 10240], P('win', 'src'), may hold values from -1000 to 1000
- dead_mask: int32 [4, 10240], P('win', 'src'), may hold values 0 or 1
- src_index: int32 [256], replicated, may hold values from 0 to 10239
Outputs:
- correlations: float32 [4, 256, 32, 10240], P('win', 'src')
All inputs are finite; a program needn't handle non-finite values. No bound on the sum of `dead_mask` on one device may be relied on, other than what follows from the above.
Results may differ from a plain program's by a relative error of at most 0.0041.
Values may be sent and summed in bfloat16 or wider, within the bound.
No kernel may reach another device: no remote copies, remote signals or barrier semaphores. Data moves between devices by JAX's collectives and lax.ppermute only.
A program may use at most 192 MiB of HBM per device.

v0:
```python
import functools
import math

import jax
import jax.numpy as jnp
from jax import lax
from jax.experimental import pallas as pl
from jax.experimental.pallas import tpu as pltpu
from jax.sharding import PartitionSpec as P


LAGS = 32
HALF = 32
EPSILON = 1e-05
TILE = 192
SPAN = 2 * HALF
ROWS = 512
VMEM_BYTES = 24 << 20

WIDTHS = (384, 512, 256, 128)
EARLY = (0, 1, 2, 3)
LATE = (1, 0, 2, 3)
STEPS = (
    [(0, c) for c in EARLY[1:]]
    + [(1, c) for c in EARLY]
    + [(2, c) for c in LATE]
    + [(3, c) for c in LATE]
)
STORED = {(1, 3): 4, (2, 1): 3, (2, 2): 1, (2, 3): 3, (3, 0): 1}


def passed_along(array, axis, by):
    devices = lax.axis_size(axis)
    pairs = [(i, i + by) for i in range(devices) if 0 <= i + by < devices]
    return lax.ppermute(array, axis, pairs)


def normalize_kernel(offset, strain_ref, mask_ref, lead_ref, trail_ref, flat_ref, held, rows):
    samples = strain_ref.shape[0]
    columns = pl.ds(offset, flat_ref.shape[1])
    pltpu.sync_copy(strain_ref.at[:, columns], held)
    alive = jnp.broadcast_to(mask_ref[...] > 0, held.shape)
    rows[:HALF] = lead_ref[...]
    rows[HALF : HALF + samples] = jnp.where(
        alive, held[...].astype(jnp.float32), 0.0
    ).astype(jnp.bfloat16)
    rows[HALF + samples :] = trail_ref[...]
    out_rows = flat_ref.shape[0]
    row = lax.broadcasted_iota(jnp.int32, (TILE, TILE + SPAN), 0)
    col = lax.broadcasted_iota(jnp.int32, (TILE, TILE + SPAN), 1)
    band = jnp.where((col >= row) & (col <= row + SPAN), 1.0, 0.0).astype(jnp.bfloat16)
    for start in range(0, out_rows, TILE):
        count = min(TILE, out_rows - start)
        near = rows[start : start + count + SPAN]
        sums = jnp.dot(
            band[:count, : count + SPAN], jnp.abs(near), preferred_element_type=jnp.float32
        )
        center = rows[start + HALF : start + HALF + count].astype(jnp.float32)
        flat_ref[start : start + count] = (
            center / (sums / (2 * HALF + 1) + EPSILON)
        ).astype(jnp.bfloat16)


def params():
    return pltpu.CompilerParams(vmem_limit_bytes=VMEM_BYTES)


def normalize_chunk(strain, mask, lead, trail, offset, width):
    samples = strain.shape[0]

    def block(rows):
        return pl.BlockSpec((pl.Element(rows), pl.Element(width)), lambda i: (0, offset))

    return pl.pallas_call(
        functools.partial(normalize_kernel, offset),
        out_shape=jax.ShapeDtypeStruct((samples + HALF, width), jnp.bfloat16),
        grid=(1,),
        in_specs=[pl.BlockSpec(memory_space=pltpu.HBM), block(1), block(HALF), block(SPAN)],
        out_specs=pl.BlockSpec((samples + HALF, width), lambda i: (0, 0)),
        scratch_shapes=[
            pltpu.VMEM((samples, width), jnp.bfloat16),
            pltpu.VMEM((samples + HALF + SPAN, width), jnp.bfloat16),
        ],
        compiler_params=pltpu.CompilerParams(vmem_limit_bytes=52 << 20),
        cost_estimate=pl.CostEstimate(
            flops=2 * (samples + HALF) * (TILE + SPAN) * width,
            bytes_accessed=4 * samples * width,
            transcendentals=0,
        ),
        name="normalize",
    )(strain, mask, lead, trail)


def select_kernel(own, me_ref, index_ref, *refs):
    flats, (theirs_ref, mine_ref) = refs[:-2], refs[-2:]
    half = theirs_ref.shape[0]
    me = me_ref[0]
    spot, side = me >> 1, me & 1
    line = half // own
    index = jnp.concatenate(
        [
            index_ref[pl.ds(pl.multiple_of(block * own, own), own), :]
            for far in (1, 0)
            for block in [
                2 * ((spot + by) & (line - 1)) + (side ^ far) for by in range(line)
            ]
        ],
        axis=0,
    )
    offset = me * sum(flat.shape[1] for flat in flats)
    total = jnp.zeros((2 * half, theirs_ref.shape[1]), jnp.float32)
    for flat_ref in flats:
        width = flat_ref.shape[1]
        channel = lax.broadcasted_iota(jnp.int32, (2 * half, width), 1) + offset
        onehot = jnp.where(index == channel, 1.0, 0.0).astype(jnp.bfloat16)
        total += lax.dot_general(
            onehot, flat_ref[...], (((1,), (1,)), ((), ())), preferred_element_type=jnp.float32
        )
        offset += width
    theirs_ref[...] = total[:half].astype(jnp.bfloat16)
    mine_ref[...] = total[half:].astype(jnp.bfloat16)


def select_sources(flats, index, me, samples, own):
    sources = index.shape[0]
    channels = sum(f.shape[1] for f in flats)
    return pl.pallas_call(
        functools.partial(select_kernel, own),
        out_shape=[jax.ShapeDtypeStruct((sources // 2, samples), jnp.bfloat16)] * 2,
        grid_spec=pltpu.PrefetchScalarGridSpec(
            num_scalar_prefetch=1,
            grid=(samples // 256,),
            in_specs=[pl.BlockSpec((sources, 1), lambda i, me: (0, 0))]
            + [pl.BlockSpec((256, f.shape[1]), lambda i, me: (i, 0)) for f in flats],
            out_specs=[pl.BlockSpec((sources // 2, 256), lambda i, me: (0, i))] * 2,
        ),
        compiler_params=params(),
        cost_estimate=pl.CostEstimate(
            flops=2 * sources * samples * channels,
            bytes_accessed=2 * samples * channels,
            transcendentals=0,
        ),
        name="select",
    )(me, index[:, None], *flats)


def hankel_kernel(trace_ref, out_ref):
    width = out_ref.shape[1]
    for source in range(trace_ref.shape[0]):
        spread = jnp.broadcast_to(trace_ref[source : source + 1], (LAGS, width))
        shifted = pltpu.roll(spread, 0, 1, stride=1, stride_axis=0)
        out_ref[source * LAGS : (source + 1) * LAGS] = shifted.astype(jnp.bfloat16)


def hankel(traces):
    sources, samples = traces.shape
    width = samples + 128
    padded = jnp.pad(traces.astype(jnp.float32), ((0, 0), (0, 128)))
    return pl.pallas_call(
        hankel_kernel,
        out_shape=jax.ShapeDtypeStruct((sources * LAGS, width), jnp.bfloat16),
        grid=(sources // 8,),
        in_specs=[pl.BlockSpec((8, width), lambda i: (i, 0))],
        out_specs=pl.BlockSpec((8 * LAGS, width), lambda i: (i, 0)),
        compiler_params=params(),
        cost_estimate=pl.CostEstimate(
            flops=sources * LAGS * width, bytes_accessed=2 * sources * LAGS * width, transcendentals=0
        ),
        name="hankel",
    )(padded)


def at_end(spot):
    return (spot == 0) | (spot == 3)


def origin(slot, me):
    spot, side = me >> 1, me & 1
    near = spot < 2
    there = [
        spot,
        spot ^ 1,
        jnp.where(near, 2, 1),
        jnp.where(near, 3, 0),
    ][slot]
    return 2 * there + side


def correlate_kernel(rows, two, aliased, scale, me_ref, *refs):
    refs = list(refs)
    hankels = [refs.pop(0) for _ in range(rows)]
    first = refs.pop(0)
    second = refs.pop(0) if two else None
    if aliased:
        refs.pop(0)
    held = refs.pop()
    out_ref = refs.pop(0)
    depth, width = first.shape
    step = pl.program_id(0)
    each = hankels[0].shape[0] // ROWS

    @pl.when(step == 0)
    def _():
        held[depth:] = jnp.zeros((held.shape[0] - depth, width), held.dtype)
        if two:
            end = at_end(me_ref[0] >> 1)

            @pl.when(end)
            def _():
                held[:depth] = first[...]

            @pl.when(jnp.logical_not(end))
            def _():
                held[:depth] = second[...]
        else:
            held[:depth] = first[...]

    def product(ref, at):
        lagged = ref[pl.ds(pl.multiple_of(at * ROWS, ROWS), ROWS), :]
        return jnp.dot(lagged, held[...], preferred_element_type=jnp.float32) * scale

    if rows == 1:
        out_ref[...] = product(hankels[0], step).reshape(out_ref.shape).astype(out_ref.dtype)
        return
    sent_ref = refs.pop(0)

    @pl.when(step < each)
    def _():
        sent_ref[...] = product(hankels[1], step).reshape(sent_ref.shape).astype(sent_ref.dtype)

    @pl.when(step >= each)
    def _():
        out_ref[...] = product(hankels[0], step - each).reshape(out_ref.shape)


def correlate(hankels, operands, me, place, scale, out, channels, sent=False):
    lanes, span = hankels[0].shape
    sources = lanes // LAGS
    depth, width = operands[0].shape
    group = ROWS // LAGS
    each = lanes // ROWS
    rows = len(hankels)
    skip = (rows - 1) * each
    resident = pl.BlockSpec(memory_space=pltpu.VMEM)
    in_specs = [resident] * rows
    in_specs += [pl.BlockSpec((depth, width), lambda i, me: (0, 0))] * len(operands)
    arguments = [*hankels, *operands]
    aliases = {}
    if out is not None and not sent:
        in_specs.append(pl.BlockSpec(memory_space=pl.ANY))
        arguments.append(out)
        aliases = {len(arguments): 0}
    sent_shape = jax.ShapeDtypeStruct((sources, LAGS, width), jnp.bfloat16)
    sent_spec = pl.BlockSpec((group, LAGS, width), lambda i, me: (jnp.minimum(i, each - 1), 0, 0))
    out_shape = [jax.ShapeDtypeStruct((1, sources, LAGS, channels), jnp.float32)]
    out_specs = [
        pl.BlockSpec(
            (pl.Element(1), pl.Element(group), pl.Element(LAGS), pl.Element(width)),
            lambda i, me: (
                0,
                jnp.maximum(i - skip, 0) * group,
                0,
                pl.multiple_of(place(me[0]), 128),
            ),
        )
    ]
    if rows == 2:
        out_shape.append(sent_shape)
        out_specs.append(sent_spec)
    if sent:
        out_shape, out_specs = [sent_shape], [sent_spec]
    return pl.pallas_call(
        functools.partial(correlate_kernel, rows, len(operands) == 2, bool(aliases), scale),
        out_shape=out_shape,
        grid_spec=pltpu.PrefetchScalarGridSpec(
            num_scalar_prefetch=1,
            grid=(rows * each,),
            in_specs=in_specs,
            out_specs=out_specs,
            scratch_shapes=[pltpu.VMEM((span, width), jnp.bfloat16)],
        ),
        input_output_aliases=aliases,
        compiler_params=params(),
        cost_estimate=pl.CostEstimate(
            flops=2 * rows * lanes * span * width,
            bytes_accessed=2 * depth * width + 4 * lanes * width,
            transcendentals=0,
        ),
        name="correlate",
    )(me, *arguments)


def store_kernel(me_ref, got_ref, kept_ref, out_ref):
    out_ref[...] = got_ref[...].astype(jnp.float32)[None]


def store(got, me, place, out):
    sources, lags, width = got.shape
    group = ROWS // LAGS
    return pl.pallas_call(
        store_kernel,
        out_shape=jax.ShapeDtypeStruct(out.shape, out.dtype),
        grid_spec=pltpu.PrefetchScalarGridSpec(
            num_scalar_prefetch=1,
            grid=(sources // group,),
            in_specs=[
                pl.BlockSpec((group, lags, width), lambda i, me: (i, 0, 0)),
                pl.BlockSpec(memory_space=pl.ANY),
            ],
            out_specs=pl.BlockSpec(
                (pl.Element(1), pl.Element(group), pl.Element(lags), pl.Element(width)),
                lambda i, me: (0, i * group, 0, pl.multiple_of(place(me[0]), 128)),
            ),
        ),
        input_output_aliases={2: 0},
        compiler_params=params(),
        cost_estimate=pl.CostEstimate(
            flops=0, bytes_accessed=6 * sources * lags * width, transcendentals=0
        ),
        name="store",
    )(me, got, out)


def hop(array, pairs):
    return lax.ppermute(array, "src", pairs)


def line_of_four(strain, dead_mask, src_index):
    samples, channels = strain.shape
    devices = lax.axis_size("src")
    line = devices // 2
    count = len(WIDTHS)
    offsets = [sum(WIDTHS[:c]) for c in range(count)]
    total = channels * devices
    own = src_index.shape[0] // devices
    scale = 1.0 / math.sqrt(samples)
    me = lax.axis_index("src")

    def along(pairs):
        return [(2 * a + s, 2 * b + s) for a, b in pairs for s in range(2)]

    outer = along([(0, 1), (1, 0), (2, 3), (3, 2)])
    inner = along([(1, 2), (2, 1)])
    outward = along([(1, 0), (2, 3)])
    across = [(i, i ^ 1) for i in range(devices)]

    def masked(rows):
        return jnp.where(dead_mask > 0, rows, jnp.zeros((), rows.dtype))

    lead = passed_along(masked(strain[samples - HALF :]), "win", 1)
    trail = passed_along(masked(strain[:SPAN]), "win", -1)
    alive = (dead_mask > 0).astype(jnp.int32)
    flats = []
    for c in range(count):
        flats.append(
            normalize_chunk(strain, alive, lead, trail, offsets[c], WIDTHS[c])
        )

    here = jnp.reshape(me, (1,)).astype(jnp.int32)
    theirs, mine = select_sources(flats, src_index, here, samples, own)
    heard = hop(theirs, across)
    blocks = [
        mine[by * own : (by + 1) * own] + heard[by * own : (by + 1) * own] for by in range(line)
    ]
    traces = blocks[0]
    for by in range(1, line):
        traces = traces + hop(blocks[by], along([(i, (i + by) % line) for i in range(line)]))
    partner_traces = hop(traces, across)
    own_rows = hankel(traces)
    partner_rows = hankel(partner_traces)

    def hops(arrays, pairs):
        return [hop(a, pairs) for a in arrays]

    first_out = hops(flats, outer)
    first_in = hops(flats, inner)
    swapped = hop(flats[0], across)
    second_out = hops(first_in, outward)
    second_in = hops(first_out, inner)
    third_out = hops(second_in, outward)

    arrivals = [
        [[f] for f in flats],
        [[f] for f in first_out],
        [list(pair) for pair in zip(second_out, first_in)],
        [list(pair) for pair in zip(third_out, second_in)],
    ]
    out = None
    waiting = []

    def place(slot, c, partner):
        return lambda me: (origin(slot, me) ^ partner) * channels + offsets[c]

    def add(slot, c, partner, chunk, hankels):
        nonlocal out
        out, *sent = correlate(
            hankels, chunk, here, place(slot, c, partner), scale, out, total
        )
        return sent

    def keep():
        nonlocal out
        out = store(*waiting.pop(0), out)

    add(0, 0, 0, [flats[0]], [own_rows])
    for slot, c in STEPS:
        chunk = arrivals[slot][c]
        if slot < line - 1:
            (made,) = add(slot, c, 0, chunk, [own_rows, partner_rows])
        else:
            (made,) = correlate(
                [partner_rows], chunk, here, place(slot, c, 0), scale, out, total, sent=True
            )
            add(slot, c, 0, chunk, [own_rows])
        waiting.append((hop(made, across), here, place(slot, c, 1)))
        if (slot, c) == (0, count - 1):
            add(0, 0, 1, [swapped], [own_rows])
        for _ in range(STORED.get((slot, c), 0)):
            keep()
    while waiting:
        keep()
    return out


def gathered(strain, dead_mask, src_index):
    samples, channels = strain.shape
    devices = lax.axis_size("src")
    scale = 1.0 / math.sqrt(samples)
    masked = jnp.where(dead_mask > 0, strain, jnp.zeros((), strain.dtype))
    lead = passed_along(masked[samples - HALF :], "win", 1)
    trail = passed_along(masked[:SPAN], "win", -1)
    rows = jnp.concatenate([lead, masked, trail], axis=0).astype(jnp.float32)
    sums = lax.reduce_window(
        jnp.abs(rows), jnp.zeros((), jnp.float32), lax.add, (2 * HALF + 1, 1), (1, 1), "VALID"
    )
    center = rows[HALF : rows.shape[0] - HALF]
    flat = (center / (sums / (2 * HALF + 1) + EPSILON)).astype(jnp.bfloat16)
    offset = lax.axis_index("src") * channels
    onehot = (src_index[:, None] - offset == jnp.arange(channels, dtype=jnp.int32)[None, :]).astype(
        jnp.bfloat16
    )
    selected = lax.dot_general(
        onehot, flat[:samples], (((1,), (1,)), ((), ())), preferred_element_type=jnp.float32
    )
    traces = lax.psum_scatter(
        selected.astype(jnp.bfloat16), "src", scatter_dimension=0, tiled=True
    )
    sources = traces.shape[0]
    tail = flat.shape[0] - samples
    shifted = [jnp.pad(traces, ((0, 0), (lag, tail - lag))) for lag in range(LAGS)]
    lagged = jnp.stack(shifted, axis=1).reshape(sources * LAGS, flat.shape[0])
    everywhere = lax.all_gather(flat, "src", axis=1, tiled=True)
    joined = jnp.dot(lagged, everywhere, preferred_element_type=jnp.float32) * scale
    return joined.reshape(1, sources, LAGS, channels * devices)


def lined(devices, channels):
    return devices == 8 and channels == sum(WIDTHS)


def shards(strain, dead_mask, src_index):
    if lined(lax.axis_size("src"), strain.shape[1]):
        return line_of_four(strain, dead_mask, src_index)
    return gathered(strain, dead_mask, src_index)


def solution(mesh):
    in_specs = (P("win", "src"), P("win", "src"), P())
    out_specs = P("win", "src", None, None)
    return jax.shard_map(shards, mesh=mesh, in_specs=in_specs, out_specs=out_specs, check_vma=False)
```

profile of v0, /device:TPU:0, one launch (start us, length us, event | category | flops | bytes accessed | tf_op | source)
XLA Modules:
  0.0 423.9 jit_solution(2378092112776187687)
XLA Ops:
  3.9 3.0 collective-permute-start
  18.3 3.1 collective-permute-start.2
  21.4 8.8 %collective-permute-done.2 = bf16[128,1536]{1,0:T(8,128)(2,1)S(1)} collective-permute-done((bf16[128,1536]{1,0:T(8,128)(2,1)S(1)}, bf16[128,1536]{1,0:T(8,128)(2,1)S(1)}, u32[]{:S(2)}, u32[]{:S(2)}) %collective-permute-start.2) | collective-permute-done | bytes 393248 | tf_op jit(solution)/shard_map/ppermute | solution.py:325
  39.5 3.2 collective-permute-done.4
  46.2 3.2 correlate.25.refs_3_
  49.4 53.4 %collective-permute-done.7.refs_2_ = bf16[1568,128]{1,0:T(8,128)(2,1)S(1)} collective-permute-done((bf16[1568,128]{1,0:T(8,128)(2,1)S(1)}, bf16[1568,128]{1,0:T(8,128)(2,1)S(1)}, u32[]{:S(2)}, u32[]{:S(2)}) %collective-permute-start.7) | collective-permute-done | bytes 401440 | tf_op jit(solution)/shard_map/ppermute | solution.py:325
  106.7 5.7 %correlate.26 = (f32[1,32,32,10240]{3,2,1,0:T(8,128)}, bf16[32,32,512]{2,1,0:T(8,128)(2,1)S(1)}) custom-call(s32[1]{0:T(128)} %bitcast.me_ref, bf16[1024,1664]{1,0:T(8,128)(2,1)S(1)} %hankel.3.refs_0_, bf16[1024,1664]{1,0:T(8,128)(2,1)S(1)} %hankel.2.refs_0_.refs_1_, ...), custom_call_target="tpu_custom_call", output_to_operand_aliasing={{0}: (4, {})} | custom-call | flops 3489660928 | bytes 3702784 | tf_op jit(solution)/shard_map/correlate/pallas_call | solution.py:272
  112.4 3.5 correlate.27
  117.5 3.3 correlate.28
  123.6 8.8 %collective-permute-start.15 = (bf16[1568,384]{1,0:T(8,128)(2,1)S(1)}, bf16[1568,384]{1,0:T(8,128)(2,1)S(1)}, u32[]{:S(2)}, u32[]{:S(2)}) collective-permute-start(bf16[1568,384]{1,0:T(8,128)(2,1)S(1)} %normalize.4.refs_0_.refs_1_), channel_id=1, source_target_pairs={{0,2},{1,3},{2,0},{3,1},{4,6},{5,7},{6,4},{7,5},{8,10},{9,11},{10,... | collective-permute-start | bytes 3612680 | tf_op jit(solution)/shard_map/ppermute | solution.py:325
  132.4 4.0 collective-permute-done.29.got_ref
  140.7 20.1 %collective-permute-done.27.refs_1_ = bf16[1568,384]{1,0:T(8,128)(2,1)S(1)} collective-permute-done((bf16[1568,384]{1,0:T(8,128)(2,1)S(1)}, bf16[1568,384]{1,0:T(8,128)(2,1)S(1)}, u32[]{:S(2)}, u32[]{:S(2)}) %collective-permute-start.27) | collective-permute-done | bytes 1204256 | tf_op jit(solution)/shard_map/ppermute | solution.py:325
  162.3 3.1 correlate.29.refs_3_
  167.7 5.4 %correlate.30 = (f32[1,32,32,10240]{3,2,1,0:T(8,128)}, bf16[32,32,384]{2,1,0:T(8,128)(2,1)S(1)}) custom-call(s32[1]{0:T(128)} %bitcast.me_ref, bf16[1024,1664]{1,0:T(8,128)(2,1)S(1)} %hankel.3.refs_0_, bf16[1024,1664]{1,0:T(8,128)(2,1)S(1)} %hankel.2.refs_0_.refs_1_, ...), custom_call_target="tpu_custom_call", output_to_operand_aliasing={{0}: (4, {})} | custom-call | flops 2617245696 | bytes 2777088 | tf_op jit(solution)/shard_map/correlate/pallas_call | solution.py:272
  173.1 5.6 %correlate.31 = (f32[1,32,32,10240]{3,2,1,0:T(8,128)}, bf16[32,32,512]{2,1,0:T(8,128)(2,1)S(1)}) custom-call(s32[1]{0:T(128)} %bitcast.me_ref, bf16[1024,1664]{1,0:T(8,128)(2,1)S(1)} %hankel.3.refs_0_, bf16[1024,1664]{1,0:T(8,128)(2,1)S(1)} %hankel.2.refs_0_.refs_1_, ...), custom_call_target="tpu_custom_call", output_to_operand_aliasing={{0}: (4, {})} | custom-call | flops 3489660928 | bytes 3702784 | tf_op jit(solution)/shard_map/correlate/pallas_call | solution.py:272
  183.2 3.6 correlate.32
  186.8 3.3 correlate.33
  192.2 14.8 %collective-permute-done.37.got_ref = bf16[32,32,128]{2,1,0:T(8,128)(2,1)S(1)} collective-permute-done((bf16[32,32,128]{2,1,0:T(8,128)(2,1)S(1)}, bf16[32,32,128]{2,1,0:T(8,128)(2,1)S(1)}, u32[]{:S(2)}, u32[]{:S(2)}) %collective-permute-start.37) | collective-permute-done | bytes 262176 | tf_op jit(solution)/shard_map/ppermute | solution.py:325
  210.4 11.4 %collective-permute-done.38.got_ref = bf16[32,32,256]{2,1,0:T(8,128)(2,1)S(1)} collective-permute-done((bf16[32,32,256]{2,1,0:T(8,128)(2,1)S(1)}, bf16[32,32,256]{2,1,0:T(8,128)(2,1)S(1)}, u32[]{:S(2)}, u32[]{:S(2)}) %collective-permute-start.38) | collective-permute-done | bytes 524320 | tf_op jit(solution)/shard_map/ppermute | solution.py:325
  229.2 5.1 %collective-permute-done.26.refs_2_ = bf16[1568,512]{1,0:T(8,128)(2,1)S(1)} collective-permute-done((bf16[1568,512]{1,0:T(8,128)(2,1)S(1)}, bf16[1568,512]{1,0:T(8,128)(2,1)S(1)}, u32[]{:S(2)}, u32[]{:S(2)}) %collective-permute-start.26) | collective-permute-done | bytes 1605664 | tf_op jit(solution)/shard_map/ppermute | solution.py:325
  235.6 5.7 %correlate.34 = (f32[1,32,32,10240]{3,2,1,0:T(8,128)}, bf16[32,32,512]{2,1,0:T(8,128)(2,1)S(1)}) custom-call(s32[1]{0:T(128)} %bitcast.me_ref, bf16[1024,1664]{1,0:T(8,128)(2,1)S(1)} %hankel.3.refs_0_, bf16[1024,1664]{1,0:T(8,128)(2,1)S(1)} %hankel.2.refs_0_.refs_1_, ...), custom_call_target="tpu_custom_call", output_to_operand_aliasing={{0}: (5, {})} | custom-call | flops 3489660928 | bytes 3702784 | tf_op jit(solution)/shard_map/correlate/pallas_call | solution.py:272
  246.3 81.5 %collective-permute-done.36.refs_2_ = bf16[1568,384]{1,0:T(8,128)(2,1)} collective-permute-done((bf16[1568,384]{1,0:T(8,128)(2,1)}, bf16[1568,384]{1,0:T(8,128)(2,1)}, u32[]{:S(2)}, u32[]{:S(2)}) %collective-permute-start.36) | collective-permute-done | bytes 1204256 | tf_op jit(solution)/shard_map/ppermute | solution.py:325
  329.4 7.1 %correlate.35 = (f32[1,32,32,10240]{3,2,1,0:T(8,128)}, bf16[32,32,384]{2,1,0:T(8,128)(2,1)S(1)}) custom-call(s32[1]{0:T(128)} %bitcast.me_ref, bf16[1024,1664]{1,0:T(8,128)(2,1)S(1)} %hankel.3.refs_0_, bf16[1024,1664]{1,0:T(8,128)(2,1)S(1)} %hankel.2.refs_0_.refs_1_, ...), custom_call_target="tpu_custom_call", output_to_operand_aliasing={{0}: (5, {})} | custom-call | flops 2617245696 | bytes 2777088 | tf_op jit(solution)/shard_map/correlate/pallas_call | solution.py:272
  337.0 5.1 %correlate.24 = bf16[32,32,512]{2,1,0:T(8,128)(2,1)} custom-call(s32[1]{0:T(128)} %bitcast.me_ref, bf16[1024,1664]{1,0:T(8,128)(2,1)S(1)} %hankel.2.refs_0_.refs_1_, bf16[1568,512]{1,0:T(8,128)(2,1)} %collective-permute-done.21.refs_1_, bf16[1568,512]{1,0:T(8,128)(2,1)} %collective-permute-done.20.refs_2_), custom_call_target="tpu_custom_call" | custom-call | flops 1744830464 | bytes 3702784 | tf_op jit(solution)/shard_map/correlate/pallas_call | solution.py:272
  342.1 2.9 collective-permute-done.34.refs_2_
  345.5 3.5 correlate.36
  349.0 21.0 %collective-permute-done.17.refs_1_ = bf16[1568,384]{1,0:T(8,128)(2,1)S(1)} collective-permute-done((bf16[1568,384]{1,0:T(8,128)(2,1)S(1)}, bf16[1568,384]{1,0:T(8,128)(2,1)S(1)}, u32[]{:S(2)}, u32[]{:S(2)}) %collective-permute-start.17) | collective-permute-done | bytes 1204256 | tf_op jit(solution)/shard_map/ppermute | solution.py:325
  370.5 3.0 correlate.23
  376.5 3.3 correlate.37
  388.7 13.5 %collective-permute-done.40.got_ref = bf16[32,32,128]{2,1,0:T(8,128)(2,1)S(1)} collective-permute-done((bf16[32,32,128]{2,1,0:T(8,128)(2,1)S(1)}, bf16[32,32,128]{2,1,0:T(8,128)(2,1)S(1)}, u32[]{:S(2)}, u32[]{:S(2)}) %collective-permute-start.40) | collective-permute-done | bytes 262176 | tf_op jit(solution)/shard_map/ppermute | solution.py:325
  403.1 5.2 %correlate.38.refs_3_ = f32[1,32,32,10240]{3,2,1,0:T(8,128)} custom-call(s32[1]{0:T(128)} %bitcast.me_ref, bf16[1024,1664]{1,0:T(8,128)(2,1)S(1)} %hankel.3.refs_0_, bf16[1568,512]{1,0:T(8,128)(2,1)} %collective-permute-done.21.refs_1_, bf16[1568,512]{1,0:T(8,128)(2,1)} %collective-permute-done.20.refs_2_, ...), custom_call_target="tpu_custom_call", output_to_operand_aliasing={{}: (4, {})} | custom-call | flops 1744830464 | bytes 3702784 | tf_op jit(solution)/shard_map/correlate/pallas_call | solution.py:272
  408.3 3.2 correlate.39.kept_ref
  (131 shorter events, 96.0 us)
Async XLA Ops:
  36.7 102.1 %collective-permute-start.19 = (bf16[1568,512]{1,0:T(8,128)(2,1)S(1)}, bf16[1568,512]{1,0:T(8,128)(2,1)S(1)}, u32[]{:S(2)}, u32[]{:S(2)}) collective-permute-start(bf16[1568,512]{1,0:T(8,128)(2,1)S(1)} %normalize.5.refs_1_.refs_2_), channel_id=1, source_target_pairs={{0,2},{1,3},{2,0},{3,1},{4,6},{5,7},{6,4},{7,5},{8,10},{9,11},{10,... | collective-permute-start | bytes 4816904 | tf_op jit(solution)/shard_map/ppermute | solution.py:325
  37.4 78.6 %collective-permute-start.11 = (bf16[1568,256]{1,0:T(8,128)(2,1)S(1)}, bf16[1568,256]{1,0:T(8,128)(2,1)S(1)}, u32[]{:S(2)}, u32[]{:S(2)}) collective-permute-start(bf16[1568,256]{1,0:T(8,128)(2,1)S(1)} %normalize.6.refs_2_), channel_id=1, source_target_pairs={{0,2},{1,3},{2,0},{3,1},{4,6},{5,7},{6,4},{7,5},{8,10},{9,11},{10,... | collective-permute-start | bytes 2408456 | tf_op jit(solution)/shard_map/ppermute | solution.py:325
  38.8 64.0 %collective-permute-start.7 = (bf16[1568,128]{1,0:T(8,128)(2,1)S(1)}, bf16[1568,128]{1,0:T(8,128)(2,1)S(1)}, u32[]{:S(2)}, u32[]{:S(2)}) collective-permute-start(bf16[1568,128]{1,0:T(8,128)(2,1)S(1)} %normalize.7.refs_3_.refs_2_), channel_id=1, source_target_pairs={{0,2},{1,3},{2,0},{3,1},{4,6},{5,7},{6,4},{7,5},{8,10},{9,11},{10,... | collective-permute-start | bytes 1204232 | tf_op jit(solution)/shard_map/ppermute | solution.py:325
  42.6 60.8 %collective-permute-start.23 = (bf16[1568,128]{1,0:T(8,128)(2,1)S(1)}, bf16[1568,128]{1,0:T(8,128)(2,1)S(1)}, u32[]{:S(2)}, u32[]{:S(2)}) collective-permute-start(bf16[1568,128]{1,0:T(8,128)(2,1)S(1)} %normalize.7.refs_3_.refs_2_), channel_id=1, source_target_pairs={{2,4},{3,5},{4,2},{5,3},{10,12},{11,13},{12,10},{13,11},{18,20},{1... | collective-permute-start | bytes 1204232 | tf_op jit(solution)/shard_map/ppermute | solution.py:325
  43.4 61.4 %collective-permute-start.6 = (bf16[32,1536]{1,0:T(8,128)(2,1)S(1)}, bf16[32,1536]{1,0:T(8,128)(2,1)S(1)}, u32[]{:S(2)}, u32[]{:S(2)}) collective-permute-start(bf16[32,1536]{1,0:T(8,128)(2,1)S(1)} %fusion.2), channel_id=1, source_target_pairs={{0,1},{1,0},{2,3},{3,2},{4,5},{5,4},{6,7},{7,6},{8,9},{9,8},{10,11... | collective-permute-start | bytes 294920 | tf_op jit(solution)/shard_map/ppermute | solution.py:325
  102.7 18.1 %collective-permute-start.33 = (bf16[1568,256]{1,0:T(8,128)(2,1)S(1)}, bf16[1568,256]{1,0:T(8,128)(2,1)S(1)}, u32[]{:S(2)}, u32[]{:S(2)}) collective-permute-start(bf16[1568,256]{1,0:T(8,128)(2,1)S(1)} %normalize.6.refs_2_), channel_id=1, source_target_pairs={{2,4},{3,5},{4,2},{5,3},{10,12},{11,13},{12,10},{13,11},{18,20},{1... | collective-permute-start | bytes 2408456 | tf_op jit(solution)/shard_map/ppermute | solution.py:325
  103.5 17.9 %collective-permute-start.24 = (bf16[1568,128]{1,0:T(8,128)(2,1)S(1)}, bf16[1568,128]{1,0:T(8,128)(2,1)S(1)}, u32[]{:S(2)}, u32[]{:S(2)}) collective-permute-start(bf16[1568,128]{1,0:T(8,128)(2,1)S(1)} %collective-permute-done.23.refs_3_), channel_id=1, source_target_pairs={{2,0},{3,1},{4,6},{5,7},{10,8},{11,9},{12,14},{13,15},{18,16},{19,... | collective-permute-start | bytes 1204232 | tf_op jit(solution)/shard_map/ppermute | solution.py:325
  104.8 18.8 %collective-permute-start.8 = (bf16[1568,128]{1,0:T(8,128)(2,1)S(1)}, bf16[1568,128]{1,0:T(8,128)(2,1)S(1)}, u32[]{:S(2)}, u32[]{:S(2)}) collective-permute-start(bf16[1568,128]{1,0:T(8,128)(2,1)S(1)} %collective-permute-done.7.refs_2_), channel_id=1, source_target_pairs={{2,4},{3,5},{4,2},{5,3},{10,12},{11,13},{12,10},{13,11},{18,20},{1... | collective-permute-start | bytes 1204232 | tf_op jit(solution)/shard_map/ppermute | solution.py:325
  116.0 22.1 %collective-permute-start.30 = (bf16[32,32,256]{2,1,0:T(8,128)(2,1)S(1)}, bf16[32,32,256]{2,1,0:T(8,128)(2,1)S(1)}, u32[]{:S(2)}, u32[]{:S(2)}) collective-permute-start(bf16[32,32,256]{2,1,0:T(8,128)(2,1)S(1)} %get-tuple-element.36), channel_id=1, source_target_pairs={{0,1},{1,0},{2,3},{3,2},{4,5},{5,4},{6,7},{7,6},{8,9},{9,8},{10,11... | collective-permute-start | bytes 1572872 | tf_op jit(solution)/shard_map/ppermute | solution.py:325
  122.1 38.7 %collective-permute-start.27 = (bf16[1568,384]{1,0:T(8,128)(2,1)S(1)}, bf16[1568,384]{1,0:T(8,128)(2,1)S(1)}, u32[]{:S(2)}, u32[]{:S(2)}) collective-permute-start(bf16[1568,384]{1,0:T(8,128)(2,1)S(1)} %normalize.4.refs_0_.refs_1_), channel_id=1, source_target_pairs={{0,1},{1,0},{2,3},{3,2},{4,5},{5,4},{6,7},{7,6},{8,9},{9,8},{10,11... | collective-permute-start | bytes 3612680 | tf_op jit(solution)/shard_map/ppermute | solution.py:325
  123.6 41.9 %collective-permute-start.15 = (bf16[1568,384]{1,0:T(8,128)(2,1)S(1)}, bf16[1568,384]{1,0:T(8,128)(2,1)S(1)}, u32[]{:S(2)}, u32[]{:S(2)}) collective-permute-start(bf16[1568,384]{1,0:T(8,128)(2,1)S(1)} %normalize.4.refs_0_.refs_1_), channel_id=1, source_target_pairs={{0,2},{1,3},{2,0},{3,1},{4,6},{5,7},{6,4},{7,5},{8,10},{9,11},{10,... | collective-permute-start | bytes 3612680 | tf_op jit(solution)/shard_map/ppermute | solution.py:325
  136.4 29.8 %collective-permute-start.35 = (bf16[1568,384]{1,0:T(8,128)(2,1)S(1)}, bf16[1568,384]{1,0:T(8,128)(2,1)}, u32[]{:S(2)}, u32[]{:S(2)}) collective-permute-start(bf16[1568,384]{1,0:T(8,128)(2,1)S(1)} %normalize.4.refs_0_.refs_1_), channel_id=1, source_target_pairs={{2,4},{3,5},{4,2},{5,3},{10,12},{11,13},{12,10},{13,11},{18,20},{1... | collective-permute-start | bytes 3612680 | tf_op jit(solution)/shard_map/ppermute | solution.py:325
  138.1 43.8 %collective-permute-start.25 = (bf16[1568,512]{1,0:T(8,128)(2,1)S(1)}, bf16[1568,512]{1,0:T(8,128)(2,1)S(1)}, u32[]{:S(2)}, u32[]{:S(2)}) collective-permute-start(bf16[1568,512]{1,0:T(8,128)(2,1)S(1)} %normalize.5.refs_1_.refs_2_), channel_id=1, source_target_pairs={{2,4},{3,5},{4,2},{5,3},{10,12},{11,13},{12,10},{13,11},{18,20},{1... | collective-permute-start | bytes 4816904 | tf_op jit(solution)/shard_map/ppermute | solution.py:325
  138.9 69.7 %collective-permute-start.20 = (bf16[1568,512]{1,0:T(8,128)(2,1)S(1)}, bf16[1568,512]{1,0:T(8,128)(2,1)}, u32[]{:S(2)}, u32[]{:S(2)}) collective-permute-start(bf16[1568,512]{1,0:T(8,128)(2,1)S(1)} %collective-permute-done.19.refs_2_), channel_id=1, source_target_pairs={{2,4},{3,5},{4,2},{5,3},{10,12},{11,13},{12,10},{13,11},{18,20},{1... | collective-permute-start | bytes 4816904 | tf_op jit(solution)/shard_map/ppermute | solution.py:325
  160.8 30.7 %collective-permute-start.31 = (bf16[32,32,512]{2,1,0:T(8,128)(2,1)S(1)}, bf16[32,32,512]{2,1,0:T(8,128)(2,1)S(1)}, u32[]{:S(2)}, u32[]{:S(2)}) collective-permute-start(bf16[32,32,512]{2,1,0:T(8,128)(2,1)S(1)} %get-tuple-element.37), channel_id=1, source_target_pairs={{0,1},{1,0},{2,3},{3,2},{4,5},{5,4},{6,7},{7,6},{8,9},{9,8},{10,11... | collective-permute-start | bytes 3145736 | tf_op jit(solution)/shard_map/ppermute | solution.py:325
  165.5 24.6 %collective-permute-start.12 = (bf16[1568,256]{1,0:T(8,128)(2,1)S(1)}, bf16[1568,256]{1,0:T(8,128)(2,1)S(1)}, u32[]{:S(2)}, u32[]{:S(2)}) collective-permute-start(bf16[1568,256]{1,0:T(8,128)(2,1)S(1)} %collective-permute-done.11.refs_2_), channel_id=1, source_target_pairs={{2,4},{3,5},{4,2},{5,3},{10,12},{11,13},{12,10},{13,11},{18,20},{1... | collective-permute-start | bytes 2408456 | tf_op jit(solution)/shard_map/ppermute | solution.py:325
  181.2 28.7 %collective-permute-start.28 = (bf16[32,32,384]{2,1,0:T(8,128)(2,1)S(1)}, bf16[32,32,384]{2,1,0:T(8,128)(2,1)S(1)}, u32[]{:S(2)}, u32[]{:S(2)}) collective-permute-start(bf16[32,32,384]{2,1,0:T(8,128)(2,1)S(1)} %get-tuple-element.34), channel_id=1, source_target_pairs={{0,1},{1,0},{2,3},{3,2},{4,5},{5,4},{6,7},{7,6},{8,9},{9,8},{10,11... | collective-permute-start | bytes 2359304 | tf_op jit(solution)/shard_map/ppermute | solution.py:325
  181.9 52.4 %collective-permute-start.26 = (bf16[1568,512]{1,0:T(8,128)(2,1)S(1)}, bf16[1568,512]{1,0:T(8,128)(2,1)S(1)}, u32[]{:S(2)}, u32[]{:S(2)}) collective-permute-start(bf16[1568,512]{1,0:T(8,128)(2,1)S(1)} %collective-permute-done.25.refs_3_), channel_id=1, source_target_pairs={{2,0},{3,1},{4,6},{5,7},{10,8},{11,9},{12,14},{13,15},{18,16},{19,... | collective-permute-start | bytes 4816904 | tf_op jit(solution)/shard_map/ppermute | solution.py:325
  191.5 36.1 %collective-permute-start.16 = (bf16[1568,384]{1,0:T(8,128)(2,1)S(1)}, bf16[1568,384]{1,0:T(8,128)(2,1)S(1)}, u32[]{:S(2)}, u32[]{:S(2)}) collective-permute-start(bf16[1568,384]{1,0:T(8,128)(2,1)S(1)} %collective-permute-done.15.refs_2_), channel_id=1, source_target_pairs={{2,4},{3,5},{4,2},{5,3},{10,12},{11,13},{12,10},{13,11},{18,20},{1... | collective-permute-start | bytes 3612680 | tf_op jit(solution)/shard_map/ppermute | solution.py:325
  208.6 127.9 %collective-permute-start.21 = (bf16[1568,512]{1,0:T(8,128)(2,1)}, bf16[1568,512]{1,0:T(8,128)(2,1)}, u32[]{:S(2)}, u32[]{:S(2)}) collective-permute-start(bf16[1568,512]{1,0:T(8,128)(2,1)} %collective-permute-done.20.refs_2_), channel_id=1, source_target_pairs={{2,0},{3,1},{4,6},{5,7},{10,8},{11,9},{12,14},{13,15},{18,16},{19,... | collective-permute-start | bytes 4816904 | tf_op jit(solution)/shard_map/ppermute | solution.py:325
  209.9 31.7 %collective-permute-start.39 = (bf16[32,32,512]{2,1,0:T(8,128)(2,1)S(1)}, bf16[32,32,512]{2,1,0:T(8,128)(2,1)S(1)}, u32[]{:S(2)}, u32[]{:S(2)}) collective-permute-start(bf16[32,32,512]{2,1,0:T(8,128)(2,1)S(1)} %get-tuple-element.45), channel_id=1, source_target_pairs={{0,1},{1,0},{2,3},{3,2},{4,5},{5,4},{6,7},{7,6},{8,9},{9,8},{10,11... | collective-permute-start | bytes 3145736 | tf_op jit(solution)/shard_map/ppermute | solution.py:325
  221.8 106.0 %collective-permute-start.36 = (bf16[1568,384]{1,0:T(8,128)(2,1)}, bf16[1568,384]{1,0:T(8,128)(2,1)}, u32[]{:S(2)}, u32[]{:S(2)}) collective-permute-start(bf16[1568,384]{1,0:T(8,128)(2,1)} %collective-permute-done.35.refs_3_), channel_id=1, source_target_pairs={{2,0},{3,1},{4,6},{5,7},{10,8},{11,9},{12,14},{13,15},{18,16},{19,... | collective-permute-start | bytes 3612680 | tf_op jit(solution)/shard_map/ppermute | solution.py:325
  227.9 117.0 %collective-permute-start.34 = (bf16[1568,256]{1,0:T(8,128)(2,1)S(1)}, bf16[1568,256]{1,0:T(8,128)(2,1)S(1)}, u32[]{:S(2)}, u32[]{:S(2)}) collective-permute-start(bf16[1568,256]{1,0:T(8,128)(2,1)S(1)} %copy-done.6), channel_id=1, source_target_pairs={{2,0},{3,1},{4,6},{5,7},{10,8},{11,9},{12,14},{13,15},{18,16},{19,... | collective-permute-start | bytes 2408456 | tf_op jit(solution)/shard_map/ppermute | solution.py:325
  234.3 135.7 %collective-permute-start.17 = (bf16[1568,384]{1,0:T(8,128)(2,1)S(1)}, bf16[1568,384]{1,0:T(8,128)(2,1)S(1)}, u32[]{:S(2)}, u32[]{:S(2)}) collective-permute-start(bf16[1568,384]{1,0:T(8,128)(2,1)S(1)} %collective-permute-done.16.refs_2_), channel_id=1, source_target_pairs={{2,0},{3,1},{4,6},{5,7},{10,8},{11,9},{12,14},{13,15},{18,16},{19,... | collective-permute-start | bytes 3612680 | tf_op jit(solution)/shard_map/ppermute | solution.py:325
  241.6 131.9 %collective-permute-start.32 = (bf16[32,32,512]{2,1,0:T(8,128)(2,1)S(1)}, bf16[32,32,512]{2,1,0:T(8,128)(2,1)S(1)}, u32[]{:S(2)}, u32[]{:S(2)}) collective-permute-start(bf16[32,32,512]{2,1,0:T(8,128)(2,1)S(1)} %get-tuple-element.42), channel_id=1, source_target_pairs={{0,1},{1,0},{2,3},{3,2},{4,5},{5,4},{6,7},{7,6},{8,9},{9,8},{10,11... | collective-permute-start | bytes 3145736 | tf_op jit(solution)/shard_map/ppermute | solution.py:325
  327.9 52.0 %collective-permute-start.13 = (bf16[1568,256]{1,0:T(8,128)(2,1)S(1)}, bf16[1568,256]{1,0:T(8,128)(2,1)S(1)}, u32[]{:S(2)}, u32[]{:S(2)}) collective-permute-start(bf16[1568,256]{1,0:T(8,128)(2,1)S(1)} %copy-done.1), channel_id=1, source_target_pairs={{2,0},{3,1},{4,6},{5,7},{10,8},{11,9},{12,14},{13,15},{18,16},{19,... | collective-permute-start | bytes 2408456 | tf_op jit(solution)/shard_map/ppermute | solution.py:325
  336.5 46.0 %collective-permute-start.42 = (bf16[32,32,384]{2,1,0:T(8,128)(2,1)S(1)}, bf16[32,32,384]{2,1,0:T(8,128)(2,1)S(1)}, u32[]{:S(2)}, u32[]{:S(2)}) collective-permute-start(bf16[32,32,384]{2,1,0:T(8,128)(2,1)S(1)} %get-tuple-element.51), channel_id=1, source_target_pairs={{0,1},{1,0},{2,3},{3,2},{4,5},{5,4},{6,7},{7,6},{8,9},{9,8},{10,11... | collective-permute-start | bytes 2359304 | tf_op jit(solution)/shard_map/ppermute | solution.py:325
  345.0 66.5 %collective-permute-start.22 = (bf16[32,32,512]{2,1,0:T(8,128)(2,1)}, bf16[32,32,512]{2,1,0:T(8,128)(2,1)}, u32[]{:S(2)}, u32[]{:S(2)}) collective-permute-start(bf16[32,32,512]{2,1,0:T(8,128)(2,1)} %correlate.24), channel_id=1, source_target_pairs={{0,1},{1,0},{2,3},{3,2},{4,5},{5,4},{6,7},{7,6},{8,9},{9,8},{10,11... | collective-permute-start | bytes 3145736 | tf_op jit(solution)/shard_map/ppermute | solution.py:325
  373.5 44.5 %collective-permute-start.18 = (bf16[32,32,384]{2,1,0:T(8,128)(2,1)}, bf16[32,32,384]{2,1,0:T(8,128)(2,1)}, u32[]{:S(2)}, u32[]{:S(2)}) collective-permute-start(bf16[32,32,384]{2,1,0:T(8,128)(2,1)} %correlate.23), channel_id=1, source_target_pairs={{0,1},{1,0},{2,3},{3,2},{4,5},{5,4},{6,7},{7,6},{8,9},{9,8},{10,11... | collective-permute-start | bytes 2359304 | tf_op jit(solution)/shard_map/ppermute | solution.py:325
  379.9 22.4 %collective-permute-start.40 = (bf16[32,32,128]{2,1,0:T(8,128)(2,1)S(1)}, bf16[32,32,128]{2,1,0:T(8,128)(2,1)S(1)}, u32[]{:S(2)}, u32[]{:S(2)}) collective-permute-start(bf16[32,32,128]{2,1,0:T(8,128)(2,1)S(1)} %get-tuple-element.49), channel_id=1, source_target_pairs={{0,1},{1,0},{2,3},{3,2},{4,5},{5,4},{6,7},{7,6},{8,9},{9,8},{10,11... | collective-permute-start | bytes 786440 | tf_op jit(solution)/shard_map/ppermute | solution.py:325
  382.5 37.7 %collective-permute-start.14 = (bf16[32,32,256]{2,1,0:T(8,128)(2,1)}, bf16[32,32,256]{2,1,0:T(8,128)(2,1)}, u32[]{:S(2)}, u32[]{:S(2)}) collective-permute-start(bf16[32,32,256]{2,1,0:T(8,128)(2,1)} %correlate.22), channel_id=1, source_target_pairs={{0,1},{1,0},{2,3},{3,2},{4,5},{5,4},{6,7},{7,6},{8,9},{9,8},{10,11... | collective-permute-start | bytes 1572872 | tf_op jit(solution)/shard_map/ppermute | solution.py:325
  387.2 35.0 %collective-permute-start.10 = (bf16[32,32,128]{2,1,0:T(8,128)(2,1)}, bf16[32,32,128]{2,1,0:T(8,128)(2,1)}, u32[]{:S(2)}, u32[]{:S(2)}) collective-permute-start(bf16[32,32,128]{2,1,0:T(8,128)(2,1)} %correlate.21), channel_id=1, source_target_pairs={{0,1},{1,0},{2,3},{3,2},{4,5},{5,4},{6,7},{7,6},{8,9},{9,8},{10,11... | collective-permute-start | bytes 786440 | tf_op jit(solution)/shard_map/ppermute | solution.py:325
  (24 other events, 344.0 us)
where the time goes:
time: 425 us; the launch traced here: 424 us
  waiting for transfers between devices  243 us (57%)
  Pallas kernels  115 us (27%)
  starting transfers between devices  61.8 us (15%)
    ppermute x41, waiting for transfers between devices, hop(): return lax.ppermute(array, 'src', pairs)  242 us
    pallas_call x21, Pallas kernels, correlate(): pl.pallas_call(functools.partial(correlate_kernel, rows, len(operands) ==...  81.3 us
    ppermute x41, starting transfers between devices, hop(): return lax.ppermute(array, 'src', pairs)  57.5 us
    pallas_call x15, Pallas kernels, store(): pl.pallas_call(store_kernel, out_shape=jax.ShapeDtypeStruct(out.shape, ou...  20.3 us
  transfers between devices with their start and end apart: 43, of which 15 were waited for; matrix products, arithmetic and copies ran while one was open for 0% of the time, Pallas kernels for 24%

commit v1 on v0

--- a/solution.py
+++ b/solution.py
@@ -20,8 +20,9 @@
 WIDTHS = (384, 512, 256, 128)
 EARLY = (0, 1, 2, 3)
 LATE = (1, 0, 2, 3)
+SHARED = 2
 STEPS = (
-    [(0, c) for c in EARLY[1:]]
+    [(0, c) for c in LATE if c != SHARED]
     + [(1, c) for c in EARLY]
     + [(2, c) for c in LATE]
     + [(3, c) for c in LATE]
@@ -35,15 +36,20 @@
     return lax.ppermute(array, axis, pairs)
 
 
-def normalize_kernel(offset, strain_ref, mask_ref, lead_ref, trail_ref, flat_ref, held, rows):
+def normalize_kernel(offset, masks, strain_ref, *refs):
+    mask_ref = refs[0] if masks else None
+    lead_ref, trail_ref, flat_ref, held, rows = refs[masks:]
     samples = strain_ref.shape[0]
     columns = pl.ds(offset, flat_ref.shape[1])
     pltpu.sync_copy(strain_ref.at[:, columns], held)
-    alive = jnp.broadcast_to(mask_ref[...] > 0, held.shape)
+    if masks:
+        alive = jnp.broadcast_to(mask_ref[...] > 0, held.shape)
+        rows[HALF : HALF + samples] = jnp.where(
+            alive, held[...].astype(jnp.float32), 0.0
+        ).astype(jnp.bfloat16)
+    else:
+        rows[HALF : HALF + samples] = held[...]
     rows[:HALF] = lead_ref[...]
-    rows[HALF : HALF + samples] = jnp.where(
-        alive, held[...].astype(jnp.float32), 0.0
-    ).astype(jnp.bfloat16)
     rows[HALF + samples :] = trail_ref[...]
     out_rows = flat_ref.shape[0]
     row = lax.broadcasted_iota(jnp.int32, (TILE, TILE + SPAN), 0)
@@ -67,15 +73,18 @@
 
 def normalize_chunk(strain, mask, lead, trail, offset, width):
     samples = strain.shape[0]
+    masks = [] if mask is None else [mask]
 
     def block(rows):
         return pl.BlockSpec((pl.Element(rows), pl.Element(width)), lambda i: (0, offset))
 
     return pl.pallas_call(
-        functools.partial(normalize_kernel, offset),
+        functools.partial(normalize_kernel, offset, len(masks)),
         out_shape=jax.ShapeDtypeStruct((samples + HALF, width), jnp.bfloat16),
         grid=(1,),
-        in_specs=[pl.BlockSpec(memory_space=pltpu.HBM), block(1), block(HALF), block(SPAN)],
+        in_specs=[pl.BlockSpec(memory_space=pltpu.HBM)]
+        + [block(1)] * len(masks)
+        + [block(HALF), block(SPAN)],
         out_specs=pl.BlockSpec((samples + HALF, width), lambda i: (0, 0)),
         scratch_shapes=[
             pltpu.VMEM((samples, width), jnp.bfloat16),
@@ -88,7 +97,7 @@
             transcendentals=0,
         ),
         name="normalize",
-    )(strain, mask, lead, trail)
+    )(strain, *masks, lead, trail)
 
 
 def select_kernel(own, me_ref, index_ref, *refs):
@@ -347,8 +356,17 @@
     def masked(rows):
         return jnp.where(dead_mask > 0, rows, jnp.zeros((), rows.dtype))
 
-    lead = passed_along(masked(strain[samples - HALF :]), "win", 1)
-    trail = passed_along(masked(strain[:SPAN]), "win", -1)
+    def around(rows):
+        trail = passed_along(rows(0, SPAN), "win", -1)
+        lead = passed_along(rows(samples - HALF, samples), "win", 1)
+        return lead, trail
+
+    raw = jnp.where(
+        dead_mask[:, : WIDTHS[0]] > 0, strain[:, : WIDTHS[0]], jnp.zeros((), strain.dtype)
+    )
+    raw_out = hop(raw, outer)
+    raw_in = hop(raw, inner)
+    lead, trail = around(lambda a, b: masked(strain[a:b]))
     alive = (dead_mask > 0).astype(jnp.int32)
     flats = []
     for c in range(count):
@@ -372,9 +390,15 @@
     def hops(arrays, pairs):
         return [hop(a, pairs) for a in arrays]
 
-    first_out = hops(flats, outer)
-    first_in = hops(flats, inner)
-    swapped = hop(flats[0], across)
+    def received(chunk):
+        before, after = around(lambda a, b: chunk[a:b])
+        return normalize_chunk(chunk, None, before, after, 0, WIDTHS[0])
+
+    first_out = [received(raw_out)]
+    first_in = [received(raw_in)]
+    first_out += [hop(flats[c], outer) for c in range(1, count)]
+    first_in += [hop(flats[c], inner) for c in range(1, count)]
+    swapped = hop(flats[SHARED], across)
     second_out = hops(first_in, outward)
     second_in = hops(first_out, inner)
     third_out = hops(second_in, outward)
@@ -402,7 +426,7 @@
         nonlocal out
         out = store(*waiting.pop(0), out)
 
-    add(0, 0, 0, [flats[0]], [own_rows])
+    add(0, SHARED, 0, [flats[SHARED]], [own_rows])
     for slot, c in STEPS:
         chunk = arrivals[slot][c]
         if slot < line - 1:
@@ -414,7 +438,7 @@
             add(slot, c, 0, chunk, [own_rows])
         waiting.append((hop(made, across), here, place(slot, c, 1)))
         if (slot, c) == (0, count - 1):
-            add(0, 0, 1, [swapped], [own_rows])
+            add(0, SHARED, 1, [swapped], [own_rows])
         for _ in range(STORED.get((slot, c), 0)):
             keep()
     while waiting:

time: 425 us -> 404 us (0.951); the launches traced: 424 us -> 398 us
  waiting for transfers between devices: 243 us -> 194 us
  Pallas kernels: 115 us -> 128 us
  local copies, waits for them, and re-layouts: 2.07 us -> 7.95 us
    ppermute x41, waiting for transfers between devices: 242 us -> 187 us  [hop(): return lax.ppermute(array, 'src', pairs)]
    ppermute x2 -> x6, waiting for transfers between devices: 0.08 us -> 7.47 us  [passed_along(): return lax.ppermute(array, axis, pairs)]
    ppermute x2 -> x6, starting transfers between devices: 4.33 us -> 10.4 us  [passed_along(): return lax.ppermute(array, axis, pairs)]
    unnamed x26 -> x50, local copies, waits for them, and re-layouts: 1.27 us -> 7.13 us
    pallas_call x21, Pallas kernels: 81.3 us -> 87.1 us  [correlate(): pl.pallas_call(functools.partial(correlate_kernel, rows, len(operands) ==...]
    ppermute x41, starting transfers between devices: 57.5 us -> 52.8 us  [hop(): return lax.ppermute(array, 'src', pairs)]
    pallas_call x4 -> x6, Pallas kernels: 7.76 us -> 12 us  [normalize_chunk(): pl.pallas_call(functools.partial(normalize_kernel, offset, len(masks)), o...]
  transfers between devices with their start and end apart: 43 -> 47, of which waited for: 15 -> 18; matrix products, arithmetic and copies ran while one was open for 0% -> 1% of each run, Pallas kernels for 24% -> 29%
where the time goes in v1:
time: 404 us; the launch traced here: 398 us
  waiting for transfers between devices  194 us (48%)
  Pallas kernels  128 us (32%)
  starting transfers between devices  63.3 us (16%)
  local copies, waits for them, and re-layouts  7.95 us (2%)
  other arithmetic  4.73 us (1%)
    ppermute x41, waiting for transfers between devices, hop(): return lax.ppermute(array, 'src', pairs)  187 us
    pallas_call x21, Pallas kernels, correlate(): pl.pallas_call(functools.partial(correlate_kernel, rows, len(operands) ==...  87.1 us
    ppermute x41, starting transfers between devices, hop(): return lax.ppermute(array, 'src', pairs)  52.8 us
    pallas_call x15, Pallas kernels, store(): pl.pallas_call(store_kernel, out_shape=jax.ShapeDtypeStruct(out.shape, ou...  23.5 us
    pallas_call x6, Pallas kernels, normalize_chunk(): pl.pallas_call(functools.partial(normalize_kernel, offset, len(masks)), o...  12 us
    ppermute x6, starting transfers between devices, passed_along(): return lax.ppermute(array, axis, pairs)  10.4 us
  transfers between devices with their start and end apart: 47, of which 18 were waited for; matrix products, arithmetic and copies ran while one was open for 1% of the time, Pallas kernels for 29%

profile of v1, /device:TPU:0, one launch (start us, length us, event | category | flops | bytes accessed | tf_op | source)
XLA Modules:
  0.0 398.2 jit_solution(7825405867089455666)
XLA Ops:
  3.9 3.0 collective-permute-start
  18.3 3.1 collective-permute-start.2
  21.4 8.8 %collective-permute-done.2 = bf16[128,1536]{1,0:T(8,128)(2,1)S(1)} collective-permute-done((bf16[128,1536]{1,0:T(8,128)(2,1)S(1)}, bf16[128,1536]{1,0:T(8,128)(2,1)S(1)}, u32[]{:S(2)}, u32[]{:S(2)}) %collective-permute-start.2) | collective-permute-done | bytes 393248 | tf_op jit(solution)/shard_map/ppermute | solution.py:334
  44.1 24.3 %collective-permute-done.7.refs_2_ = bf16[1568,128]{1,0:T(8,128)(2,1)S(1)} collective-permute-done((bf16[1568,128]{1,0:T(8,128)(2,1)S(1)}, bf16[1568,128]{1,0:T(8,128)(2,1)S(1)}, u32[]{:S(2)}, u32[]{:S(2)}) %collective-permute-start.7) | collective-permute-done | bytes 401440 | tf_op jit(solution)/shard_map/ppermute | solution.py:334
  76.0 2.7 collective-permute-start.15
  83.8 34.1 %collective-permute-done.26.refs_2_ = bf16[1568,128]{1,0:T(8,128)(2,1)S(1)} collective-permute-done((bf16[1568,128]{1,0:T(8,128)(2,1)S(1)}, bf16[1568,128]{1,0:T(8,128)(2,1)S(1)}, u32[]{:S(2)}, u32[]{:S(2)}) %collective-permute-start.26) | collective-permute-done | bytes 401440 | tf_op jit(solution)/shard_map/ppermute | solution.py:334
  119.4 5.9 %correlate.26 = (f32[1,32,32,10240]{3,2,1,0:T(8,128)}, bf16[32,32,512]{2,1,0:T(8,128)(2,1)}) custom-call(s32[1]{0:T(128)} %bitcast.me_ref, bf16[1024,1664]{1,0:T(8,128)(2,1)S(1)} %hankel.3.refs_0_, bf16[1024,1664]{1,0:T(8,128)(2,1)S(1)} %hankel.2.refs_0_.refs_1_, bf16[1568,512]{1,0:T(8,128)(2,1)S(1)} %normalize.7.refs_1_.refs_2_, ...), custom_call_target="tpu_custom_call", output_to_operand_aliasing={{0}: (4, {})} | custom-call | flops 3489660928 | bytes 3702784 | tf_op jit(solution)/shard_map/correlate/pallas_call | solution.py:281
  125.3 5.6 %correlate.27 = (f32[1,32,32,10240]{3,2,1,0:T(8,128)}, bf16[32,32,384]{2,1,0:T(8,128)(2,1)}) custom-call(s32[1]{0:T(128)} %bitcast.me_ref, bf16[1024,1664]{1,0:T(8,128)(2,1)S(1)} %hankel.3.refs_0_, bf16[1024,1664]{1,0:T(8,128)(2,1)S(1)} %hankel.2.refs_0_.refs_1_, bf16[1568,384]{1,0:T(8,128)(2,1)S(1)} %normalize.6.refs_0_.refs_2_, ...), custom_call_target="tpu_custom_call", output_to_operand_aliasing={{0}: (4, {})} | custom-call | flops 2617245696 | bytes 2777088 | tf_op jit(solution)/shard_map/correlate/pallas_call | solution.py:281
  130.9 3.3 correlate.28
  135.8 6.2 %collective-permute-done.31.got_ref = bf16[32,32,128]{2,1,0:T(8,128)(2,1)S(1)} collective-permute-done((bf16[32,32,128]{2,1,0:T(8,128)(2,1)S(1)}, bf16[32,32,128]{2,1,0:T(8,128)(2,1)S(1)}, u32[]{:S(2)}, u32[]{:S(2)}) %collective-permute-start.31) | collective-permute-done | bytes 262176 | tf_op jit(solution)/shard_map/ppermute | solution.py:334
  158.8 4.5 %collective-permute-done.39.refs_1_ = bf16[64,384]{1,0:T(8,128)(2,1)S(1)} collective-permute-done((bf16[64,384]{1,0:T(8,128)(2,1)S(1)}, bf16[64,384]{1,0:T(8,128)(2,1)S(1)}, u32[]{:S(2)}, u32[]{:S(2)}) %collective-permute-start.39) | collective-permute-done | bytes 49184 | tf_op jit(solution)/shard_map/ppermute | solution.py:36
  164.7 3.2 collective-permute-done.9.refs_1_
  173.9 6.7 %correlate.30 = (f32[1,32,32,10240]{3,2,1,0:T(8,128)}, bf16[32,32,384]{2,1,0:T(8,128)(2,1)S(1)}) custom-call(s32[1]{0:T(128)} %bitcast.me_ref, bf16[1024,1664]{1,0:T(8,128)(2,1)S(1)} %hankel.3.refs_0_, bf16[1024,1664]{1,0:T(8,128)(2,1)S(1)} %hankel.2.refs_0_.refs_1_, bf16[1568,384]{1,0:T(8,128)(2,1)} %normalize.10.refs_2_, ...), custom_call_target="tpu_custom_call", output_to_operand_aliasing={{0}: (4, {})} | custom-call | flops 2617245696 | bytes 2777088 | tf_op jit(solution)/shard_map/correlate/pallas_call | solution.py:281
  182.4 7.4 %correlate.31 = (f32[1,32,32,10240]{3,2,1,0:T(8,128)}, bf16[32,32,512]{2,1,0:T(8,128)(2,1)}) custom-call(s32[1]{0:T(128)} %bitcast.me_ref, bf16[1024,1664]{1,0:T(8,128)(2,1)S(1)} %hankel.3.refs_0_, bf16[1024,1664]{1,0:T(8,128)(2,1)S(1)} %hankel.2.refs_0_.refs_1_, bf16[1568,512]{1,0:T(8,128)(2,1)} %collective-permute-done.21.refs_2_, ...), custom_call_target="tpu_custom_call", output_to_operand_aliasing={{0}: (4, {})} | custom-call | flops 3489660928 | bytes 3702784 | tf_op jit(solution)/shard_map/correlate/pallas_call | solution.py:281
  190.5 5.0 %correlate.32 = (f32[1,32,32,10240]{3,2,1,0:T(8,128)}, bf16[32,32,256]{2,1,0:T(8,128)(2,1)}) custom-call(s32[1]{0:T(128)} %bitcast.me_ref, bf16[1024,1664]{1,0:T(8,128)(2,1)S(1)} %hankel.3.refs_0_, bf16[1024,1664]{1,0:T(8,128)(2,1)S(1)} %hankel.2.refs_0_.refs_1_, bf16[1568,256]{1,0:T(8,128)(2,1)} %collective-permute-done.11.refs_2_, ...), custom_call_target="tpu_custom_call", output_to_operand_aliasing={{0}: (4, {})} | custom-call | flops 1744830464 | bytes 1851392 | tf_op jit(solution)/shard_map/correlate/pallas_call | solution.py:281
  197.1 3.3 correlate.33
  200.4 4.0 collective-permute-done.30.got_ref
  207.9 13.3 %collective-permute-done.41.got_ref = bf16[32,32,128]{2,1,0:T(8,128)(2,1)S(1)} collective-permute-done((bf16[32,32,128]{2,1,0:T(8,128)(2,1)S(1)}, bf16[32,32,128]{2,1,0:T(8,128)(2,1)S(1)}, u32[]{:S(2)}, u32[]{:S(2)}) %collective-permute-start.41) | collective-permute-done | bytes 262176 | tf_op jit(solution)/shard_map/ppermute | solution.py:334
  236.8 7.1 %correlate.34 = (f32[1,32,32,10240]{3,2,1,0:T(8,128)}, bf16[32,32,512]{2,1,0:T(8,128)(2,1)S(1)}) custom-call(s32[1]{0:T(128)} %bitcast.me_ref, bf16[1024,1664]{1,0:T(8,128)(2,1)S(1)} %hankel.3.refs_0_, bf16[1024,1664]{1,0:T(8,128)(2,1)S(1)} %hankel.2.refs_0_.refs_1_, ...), custom_call_target="tpu_custom_call", output_to_operand_aliasing={{0}: (5, {})} | custom-call | flops 3489660928 | bytes 3702784 | tf_op jit(solution)/shard_map/correlate/pallas_call | solution.py:281
  243.9 2.9 collective-permute-done.43.got_ref
  252.4 41.6 %collective-permute-done.40.refs_2_ = bf16[1568,384]{1,0:T(8,128)(2,1)} collective-permute-done((bf16[1568,384]{1,0:T(8,128)(2,1)}, bf16[1568,384]{1,0:T(8,128)(2,1)}, u32[]{:S(2)}, u32[]{:S(2)}) %collective-permute-start.40) | collective-permute-done | bytes 1204256 | tf_op jit(solution)/shard_map/ppermute | solution.py:334
  295.5 6.7 %correlate.35 = (f32[1,32,32,10240]{3,2,1,0:T(8,128)}, bf16[32,32,384]{2,1,0:T(8,128)(2,1)S(1)}) custom-call(s32[1]{0:T(128)} %bitcast.me_ref, bf16[1024,1664]{1,0:T(8,128)(2,1)S(1)} %hankel.3.refs_0_, bf16[1024,1664]{1,0:T(8,128)(2,1)S(1)} %hankel.2.refs_0_.refs_1_, ...), custom_call_target="tpu_custom_call", output_to_operand_aliasing={{0}: (5, {})} | custom-call | flops 2617245696 | bytes 2777088 | tf_op jit(solution)/shard_map/correlate/pallas_call | solution.py:281
  302.6 5.1 %correlate.24 = bf16[32,32,512]{2,1,0:T(8,128)(2,1)} custom-call(s32[1]{0:T(128)} %bitcast.me_ref, bf16[1024,1664]{1,0:T(8,128)(2,1)S(1)} %hankel.2.refs_0_.refs_1_, bf16[1568,512]{1,0:T(8,128)(2,1)} %collective-permute-done.23.refs_1_, bf16[1568,512]{1,0:T(8,128)(2,1)} %collective-permute-done.22.refs_2_), custom_call_target="tpu_custom_call" | custom-call | flops 1744830464 | bytes 3702784 | tf_op jit(solution)/shard_map/correlate/pallas_call | solution.py:281
  307.6 3.5 collective-permute-done.36.refs_2_
  311.4 3.6 correlate.36
  315.0 22.0 %collective-permute-done.19.refs_1_ = bf16[1568,384]{1,0:T(8,128)(2,1)S(1)} collective-permute-done((bf16[1568,384]{1,0:T(8,128)(2,1)S(1)}, bf16[1568,384]{1,0:T(8,128)(2,1)S(1)}, u32[]{:S(2)}, u32[]{:S(2)}) %collective-permute-start.19) | collective-permute-done | bytes 1204256 | tf_op jit(solution)/shard_map/ppermute | solution.py:334
  337.2 3.0 correlate.23
  343.5 3.3 correlate.37
  346.8 7.3 %collective-permute-done.13.refs_1_ = bf16[1568,256]{1,0:T(8,128)(2,1)S(1)} collective-permute-done((bf16[1568,256]{1,0:T(8,128)(2,1)S(1)}, bf16[1568,256]{1,0:T(8,128)(2,1)S(1)}, u32[]{:S(2)}, u32[]{:S(2)}) %collective-permute-start.13) | collective-permute-done | bytes 802848 | tf_op jit(solution)/shard_map/ppermute | solution.py:334
  362.7 13.9 %collective-permute-done.44.got_ref = bf16[32,32,128]{2,1,0:T(8,128)(2,1)S(1)} collective-permute-done((bf16[32,32,128]{2,1,0:T(8,128)(2,1)S(1)}, bf16[32,32,128]{2,1,0:T(8,128)(2,1)S(1)}, u32[]{:S(2)}, u32[]{:S(2)}) %collective-permute-start.44) | collective-permute-done | bytes 262176 | tf_op jit(solution)/shard_map/ppermute | solution.py:334
  377.3 5.2 %correlate.38.refs_3_ = f32[1,32,32,10240]{3,2,1,0:T(8,128)} custom-call(s32[1]{0:T(128)} %bitcast.me_ref, bf16[1024,1664]{1,0:T(8,128)(2,1)S(1)} %hankel.3.refs_0_, bf16[1568,512]{1,0:T(8,128)(2,1)} %collective-permute-done.23.refs_1_, bf16[1568,512]{1,0:T(8,128)(2,1)} %collective-permute-done.22.refs_2_, ...), custom_call_target="tpu_custom_call", output_to_operand_aliasing={{}: (4, {})} | custom-call | flops 1744830464 | bytes 3702784 | tf_op jit(solution)/shard_map/correlate/pallas_call | solution.py:281
  382.6 3.1 correlate.39.kept_ref
  (171 shorter events, 125.0 us)
Async XLA Ops:
  37.5 38.5 %collective-permute-start.29 = (bf16[1568,256]{1,0:T(8,128)(2,1)S(1)}, bf16[1568,256]{1,0:T(8,128)(2,1)S(1)}, u32[]{:S(2)}, u32[]{:S(2)}) collective-permute-start(bf16[1568,256]{1,0:T(8,128)(2,1)S(1)} %normalize.8.refs_2_.refs_1_), channel_id=1, source_target_pairs={{0,1},{1,0},{2,3},{3,2},{4,5},{5,4},{6,7},{7,6},{8,9},{9,8},{10,11... | collective-permute-start | bytes 2408456 | tf_op jit(solution)/shard_map/ppermute | solution.py:334
  39.0 41.9 %collective-permute-start.11 = (bf16[1568,256]{1,0:T(8,128)(2,1)S(1)}, bf16[1568,256]{1,0:T(8,128)(2,1)}, u32[]{:S(2)}, u32[]{:S(2)}) collective-permute-start(bf16[1568,256]{1,0:T(8,128)(2,1)S(1)} %normalize.8.refs_2_.refs_1_), channel_id=1, source_target_pairs={{0,2},{1,3},{2,0},{3,1},{4,6},{5,7},{6,4},{7,5},{8,10},{9,11},{10,... | collective-permute-start | bytes 2408456 | tf_op jit(solution)/shard_map/ppermute | solution.py:334
  39.7 28.6 %collective-permute-start.7 = (bf16[1568,128]{1,0:T(8,128)(2,1)S(1)}, bf16[1568,128]{1,0:T(8,128)(2,1)S(1)}, u32[]{:S(2)}, u32[]{:S(2)}) collective-permute-start(bf16[1568,128]{1,0:T(8,128)(2,1)S(1)} %normalize.9.refs_3_.refs_2_), channel_id=1, source_target_pairs={{0,2},{1,3},{2,0},{3,1},{4,6},{5,7},{6,4},{7,5},{8,10},{9,11},{10,... | collective-permute-start | bytes 1204232 | tf_op jit(solution)/shard_map/ppermute | solution.py:334
  42.6 40.2 %collective-permute-start.35 = (bf16[1568,256]{1,0:T(8,128)(2,1)S(1)}, bf16[1568,256]{1,0:T(8,128)(2,1)S(1)}, u32[]{:S(2)}, u32[]{:S(2)}) collective-permute-start(bf16[1568,256]{1,0:T(8,128)(2,1)S(1)} %normalize.8.refs_2_.refs_1_), channel_id=1, source_target_pairs={{2,4},{3,5},{4,2},{5,3},{10,12},{11,13},{12,10},{13,11},{18,20},{1... | collective-permute-start | bytes 2408456 | tf_op jit(solution)/shard_map/ppermute | solution.py:334
  43.3 27.9 %collective-permute-start.25 = (bf16[1568,128]{1,0:T(8,128)(2,1)S(1)}, bf16[1568,128]{1,0:T(8,128)(2,1)S(1)}, u32[]{:S(2)}, u32[]{:S(2)}) collective-permute-start(bf16[1568,128]{1,0:T(8,128)(2,1)S(1)} %normalize.9.refs_3_.refs_2_), channel_id=1, source_target_pairs={{2,4},{3,5},{4,2},{5,3},{10,12},{11,13},{12,10},{13,11},{18,20},{1... | collective-permute-start | bytes 1204232 | tf_op jit(solution)/shard_map/ppermute | solution.py:334
  71.3 74.6 %collective-permute-start.21 = (bf16[1568,512]{1,0:T(8,128)(2,1)S(1)}, bf16[1568,512]{1,0:T(8,128)(2,1)}, u32[]{:S(2)}, u32[]{:S(2)}) collective-permute-start(bf16[1568,512]{1,0:T(8,128)(2,1)S(1)} %normalize.7.refs_1_.refs_2_), channel_id=1, source_target_pairs={{0,2},{1,3},{2,0},{3,1},{4,6},{5,7},{6,4},{7,5},{8,10},{9,11},{10,... | collective-permute-start | bytes 4816904 | tf_op jit(solution)/shard_map/ppermute | solution.py:334
  73.4 44.5 %collective-permute-start.26 = (bf16[1568,128]{1,0:T(8,128)(2,1)S(1)}, bf16[1568,128]{1,0:T(8,128)(2,1)S(1)}, u32[]{:S(2)}, u32[]{:S(2)}) collective-permute-start(bf16[1568,128]{1,0:T(8,128)(2,1)S(1)} %collective-permute-done.25.refs_3_), channel_id=1, source_target_pairs={{2,0},{3,1},{4,6},{5,7},{10,8},{11,9},{12,14},{13,15},{18,16},{19,... | collective-permute-start | bytes 1204232 | tf_op jit(solution)/shard_map/ppermute | solution.py:334
  76.0 67.9 %collective-permute-start.15 = (bf16[1536,384]{1,0:T(8,128)(2,1)S(1)}, bf16[1536,384]{1,0:T(8,128)(2,1)S(1)}, u32[]{:S(2)}, u32[]{:S(2)}) collective-permute-start(bf16[1536,384]{1,0:T(8,128)(2,1)S(1)} %slice_select_fusion), channel_id=1, source_target_pairs={{0,2},{1,3},{2,0},{3,1},{4,6},{5,7},{6,4},{7,5},{8,10},{9,11},{10,... | collective-permute-start | bytes 3538952 | tf_op jit(solution)/shard_map/ppermute | solution.py:334
  80.9 66.8 %collective-permute-start.37 = (bf16[1536,384]{1,0:T(8,128)(2,1)S(1)}, bf16[1536,384]{1,0:T(8,128)(2,1)S(1)}, u32[]{:S(2)}, u32[]{:S(2)}) collective-permute-start(bf16[1536,384]{1,0:T(8,128)(2,1)S(1)} %slice_select_fusion), channel_id=1, source_target_pairs={{2,4},{3,5},{4,2},{5,3},{10,12},{11,13},{12,10},{13,11},{18,20},{1... | collective-permute-start | bytes 3538952 | tf_op jit(solution)/shard_map/ppermute | solution.py:334
  82.9 98.2 %collective-permute-start.27 = (bf16[1568,512]{1,0:T(8,128)(2,1)S(1)}, bf16[1568,512]{1,0:T(8,128)(2,1)S(1)}, u32[]{:S(2)}, u32[]{:S(2)}) collective-permute-start(bf16[1568,512]{1,0:T(8,128)(2,1)S(1)} %normalize.7.refs_1_.refs_2_), channel_id=1, source_target_pairs={{2,4},{3,5},{4,2},{5,3},{10,12},{11,13},{12,10},{13,11},{18,20},{1... | collective-permute-start | bytes 4816904 | tf_op jit(solution)/shard_map/ppermute | solution.py:334
  141.9 38.6 %collective-permute-start.32 = (bf16[32,32,384]{2,1,0:T(8,128)(2,1)}, bf16[32,32,384]{2,1,0:T(8,128)(2,1)}, u32[]{:S(2)}, u32[]{:S(2)}) collective-permute-start(bf16[32,32,384]{2,1,0:T(8,128)(2,1)} %get-tuple-element.36), channel_id=1, source_target_pairs={{0,1},{1,0},{2,3},{3,2},{4,5},{5,4},{6,7},{7,6},{8,9},{9,8},{10,11... | collective-permute-start | bytes 2359304 | tf_op jit(solution)/shard_map/ppermute | solution.py:334
  143.8 24.1 %collective-permute-start.9 = (bf16[1568,128]{1,0:T(8,128)(2,1)S(1)}, bf16[1568,128]{1,0:T(8,128)(2,1)S(1)}, u32[]{:S(2)}, u32[]{:S(2)}) collective-permute-start(bf16[1568,128]{1,0:T(8,128)(2,1)S(1)} %collective-permute-done.8.refs_2_), channel_id=1, source_target_pairs={{2,0},{3,1},{4,6},{5,7},{10,8},{11,9},{12,14},{13,15},{18,16},{19,... | collective-permute-start | bytes 1204232 | tf_op jit(solution)/shard_map/ppermute | solution.py:334
  145.9 60.7 %collective-permute-start.22 = (bf16[1568,512]{1,0:T(8,128)(2,1)}, bf16[1568,512]{1,0:T(8,128)(2,1)}, u32[]{:S(2)}, u32[]{:S(2)}) collective-permute-start(bf16[1568,512]{1,0:T(8,128)(2,1)} %collective-permute-done.21.refs_2_), channel_id=1, source_target_pairs={{2,4},{3,5},{4,2},{5,3},{10,12},{11,13},{12,10},{13,11},{18,20},{1... | collective-permute-start | bytes 4816904 | tf_op jit(solution)/shard_map/ppermute | solution.py:334
  163.4 32.2 %collective-permute-start.33 = (bf16[32,32,512]{2,1,0:T(8,128)(2,1)}, bf16[32,32,512]{2,1,0:T(8,128)(2,1)}, u32[]{:S(2)}, u32[]{:S(2)}) collective-permute-start(bf16[32,32,512]{2,1,0:T(8,128)(2,1)} %get-tuple-element.37), channel_id=1, source_target_pairs={{0,1},{1,0},{2,3},{3,2},{4,5},{5,4},{6,7},{7,6},{8,9},{9,8},{10,11... | collective-permute-start | bytes 3145736 | tf_op jit(solution)/shard_map/ppermute | solution.py:334
  180.6 23.8 %collective-permute-start.30 = (bf16[32,32,384]{2,1,0:T(8,128)(2,1)S(1)}, bf16[32,32,384]{2,1,0:T(8,128)(2,1)S(1)}, u32[]{:S(2)}, u32[]{:S(2)}) collective-permute-start(bf16[32,32,384]{2,1,0:T(8,128)(2,1)S(1)} %get-tuple-element.34), channel_id=1, source_target_pairs={{0,1},{1,0},{2,3},{3,2},{4,5},{5,4},{6,7},{7,6},{8,9},{9,8},{10,11... | collective-permute-start | bytes 2359304 | tf_op jit(solution)/shard_map/ppermute | solution.py:334
  181.1 54.4 %collective-permute-start.28 = (bf16[1568,512]{1,0:T(8,128)(2,1)S(1)}, bf16[1568,512]{1,0:T(8,128)(2,1)}, u32[]{:S(2)}, u32[]{:S(2)}) collective-permute-start(bf16[1568,512]{1,0:T(8,128)(2,1)S(1)} %collective-permute-done.27.refs_3_), channel_id=1, source_target_pairs={{2,0},{3,1},{4,6},{5,7},{10,8},{11,9},{12,14},{13,15},{18,16},{19,... | collective-permute-start | bytes 4816904 | tf_op jit(solution)/shard_map/ppermute | solution.py:334
  189.8 44.1 %collective-permute-start.18 = (bf16[1568,384]{1,0:T(8,128)(2,1)}, bf16[1568,384]{1,0:T(8,128)(2,1)S(1)}, u32[]{:S(2)}, u32[]{:S(2)}) collective-permute-start(bf16[1568,384]{1,0:T(8,128)(2,1)} %normalize.10.refs_2_), channel_id=1, source_target_pairs={{2,4},{3,5},{4,2},{5,3},{10,12},{11,13},{12,10},{13,11},{18,20},{1... | collective-permute-start | bytes 3612680 | tf_op jit(solution)/shard_map/ppermute | solution.py:334
  195.5 29.9 %collective-permute-start.42 = (bf16[32,32,256]{2,1,0:T(8,128)(2,1)}, bf16[32,32,256]{2,1,0:T(8,128)(2,1)}, u32[]{:S(2)}, u32[]{:S(2)}) collective-permute-start(bf16[32,32,256]{2,1,0:T(8,128)(2,1)} %get-tuple-element.44), channel_id=1, source_target_pairs={{0,1},{1,0},{2,3},{3,2},{4,5},{5,4},{6,7},{7,6},{8,9},{9,8},{10,11... | collective-permute-start | bytes 1572872 | tf_op jit(solution)/shard_map/ppermute | solution.py:334
  206.6 95.7 %collective-permute-start.23 = (bf16[1568,512]{1,0:T(8,128)(2,1)}, bf16[1568,512]{1,0:T(8,128)(2,1)}, u32[]{:S(2)}, u32[]{:S(2)}) collective-permute-start(bf16[1568,512]{1,0:T(8,128)(2,1)} %collective-permute-done.22.refs_2_), channel_id=1, source_target_pairs={{2,0},{3,1},{4,6},{5,7},{10,8},{11,9},{12,14},{13,15},{18,16},{19,... | collective-permute-start | bytes 4816904 | tf_op jit(solution)/shard_map/ppermute | solution.py:334
  221.9 24.9 %collective-permute-start.43 = (bf16[32,32,512]{2,1,0:T(8,128)(2,1)}, bf16[32,32,512]{2,1,0:T(8,128)(2,1)S(1)}, u32[]{:S(2)}, u32[]{:S(2)}) collective-permute-start(bf16[32,32,512]{2,1,0:T(8,128)(2,1)} %get-tuple-element.45), channel_id=1, source_target_pairs={{0,1},{1,0},{2,3},{3,2},{4,5},{5,4},{6,7},{7,6},{8,9},{9,8},{10,11... | collective-permute-start | bytes 3145736 | tf_op jit(solution)/shard_map/ppermute | solution.py:334
  225.4 68.6 %collective-permute-start.40 = (bf16[1568,384]{1,0:T(8,128)(2,1)}, bf16[1568,384]{1,0:T(8,128)(2,1)}, u32[]{:S(2)}, u32[]{:S(2)}) collective-permute-start(bf16[1568,384]{1,0:T(8,128)(2,1)} %normalize.11.refs_3_), channel_id=1, source_target_pairs={{2,0},{3,1},{4,6},{5,7},{10,8},{11,9},{12,14},{13,15},{18,16},{19,... | collective-permute-start | bytes 3612680 | tf_op jit(solution)/shard_map/ppermute | solution.py:334
  234.2 76.9 %collective-permute-start.36 = (bf16[1568,256]{1,0:T(8,128)(2,1)S(1)}, bf16[1568,256]{1,0:T(8,128)(2,1)S(1)}, u32[]{:S(2)}, u32[]{:S(2)}) collective-permute-start(bf16[1568,256]{1,0:T(8,128)(2,1)S(1)} %copy-done.14), channel_id=1, source_target_pairs={{2,0},{3,1},{4,6},{5,7},{10,8},{11,9},{12,14},{13,15},{18,16},{19,... | collective-permute-start | bytes 2408456 | tf_op jit(solution)/shard_map/ppermute | solution.py:334
  235.5 101.4 %collective-permute-start.19 = (bf16[1568,384]{1,0:T(8,128)(2,1)S(1)}, bf16[1568,384]{1,0:T(8,128)(2,1)S(1)}, u32[]{:S(2)}, u32[]{:S(2)}) collective-permute-start(bf16[1568,384]{1,0:T(8,128)(2,1)S(1)} %collective-permute-done.18.refs_2_), channel_id=1, source_target_pairs={{2,0},{3,1},{4,6},{5,7},{10,8},{11,9},{12,14},{13,15},{18,16},{19,... | collective-permute-start | bytes 3612680 | tf_op jit(solution)/shard_map/ppermute | solution.py:334
  246.8 93.5 %collective-permute-start.34 = (bf16[32,32,512]{2,1,0:T(8,128)(2,1)S(1)}, bf16[32,32,512]{2,1,0:T(8,128)(2,1)S(1)}, u32[]{:S(2)}, u32[]{:S(2)}) collective-permute-start(bf16[32,32,512]{2,1,0:T(8,128)(2,1)S(1)} %get-tuple-element.42), channel_id=1, source_target_pairs={{0,1},{1,0},{2,3},{3,2},{4,5},{5,4},{6,7},{7,6},{8,9},{9,8},{10,11... | collective-permute-start | bytes 3145736 | tf_op jit(solution)/shard_map/ppermute | solution.py:334
  294.0 60.1 %collective-permute-start.13 = (bf16[1568,256]{1,0:T(8,128)(2,1)S(1)}, bf16[1568,256]{1,0:T(8,128)(2,1)S(1)}, u32[]{:S(2)}, u32[]{:S(2)}) collective-permute-start(bf16[1568,256]{1,0:T(8,128)(2,1)S(1)} %copy-done.2), channel_id=1, source_target_pairs={{2,0},{3,1},{4,6},{5,7},{10,8},{11,9},{12,14},{13,15},{18,16},{19,... | collective-permute-start | bytes 2408456 | tf_op jit(solution)/shard_map/ppermute | solution.py:334
  302.3 54.2 %collective-permute-start.46 = (bf16[32,32,384]{2,1,0:T(8,128)(2,1)S(1)}, bf16[32,32,384]{2,1,0:T(8,128)(2,1)S(1)}, u32[]{:S(2)}, u32[]{:S(2)}) collective-permute-start(bf16[32,32,384]{2,1,0:T(8,128)(2,1)S(1)} %get-tuple-element.51), channel_id=1, source_target_pairs={{0,1},{1,0},{2,3},{3,2},{4,5},{5,4},{6,7},{7,6},{8,9},{9,8},{10,11... | collective-permute-start | bytes 2359304 | tf_op jit(solution)/shard_map/ppermute | solution.py:334
  311.1 74.6 %collective-permute-start.24 = (bf16[32,32,512]{2,1,0:T(8,128)(2,1)}, bf16[32,32,512]{2,1,0:T(8,128)(2,1)}, u32[]{:S(2)}, u32[]{:S(2)}) collective-permute-start(bf16[32,32,512]{2,1,0:T(8,128)(2,1)} %correlate.24), channel_id=1, source_target_pairs={{0,1},{1,0},{2,3},{3,2},{4,5},{5,4},{6,7},{7,6},{8,9},{9,8},{10,11... | collective-permute-start | bytes 3145736 | tf_op jit(solution)/shard_map/ppermute | solution.py:334
  336.9 24.5 %collective-permute-start.45 = (bf16[32,32,256]{2,1,0:T(8,128)(2,1)S(1)}, bf16[32,32,256]{2,1,0:T(8,128)(2,1)S(1)}, u32[]{:S(2)}, u32[]{:S(2)}) collective-permute-start(bf16[32,32,256]{2,1,0:T(8,128)(2,1)S(1)} %get-tuple-element.50), channel_id=1, source_target_pairs={{0,1},{1,0},{2,3},{3,2},{4,5},{5,4},{6,7},{7,6},{8,9},{9,8},{10,11... | collective-permute-start | bytes 1572872 | tf_op jit(solution)/shard_map/ppermute | solution.py:334
  340.2 52.1 %collective-permute-start.20 = (bf16[32,32,384]{2,1,0:T(8,128)(2,1)}, bf16[32,32,384]{2,1,0:T(8,128)(2,1)}, u32[]{:S(2)}, u32[]{:S(2)}) collective-permute-start(bf16[32,32,384]{2,1,0:T(8,128)(2,1)} %correlate.23), channel_id=1, source_target_pairs={{0,1},{1,0},{2,3},{3,2},{4,5},{5,4},{6,7},{7,6},{8,9},{9,8},{10,11... | collective-permute-start | bytes 2359304 | tf_op jit(solution)/shard_map/ppermute | solution.py:334
  354.1 22.4 %collective-permute-start.44 = (bf16[32,32,128]{2,1,0:T(8,128)(2,1)S(1)}, bf16[32,32,128]{2,1,0:T(8,128)(2,1)S(1)}, u32[]{:S(2)}, u32[]{:S(2)}) collective-permute-start(bf16[32,32,128]{2,1,0:T(8,128)(2,1)S(1)} %get-tuple-element.49), channel_id=1, source_target_pairs={{0,1},{1,0},{2,3},{3,2},{4,5},{5,4},{6,7},{7,6},{8,9},{9,8},{10,11... | collective-permute-start | bytes 786440 | tf_op jit(solution)/shard_map/ppermute | solution.py:334
  356.5 38.0 %collective-permute-start.14 = (bf16[32,32,256]{2,1,0:T(8,128)(2,1)}, bf16[32,32,256]{2,1,0:T(8,128)(2,1)}, u32[]{:S(2)}, u32[]{:S(2)}) collective-permute-start(bf16[32,32,256]{2,1,0:T(8,128)(2,1)} %correlate.22), channel_id=1, source_target_pairs={{0,1},{1,0},{2,3},{3,2},{4,5},{5,4},{6,7},{7,6},{8,9},{9,8},{10,11... | collective-permute-start | bytes 1572872 | tf_op jit(solution)/shard_map/ppermute | solution.py:334
  361.4 35.1 %collective-permute-start.10 = (bf16[32,32,128]{2,1,0:T(8,128)(2,1)}, bf16[32,32,128]{2,1,0:T(8,128)(2,1)}, u32[]{:S(2)}, u32[]{:S(2)}) collective-permute-start(bf16[32,32,128]{2,1,0:T(8,128)(2,1)} %correlate.21), channel_id=1, source_target_pairs={{0,1},{1,0},{2,3},{3,2},{4,5},{5,4},{6,7},{7,6},{8,9},{9,8},{10,11... | collective-permute-start | bytes 786440 | tf_op jit(solution)/shard_map/ppermute | solution.py:334
  (40 other events, 436.6 us)

commit v2 on v1

--- a/solution.py
+++ b/solution.py
@@ -16,6 +16,7 @@
 SPAN = 2 * HALF
 ROWS = 512
 VMEM_BYTES = 24 << 20
+NORMALIZE_BYTES = 50 << 20
 
 WIDTHS = (384, 512, 256, 128)
 EARLY = (0, 1, 2, 3)
@@ -36,64 +37,72 @@
     return lax.ppermute(array, axis, pairs)
 
 
-def normalize_kernel(offset, masks, strain_ref, *refs):
+def normalize_kernel(widths, masks, strain_ref, *refs):
     mask_ref = refs[0] if masks else None
-    lead_ref, trail_ref, flat_ref, held, rows = refs[masks:]
+    lead_ref, trail_ref = refs[masks : masks + 2]
+    flats = refs[masks + 2 : -3]
+    held, rows, arrived = refs[-3:]
     samples = strain_ref.shape[0]
-    columns = pl.ds(offset, flat_ref.shape[1])
-    pltpu.sync_copy(strain_ref.at[:, columns], held)
-    if masks:
-        alive = jnp.broadcast_to(mask_ref[...] > 0, held.shape)
-        rows[HALF : HALF + samples] = jnp.where(
-            alive, held[...].astype(jnp.float32), 0.0
-        ).astype(jnp.bfloat16)
-    else:
-        rows[HALF : HALF + samples] = held[...]
-    rows[:HALF] = lead_ref[...]
-    rows[HALF + samples :] = trail_ref[...]
-    out_rows = flat_ref.shape[0]
+    offsets = [sum(widths[:c]) for c in range(len(widths))]
+    copies = [
+        pltpu.make_async_copy(
+            strain_ref.at[:, pl.ds(offset, width)],
+            held.at[:, pl.ds(offset, width)],
+            arrived.at[c],
+        )
+        for c, (offset, width) in enumerate(zip(offsets, widths))
+    ]
+    for copy in copies:
+        copy.start()
     row = lax.broadcasted_iota(jnp.int32, (TILE, TILE + SPAN), 0)
     col = lax.broadcasted_iota(jnp.int32, (TILE, TILE + SPAN), 1)
     band = jnp.where((col >= row) & (col <= row + SPAN), 1.0, 0.0).astype(jnp.bfloat16)
-    for start in range(0, out_rows, TILE):
-        count = min(TILE, out_rows - start)
-        near = rows[start : start + count + SPAN]
-        sums = jnp.dot(
-            band[:count, : count + SPAN], jnp.abs(near), preferred_element_type=jnp.float32
-        )
-        center = rows[start + HALF : start + HALF + count].astype(jnp.float32)
-        flat_ref[start : start + count] = (
-            center / (sums / (2 * HALF + 1) + EPSILON)
-        ).astype(jnp.bfloat16)
+    for copy, flat_ref, offset, width in zip(copies, flats, offsets, widths):
+        columns = slice(offset, offset + width)
+        copy.wait()
+        center = held[:, columns]
+        if masks:
+            alive = jnp.broadcast_to(mask_ref[:, columns] > 0, center.shape)
+            center = jnp.where(alive, center.astype(jnp.float32), 0.0).astype(jnp.bfloat16)
+        rows[:HALF, :width] = lead_ref[:, columns]
+        rows[HALF : HALF + samples, :width] = center
+        rows[HALF + samples :, :width] = trail_ref[:, columns]
+        out_rows = flat_ref.shape[0]
+        for start in range(0, out_rows, TILE):
+            count = min(TILE, out_rows - start)
+            near = rows[start : start + count + SPAN, :width]
+            sums = jnp.dot(
+                band[:count, : count + SPAN], jnp.abs(near), preferred_element_type=jnp.float32
+            )
+            middle = rows[start + HALF : start + HALF + count, :width].astype(jnp.float32)
+            flat_ref[start : start + count] = (
+                middle / (sums / (2 * HALF + 1) + EPSILON)
+            ).astype(jnp.bfloat16)
 
 
 def params():
     return pltpu.CompilerParams(vmem_limit_bytes=VMEM_BYTES)
 
 
-def normalize_chunk(strain, mask, lead, trail, offset, width):
-    samples = strain.shape[0]
+def normalize_chunks(strain, mask, lead, trail, widths):
+    samples, channels = strain.shape
     masks = [] if mask is None else [mask]
-
-    def block(rows):
-        return pl.BlockSpec((pl.Element(rows), pl.Element(width)), lambda i: (0, offset))
-
+    whole = pl.BlockSpec(memory_space=pltpu.VMEM)
+    shapes = [(samples + HALF, width) for width in widths]
     return pl.pallas_call(
-        functools.partial(normalize_kernel, offset, len(masks)),
-        out_shape=jax.ShapeDtypeStruct((samples + HALF, width), jnp.bfloat16),
-        grid=(1,),
-        in_specs=[pl.BlockSpec(memory_space=pltpu.HBM)]
-        + [block(1)] * len(masks)
-        + [block(HALF), block(SPAN)],
-        out_specs=pl.BlockSpec((samples + HALF, width), lambda i: (0, 0)),
+        functools.partial(normalize_kernel, widths, len(masks)),
+        out_shape=[jax.ShapeDtypeStruct(shape, jnp.bfloat16) for shape in shapes],
+        in_specs=[pl.BlockSpec(memory_space=pltpu.HBM)] + [whole] * (len(masks) + 2),
+        out_specs=[whole] * len(widths),
         scratch_shapes=[
-            pltpu.VMEM((samples, width), jnp.bfloat16),
-            pltpu.VMEM((samples + HALF + SPAN, width), jnp.bfloat16),
+            pltpu.VMEM((samples, channels), jnp.bfloat16),
+            pltpu.VMEM((samples + HALF + SPAN, max(widths)), jnp.bfloat16),
+            pltpu.SemaphoreType.DMA((len(widths),)),
         ],
-        compiler_params=pltpu.CompilerParams(vmem_limit_bytes=52 << 20),
+        compiler_params=pltpu.CompilerParams(vmem_limit_bytes=NORMALIZE_BYTES),
         cost_estimate=pl.CostEstimate(
-            flops=2 * (samples + HALF) * (TILE + SPAN) * width,
-            bytes_accessed=4 * samples * width,
+            flops=2 * (samples + HALF) * (TILE + SPAN) * channels,
+            bytes_accessed=4 * samples * channels,
             transcendentals=0,
         ),
         name="normalize",
@@ -216,13 +225,13 @@
 
             @pl.when(end)
             def _():
-                held[:depth] = first[...]
+                pltpu.sync_copy(first, held.at[pl.ds(0, depth)])
 
             @pl.when(jnp.logical_not(end))
             def _():
-                held[:depth] = second[...]
+                pltpu.sync_copy(second, held.at[pl.ds(0, depth)])
         else:
-            held[:depth] = first[...]
+            pltpu.sync_copy(first, held.at[pl.ds(0, depth)])
 
     def product(ref, at):
         lagged = ref[pl.ds(pl.multiple_of(at * ROWS, ROWS), ROWS), :]
@@ -252,7 +261,7 @@
     skip = (rows - 1) * each
     resident = pl.BlockSpec(memory_space=pltpu.VMEM)
     in_specs = [resident] * rows
-    in_specs += [pl.BlockSpec((depth, width), lambda i, me: (0, 0))] * len(operands)
+    in_specs += [pl.BlockSpec(memory_space=pl.ANY)] * len(operands)
     arguments = [*hankels, *operands]
     aliases = {}
     if out is not None and not sent:
@@ -368,11 +377,7 @@
     raw_in = hop(raw, inner)
     lead, trail = around(lambda a, b: masked(strain[a:b]))
     alive = (dead_mask > 0).astype(jnp.int32)
-    flats = []
-    for c in range(count):
-        flats.append(
-            normalize_chunk(strain, alive, lead, trail, offsets[c], WIDTHS[c])
-        )
+    flats = normalize_chunks(strain, alive, lead, trail, WIDTHS)
 
     here = jnp.reshape(me, (1,)).astype(jnp.int32)
     theirs, mine = select_sources(flats, src_index, here, samples, own)
@@ -392,7 +397,8 @@
 
     def received(chunk):
         before, after = around(lambda a, b: chunk[a:b])
-        return normalize_chunk(chunk, None, before, after, 0, WIDTHS[0])
+        (flat,) = normalize_chunks(chunk, None, before, after, WIDTHS[:1])
+        return flat
 
     first_out = [received(raw_out)]
     first_in = [received(raw_in)]

time: 404 us -> 399 us (0.988); the launches traced: 398 us -> 398 us
    pallas_call x6 -> x3, Pallas kernels: 12 us -> 8.14 us  [normalize_chunks(): pl.pallas_call(functools.partial(normalize_kernel, widths, len(masks)), o...]
where the time goes in v2:
time: 399 us; the launch traced here: 398 us
  waiting for transfers between devices  194 us (49%)
  Pallas kernels  126 us (32%)
  starting transfers between devices  65.4 us (16%)
  local copies, waits for them, and re-layouts  6.79 us (2%)
  other arithmetic  4.73 us (1%)
    ppermute x41, waiting for transfers between devices, hop(): return lax.ppermute(array, 'src', pairs)  185 us
    pallas_call x21, Pallas kernels, correlate(): pl.pallas_call(functools.partial(correlate_kernel, rows, len(operands) ==...  87 us
    ppermute x41, starting transfers between devices, hop(): return lax.ppermute(array, 'src', pairs)  54.8 us
    pallas_call x15, Pallas kernels, store(): pl.pallas_call(store_kernel, out_shape=jax.ShapeDtypeStruct(out.shape, ou...  23.5 us
    ppermute x6, starting transfers between devices, passed_along(): return lax.ppermute(array, axis, pairs)  10.5 us
    ppermute x6, waiting for transfers between devices, passed_along(): return lax.ppermute(array, axis, pairs)  9.08 us
    pallas_call x3, Pallas kernels, normalize_chunks(): pl.pallas_call(functools.partial(normalize_kernel, widths, len(masks)), o...  8.14 us
  transfers between devices with their start and end apart: 47, of which 18 were waited for; matrix products, arithmetic and copies ran while one was open for 1% of the time, Pallas kernels for 29%

profile of v2, /device:TPU:0, one launch (start us, length us, event | category | flops | bytes accessed | tf_op | source)
XLA Modules:
  0.0 397.6 jit_solution(8335778996564514278)
XLA Ops:
  3.9 3.0 collective-permute-start
  7.8 5.0 %normalize.3 = (bf16[1568,384]{1,0:T(8,128)(2,1)S(1)}, bf16[1568,512]{1,0:T(8,128)(2,1)}, bf16[1568,256]{1,0:T(8,128)(2,1)S(1)}, bf16[1568,128]{1,0:T(8,128)(2,1)S(1)}) custom-call(bf16[1536,1280]{1,0:T(8,128)(2,1)} %strain_ref.1, s32[1,1280]{1,0:T(1,128)S(1)} %get-tuple-element.65.refs_0_, bf16[32,1280]{1,0:T(8,128)(2,1)S(1)} %collective-permute-done.refs_1_, ...), custom_call_target="tpu_custom_call" | custom-call | flops 1027604480 | bytes 7864320 | tf_op jit(solution)/shard_map/normalize/pallas_call | solution.py:92
  12.8 4.7 %select.3 = (bf16[128,1536]{1,0:T(8,128)(2,1)S(1)}, bf16[128,1536]{1,0:T(8,128)(2,1)S(1)}) custom-call(s32[1]{0:T(128)} %bitcast.me_ref, s32[256,1]{1,0:T(8,128)S(1)} %copy.35.index_ref, bf16[1568,384]{1,0:T(8,128)(2,1)S(1)} %get-tuple-element.33.refs_0_.refs_2_, bf16[1568,512]{1,0:T(8,128)(2,1)} %get-tuple-element.34.refs_1_.refs_2_, ...), custom_call_target="tpu_custom_call" | custom-call | flops 1006632960 | bytes 3932160 | tf_op jit(solution)/shard_map/select/pallas_call | solution.py:145
  17.5 3.1 collective-permute-start.2
  20.6 8.8 %collective-permute-done.2 = bf16[128,1536]{1,0:T(8,128)(2,1)S(1)} collective-permute-done((bf16[128,1536]{1,0:T(8,128)(2,1)S(1)}, bf16[128,1536]{1,0:T(8,128)(2,1)S(1)}, u32[]{:S(2)}, u32[]{:S(2)}) %collective-permute-start.2) | collective-permute-done | bytes 393248 | tf_op jit(solution)/shard_map/ppermute | solution.py:343
  43.3 24.3 %collective-permute-done.7.refs_2_ = bf16[1568,128]{1,0:T(8,128)(2,1)S(1)} collective-permute-done((bf16[1568,128]{1,0:T(8,128)(2,1)S(1)}, bf16[1568,128]{1,0:T(8,128)(2,1)S(1)}, u32[]{:S(2)}, u32[]{:S(2)}) %collective-permute-start.7) | collective-permute-done | bytes 401440 | tf_op jit(solution)/shard_map/ppermute | solution.py:343
  83.0 34.4 %collective-permute-done.26.refs_2_ = bf16[1568,128]{1,0:T(8,128)(2,1)S(1)} collective-permute-done((bf16[1568,128]{1,0:T(8,128)(2,1)S(1)}, bf16[1568,128]{1,0:T(8,128)(2,1)S(1)}, u32[]{:S(2)}, u32[]{:S(2)}) %collective-permute-start.26) | collective-permute-done | bytes 401440 | tf_op jit(solution)/shard_map/ppermute | solution.py:343
  118.8 7.2 %correlate.26 = (f32[1,32,32,10240]{3,2,1,0:T(8,128)}, bf16[32,32,512]{2,1,0:T(8,128)(2,1)}) custom-call(s32[1]{0:T(128)} %bitcast.me_ref, bf16[1024,1664]{1,0:T(8,128)(2,1)S(1)} %hankel.3.refs_0_, bf16[1024,1664]{1,0:T(8,128)(2,1)S(1)} %hankel.2.refs_0_.refs_1_, ...), custom_call_target="tpu_custom_call", output_to_operand_aliasing={{0}: (4, {})} | custom-call | flops 3489660928 | bytes 3702784 | tf_op jit(solution)/shard_map/correlate/pallas_call | solution.py:290
  126.0 5.8 %correlate.27 = (f32[1,32,32,10240]{3,2,1,0:T(8,128)}, bf16[32,32,384]{2,1,0:T(8,128)(2,1)}) custom-call(s32[1]{0:T(128)} %bitcast.me_ref, bf16[1024,1664]{1,0:T(8,128)(2,1)S(1)} %hankel.3.refs_0_, bf16[1024,1664]{1,0:T(8,128)(2,1)S(1)} %hankel.2.refs_0_.refs_1_, ...), custom_call_target="tpu_custom_call", output_to_operand_aliasing={{0}: (4, {})} | custom-call | flops 2617245696 | bytes 2777088 | tf_op jit(solution)/shard_map/correlate/pallas_call | solution.py:290
  131.9 3.5 correlate.28
  136.9 5.5 %collective-permute-done.31.got_ref = bf16[32,32,128]{2,1,0:T(8,128)(2,1)S(1)} collective-permute-done((bf16[32,32,128]{2,1,0:T(8,128)(2,1)S(1)}, bf16[32,32,128]{2,1,0:T(8,128)(2,1)S(1)}, u32[]{:S(2)}, u32[]{:S(2)}) %collective-permute-start.31) | collective-permute-done | bytes 262176 | tf_op jit(solution)/shard_map/ppermute | solution.py:343
  155.7 3.6 collective-permute-done.17.refs_1_
  160.6 4.6 %collective-permute-done.39.refs_1_ = bf16[64,384]{1,0:T(8,128)(2,1)S(1)} collective-permute-done((bf16[64,384]{1,0:T(8,128)(2,1)S(1)}, bf16[64,384]{1,0:T(8,128)(2,1)S(1)}, u32[]{:S(2)}, u32[]{:S(2)}) %collective-permute-start.39) | collective-permute-done | bytes 49184 | tf_op jit(solution)/shard_map/ppermute | solution.py:37
  171.3 5.6 %correlate.30 = (f32[1,32,32,10240]{3,2,1,0:T(8,128)}, bf16[32,32,384]{2,1,0:T(8,128)(2,1)S(1)}) custom-call(s32[1]{0:T(128)} %bitcast.me_ref, bf16[1024,1664]{1,0:T(8,128)(2,1)S(1)} %hankel.3.refs_0_, bf16[1024,1664]{1,0:T(8,128)(2,1)S(1)} %hankel.2.refs_0_.refs_1_, bf16[1568,384]{1,0:T(8,128)(2,1)S(1)} %normalize.4.refs_2_, ...), custom_call_target="tpu_custom_call", output_to_operand_aliasing={{0}: (4, {})} | custom-call | flops 2617245696 | bytes 2777088 | tf_op jit(solution)/shard_map/correlate/pallas_call | solution.py:290
  178.8 7.3 %correlate.31 = (f32[1,32,32,10240]{3,2,1,0:T(8,128)}, bf16[32,32,512]{2,1,0:T(8,128)(2,1)}) custom-call(s32[1]{0:T(128)} %bitcast.me_ref, bf16[1024,1664]{1,0:T(8,128)(2,1)S(1)} %hankel.3.refs_0_, bf16[1024,1664]{1,0:T(8,128)(2,1)S(1)} %hankel.2.refs_0_.refs_1_, bf16[1568,512]{1,0:T(8,128)(2,1)} %collective-permute-done.21.refs_2_, ...), custom_call_target="tpu_custom_call", output_to_operand_aliasing={{0}: (4, {})} | custom-call | flops 3489660928 | bytes 3702784 | tf_op jit(solution)/shard_map/correlate/pallas_call | solution.py:290
  186.8 4.8 %correlate.32 = (f32[1,32,32,10240]{3,2,1,0:T(8,128)}, bf16[32,32,256]{2,1,0:T(8,128)(2,1)}) custom-call(s32[1]{0:T(128)} %bitcast.me_ref, bf16[1024,1664]{1,0:T(8,128)(2,1)S(1)} %hankel.3.refs_0_, bf16[1024,1664]{1,0:T(8,128)(2,1)S(1)} %hankel.2.refs_0_.refs_1_, bf16[1568,256]{1,0:T(8,128)(2,1)} %collective-permute-done.11.refs_2_, ...), custom_call_target="tpu_custom_call", output_to_operand_aliasing={{0}: (4, {})} | custom-call | flops 1744830464 | bytes 1851392 | tf_op jit(solution)/shard_map/correlate/pallas_call | solution.py:290
  193.1 3.5 correlate.33
  196.6 9.9 %collective-permute-done.30.got_ref = bf16[32,32,384]{2,1,0:T(8,128)(2,1)S(1)} collective-permute-done((bf16[32,32,384]{2,1,0:T(8,128)(2,1)S(1)}, bf16[32,32,384]{2,1,0:T(8,128)(2,1)S(1)}, u32[]{:S(2)}, u32[]{:S(2)}) %collective-permute-start.30) | collective-permute-done | bytes 786464 | tf_op jit(solution)/shard_map/ppermute | solution.py:343
  210.3 13.0 %collective-permute-done.41.got_ref = bf16[32,32,128]{2,1,0:T(8,128)(2,1)S(1)} collective-permute-done((bf16[32,32,128]{2,1,0:T(8,128)(2,1)S(1)}, bf16[32,32,128]{2,1,0:T(8,128)(2,1)S(1)}, u32[]{:S(2)}, u32[]{:S(2)}) %collective-permute-start.41) | collective-permute-done | bytes 262176 | tf_op jit(solution)/shard_map/ppermute | solution.py:343
  239.2 7.0 %correlate.34 = (f32[1,32,32,10240]{3,2,1,0:T(8,128)}, bf16[32,32,512]{2,1,0:T(8,128)(2,1)S(1)}) custom-call(s32[1]{0:T(128)} %bitcast.me_ref, bf16[1024,1664]{1,0:T(8,128)(2,1)S(1)} %hankel.3.refs_0_, bf16[1024,1664]{1,0:T(8,128)(2,1)S(1)} %hankel.2.refs_0_.refs_1_, ...), custom_call_target="tpu_custom_call", output_to_operand_aliasing={{0}: (5, {})} | custom-call | flops 3489660928 | bytes 3702784 | tf_op jit(solution)/shard_map/correlate/pallas_call | solution.py:290
  255.0 36.5 %collective-permute-done.40.refs_2_ = bf16[1568,384]{1,0:T(8,128)(2,1)} collective-permute-done((bf16[1568,384]{1,0:T(8,128)(2,1)}, bf16[1568,384]{1,0:T(8,128)(2,1)}, u32[]{:S(2)}, u32[]{:S(2)}) %collective-permute-start.40) | collective-permute-done | bytes 1204256 | tf_op jit(solution)/shard_map/ppermute | solution.py:343
  293.0 6.6 %correlate.35 = (f32[1,32,32,10240]{3,2,1,0:T(8,128)}, bf16[32,32,384]{2,1,0:T(8,128)(2,1)S(1)}) custom-call(s32[1]{0:T(128)} %bitcast.me_ref, bf16[1024,1664]{1,0:T(8,128)(2,1)S(1)} %hankel.3.refs_0_, bf16[1024,1664]{1,0:T(8,128)(2,1)S(1)} %hankel.2.refs_0_.refs_1_, ...), custom_call_target="tpu_custom_call", output_to_operand_aliasing={{0}: (5, {})} | custom-call | flops 2617245696 | bytes 2777088 | tf_op jit(solution)/shard_map/correlate/pallas_call | solution.py:290
  300.2 4.5 %correlate.24 = bf16[32,32,512]{2,1,0:T(8,128)(2,1)} custom-call(s32[1]{0:T(128)} %bitcast.me_ref, bf16[1024,1664]{1,0:T(8,128)(2,1)S(1)} %hankel.2.refs_0_.refs_1_, bf16[1568,512]{1,0:T(8,128)(2,1)} %collective-permute-done.23.refs_1_, bf16[1568,512]{1,0:T(8,128)(2,1)} %collective-permute-done.22.refs_2_), custom_call_target="tpu_custom_call" | custom-call | flops 1744830464 | bytes 3702784 | tf_op jit(solution)/shard_map/correlate/pallas_call | solution.py:290
  304.7 3.9 collective-permute-done.36.refs_2_
  309.2 3.6 correlate.36
  312.7 21.7 %collective-permute-done.19.refs_1_ = bf16[1568,384]{1,0:T(8,128)(2,1)S(1)} collective-permute-done((bf16[1568,384]{1,0:T(8,128)(2,1)S(1)}, bf16[1568,384]{1,0:T(8,128)(2,1)S(1)}, u32[]{:S(2)}, u32[]{:S(2)}) %collective-permute-start.19) | collective-permute-done | bytes 1204256 | tf_op jit(solution)/shard_map/ppermute | solution.py:343
  335.0 3.2 correlate.23
  341.2 3.5 correlate.37
  344.7 6.9 %collective-permute-done.13.refs_1_ = bf16[1568,256]{1,0:T(8,128)(2,1)S(1)} collective-permute-done((bf16[1568,256]{1,0:T(8,128)(2,1)S(1)}, bf16[1568,256]{1,0:T(8,128)(2,1)S(1)}, u32[]{:S(2)}, u32[]{:S(2)}) %collective-permute-start.13) | collective-permute-done | bytes 802848 | tf_op jit(solution)/shard_map/ppermute | solution.py:343
  360.6 15.6 %collective-permute-done.44.got_ref = bf16[32,32,128]{2,1,0:T(8,128)(2,1)S(1)} collective-permute-done((bf16[32,32,128]{2,1,0:T(8,128)(2,1)S(1)}, bf16[32,32,128]{2,1,0:T(8,128)(2,1)S(1)}, u32[]{:S(2)}, u32[]{:S(2)}) %collective-permute-start.44) | collective-permute-done | bytes 262176 | tf_op jit(solution)/shard_map/ppermute | solution.py:343
  377.0 4.6 %correlate.38.refs_3_ = f32[1,32,32,10240]{3,2,1,0:T(8,128)} custom-call(s32[1]{0:T(128)} %bitcast.me_ref, bf16[1024,1664]{1,0:T(8,128)(2,1)S(1)} %hankel.3.refs_0_, bf16[1568,512]{1,0:T(8,128)(2,1)} %collective-permute-done.23.refs_1_, bf16[1568,512]{1,0:T(8,128)(2,1)} %collective-permute-done.22.refs_2_, ...), custom_call_target="tpu_custom_call", output_to_operand_aliasing={{}: (4, {})} | custom-call | flops 1744830464 | bytes 3702784 | tf_op jit(solution)/shard_map/correlate/pallas_call | solution.py:290
  381.7 3.3 correlate.39.kept_ref
  (166 shorter events, 118.7 us)
Async XLA Ops:
  36.7 38.5 %collective-permute-start.29 = (bf16[1568,256]{1,0:T(8,128)(2,1)S(1)}, bf16[1568,256]{1,0:T(8,128)(2,1)S(1)}, u32[]{:S(2)}, u32[]{:S(2)}) collective-permute-start(bf16[1568,256]{1,0:T(8,128)(2,1)S(1)} %get-tuple-element.35.refs_2_.refs_1_), channel_id=1, source_target_pairs={{0,1},{1,0},{2,3},{3,2},{4,5},{5,4},{6,7},{7,6},{8,9},{9,8},{10,11... | collective-permute-start | bytes 2408456 | tf_op jit(solution)/shard_map/ppermute | solution.py:343
  38.3 41.8 %collective-permute-start.11 = (bf16[1568,256]{1,0:T(8,128)(2,1)S(1)}, bf16[1568,256]{1,0:T(8,128)(2,1)}, u32[]{:S(2)}, u32[]{:S(2)}) collective-permute-start(bf16[1568,256]{1,0:T(8,128)(2,1)S(1)} %get-tuple-element.35.refs_2_.refs_1_), channel_id=1, source_target_pairs={{0,2},{1,3},{2,0},{3,1},{4,6},{5,7},{6,4},{7,5},{8,10},{9,11},{10,... | collective-permute-start | bytes 2408456 | tf_op jit(solution)/shard_map/ppermute | solution.py:343
  38.9 28.6 %collective-permute-start.7 = (bf16[1568,128]{1,0:T(8,128)(2,1)S(1)}, bf16[1568,128]{1,0:T(8,128)(2,1)S(1)}, u32[]{:S(2)}, u32[]{:S(2)}) collective-permute-start(bf16[1568,128]{1,0:T(8,128)(2,1)S(1)} %get-tuple-element.36.refs_3_.refs_2_), channel_id=1, source_target_pairs={{0,2},{1,3},{2,0},{3,1},{4,6},{5,7},{6,4},{7,5},{8,10},{9,11},{10,... | collective-permute-start | bytes 1204232 | tf_op jit(solution)/shard_map/ppermute | solution.py:343
  41.9 40.2 %collective-permute-start.35 = (bf16[1568,256]{1,0:T(8,128)(2,1)S(1)}, bf16[1568,256]{1,0:T(8,128)(2,1)S(1)}, u32[]{:S(2)}, u32[]{:S(2)}) collective-permute-start(bf16[1568,256]{1,0:T(8,128)(2,1)S(1)} %get-tuple-element.35.refs_2_.refs_1_), channel_id=1, source_target_pairs={{2,4},{3,5},{4,2},{5,3},{10,12},{11,13},{12,10},{13,11},{18,20},{1... | collective-permute-start | bytes 2408456 | tf_op jit(solution)/shard_map/ppermute | solution.py:343
  42.6 27.9 %collective-permute-start.25 = (bf16[1568,128]{1,0:T(8,128)(2,1)S(1)}, bf16[1568,128]{1,0:T(8,128)(2,1)S(1)}, u32[]{:S(2)}, u32[]{:S(2)}) collective-permute-start(bf16[1568,128]{1,0:T(8,128)(2,1)S(1)} %get-tuple-element.36.refs_3_.refs_2_), channel_id=1, source_target_pairs={{2,4},{3,5},{4,2},{5,3},{10,12},{11,13},{12,10},{13,11},{18,20},{1... | collective-permute-start | bytes 1204232 | tf_op jit(solution)/shard_map/ppermute | solution.py:343
  70.5 76.5 %collective-permute-start.21 = (bf16[1568,512]{1,0:T(8,128)(2,1)}, bf16[1568,512]{1,0:T(8,128)(2,1)}, u32[]{:S(2)}, u32[]{:S(2)}) collective-permute-start(bf16[1568,512]{1,0:T(8,128)(2,1)} %get-tuple-element.34.refs_1_.refs_2_), channel_id=1, source_target_pairs={{0,2},{1,3},{2,0},{3,1},{4,6},{5,7},{6,4},{7,5},{8,10},{9,11},{10,... | collective-permute-start | bytes 4816904 | tf_op jit(solution)/shard_map/ppermute | solution.py:343
  72.6 44.8 %collective-permute-start.26 = (bf16[1568,128]{1,0:T(8,128)(2,1)S(1)}, bf16[1568,128]{1,0:T(8,128)(2,1)S(1)}, u32[]{:S(2)}, u32[]{:S(2)}) collective-permute-start(bf16[1568,128]{1,0:T(8,128)(2,1)S(1)} %collective-permute-done.25.refs_3_), channel_id=1, source_target_pairs={{2,0},{3,1},{4,6},{5,7},{10,8},{11,9},{12,14},{13,15},{18,16},{19,... | collective-permute-start | bytes 1204232 | tf_op jit(solution)/shard_map/ppermute | solution.py:343
  75.2 69.8 %collective-permute-start.15 = (bf16[1536,384]{1,0:T(8,128)(2,1)S(1)}, bf16[1536,384]{1,0:T(8,128)(2,1)S(1)}, u32[]{:S(2)}, u32[]{:S(2)}) collective-permute-start(bf16[1536,384]{1,0:T(8,128)(2,1)S(1)} %slice_select_fusion), channel_id=1, source_target_pairs={{0,2},{1,3},{2,0},{3,1},{4,6},{5,7},{6,4},{7,5},{8,10},{9,11},{10,... | collective-permute-start | bytes 3538952 | tf_op jit(solution)/shard_map/ppermute | solution.py:343
  80.1 68.7 %collective-permute-start.37 = (bf16[1536,384]{1,0:T(8,128)(2,1)S(1)}, bf16[1536,384]{1,0:T(8,128)(2,1)S(1)}, u32[]{:S(2)}, u32[]{:S(2)}) collective-permute-start(bf16[1536,384]{1,0:T(8,128)(2,1)S(1)} %slice_select_fusion), channel_id=1, source_target_pairs={{2,4},{3,5},{4,2},{5,3},{10,12},{11,13},{12,10},{13,11},{18,20},{1... | collective-permute-start | bytes 3538952 | tf_op jit(solution)/shard_map/ppermute | solution.py:343
  82.1 95.3 %collective-permute-start.27 = (bf16[1568,512]{1,0:T(8,128)(2,1)}, bf16[1568,512]{1,0:T(8,128)(2,1)S(1)}, u32[]{:S(2)}, u32[]{:S(2)}) collective-permute-start(bf16[1568,512]{1,0:T(8,128)(2,1)} %get-tuple-element.34.refs_1_.refs_2_), channel_id=1, source_target_pairs={{2,4},{3,5},{4,2},{5,3},{10,12},{11,13},{12,10},{13,11},{18,20},{1... | collective-permute-start | bytes 4816904 | tf_op jit(solution)/shard_map/ppermute | solution.py:343
  143.0 33.9 %collective-permute-start.32 = (bf16[32,32,384]{2,1,0:T(8,128)(2,1)}, bf16[32,32,384]{2,1,0:T(8,128)(2,1)}, u32[]{:S(2)}, u32[]{:S(2)}) collective-permute-start(bf16[32,32,384]{2,1,0:T(8,128)(2,1)} %get-tuple-element.44), channel_id=1, source_target_pairs={{0,1},{1,0},{2,3},{3,2},{4,5},{5,4},{6,7},{7,6},{8,9},{9,8},{10,11... | collective-permute-start | bytes 2359304 | tf_op jit(solution)/shard_map/ppermute | solution.py:343
  144.9 22.2 %collective-permute-start.9 = (bf16[1568,128]{1,0:T(8,128)(2,1)S(1)}, bf16[1568,128]{1,0:T(8,128)(2,1)S(1)}, u32[]{:S(2)}, u32[]{:S(2)}) collective-permute-start(bf16[1568,128]{1,0:T(8,128)(2,1)S(1)} %collective-permute-done.8.refs_2_), channel_id=1, source_target_pairs={{2,0},{3,1},{4,6},{5,7},{10,8},{11,9},{12,14},{13,15},{18,16},{19,... | collective-permute-start | bytes 1204232 | tf_op jit(solution)/shard_map/ppermute | solution.py:343
  147.0 62.0 %collective-permute-start.22 = (bf16[1568,512]{1,0:T(8,128)(2,1)}, bf16[1568,512]{1,0:T(8,128)(2,1)}, u32[]{:S(2)}, u32[]{:S(2)}) collective-permute-start(bf16[1568,512]{1,0:T(8,128)(2,1)} %collective-permute-done.21.refs_2_), channel_id=1, source_target_pairs={{2,4},{3,5},{4,2},{5,3},{10,12},{11,13},{12,10},{13,11},{18,20},{1... | collective-permute-start | bytes 4816904 | tf_op jit(solution)/shard_map/ppermute | solution.py:343
  165.1 26.4 %collective-permute-start.33 = (bf16[32,32,512]{2,1,0:T(8,128)(2,1)}, bf16[32,32,512]{2,1,0:T(8,128)(2,1)}, u32[]{:S(2)}, u32[]{:S(2)}) collective-permute-start(bf16[32,32,512]{2,1,0:T(8,128)(2,1)} %get-tuple-element.45), channel_id=1, source_target_pairs={{0,1},{1,0},{2,3},{3,2},{4,5},{5,4},{6,7},{7,6},{8,9},{9,8},{10,11... | collective-permute-start | bytes 3145736 | tf_op jit(solution)/shard_map/ppermute | solution.py:343
  176.9 29.5 %collective-permute-start.30 = (bf16[32,32,384]{2,1,0:T(8,128)(2,1)S(1)}, bf16[32,32,384]{2,1,0:T(8,128)(2,1)S(1)}, u32[]{:S(2)}, u32[]{:S(2)}) collective-permute-start(bf16[32,32,384]{2,1,0:T(8,128)(2,1)S(1)} %get-tuple-element.42), channel_id=1, source_target_pairs={{0,1},{1,0},{2,3},{3,2},{4,5},{5,4},{6,7},{7,6},{8,9},{9,8},{10,11... | collective-permute-start | bytes 2359304 | tf_op jit(solution)/shard_map/ppermute | solution.py:343
  177.5 60.5 %collective-permute-start.28 = (bf16[1568,512]{1,0:T(8,128)(2,1)S(1)}, bf16[1568,512]{1,0:T(8,128)(2,1)}, u32[]{:S(2)}, u32[]{:S(2)}) collective-permute-start(bf16[1568,512]{1,0:T(8,128)(2,1)S(1)} %collective-permute-done.27.refs_3_), channel_id=1, source_target_pairs={{2,0},{3,1},{4,6},{5,7},{10,8},{11,9},{12,14},{13,15},{18,16},{19,... | collective-permute-start | bytes 4816904 | tf_op jit(solution)/shard_map/ppermute | solution.py:343
  186.0 50.2 %collective-permute-start.18 = (bf16[1568,384]{1,0:T(8,128)(2,1)S(1)}, bf16[1568,384]{1,0:T(8,128)(2,1)S(1)}, u32[]{:S(2)}, u32[]{:S(2)}) collective-permute-start(bf16[1568,384]{1,0:T(8,128)(2,1)S(1)} %normalize.4.refs_2_), channel_id=1, source_target_pairs={{2,4},{3,5},{4,2},{5,3},{10,12},{11,13},{12,10},{13,11},{18,20},{1... | collective-permute-start | bytes 3612680 | tf_op jit(solution)/shard_map/ppermute | solution.py:343
  191.6 36.2 %collective-permute-start.42 = (bf16[32,32,256]{2,1,0:T(8,128)(2,1)}, bf16[32,32,256]{2,1,0:T(8,128)(2,1)}, u32[]{:S(2)}, u32[]{:S(2)}) collective-permute-start(bf16[32,32,256]{2,1,0:T(8,128)(2,1)} %get-tuple-element.52), channel_id=1, source_target_pairs={{0,1},{1,0},{2,3},{3,2},{4,5},{5,4},{6,7},{7,6},{8,9},{9,8},{10,11... | collective-permute-start | bytes 1572872 | tf_op jit(solution)/shard_map/ppermute | solution.py:343
  209.0 90.7 %collective-permute-start.23 = (bf16[1568,512]{1,0:T(8,128)(2,1)}, bf16[1568,512]{1,0:T(8,128)(2,1)}, u32[]{:S(2)}, u32[]{:S(2)}) collective-permute-start(bf16[1568,512]{1,0:T(8,128)(2,1)} %collective-permute-done.22.refs_2_), channel_id=1, source_target_pairs={{2,0},{3,1},{4,6},{5,7},{10,8},{11,9},{12,14},{13,15},{18,16},{19,... | collective-permute-start | bytes 4816904 | tf_op jit(solution)/shard_map/ppermute | solution.py:343
  224.0 25.2 %collective-permute-start.43 = (bf16[32,32,512]{2,1,0:T(8,128)(2,1)}, bf16[32,32,512]{2,1,0:T(8,128)(2,1)S(1)}, u32[]{:S(2)}, u32[]{:S(2)}) collective-permute-start(bf16[32,32,512]{2,1,0:T(8,128)(2,1)} %get-tuple-element.53), channel_id=1, source_target_pairs={{0,1},{1,0},{2,3},{3,2},{4,5},{5,4},{6,7},{7,6},{8,9},{9,8},{10,11... | collective-permute-start | bytes 3145736 | tf_op jit(solution)/shard_map/ppermute | solution.py:343
  227.8 63.8 %collective-permute-start.40 = (bf16[1568,384]{1,0:T(8,128)(2,1)}, bf16[1568,384]{1,0:T(8,128)(2,1)}, u32[]{:S(2)}, u32[]{:S(2)}) collective-permute-start(bf16[1568,384]{1,0:T(8,128)(2,1)} %normalize.5.refs_3_), channel_id=1, source_target_pairs={{2,0},{3,1},{4,6},{5,7},{10,8},{11,9},{12,14},{13,15},{18,16},{19,... | collective-permute-start | bytes 3612680 | tf_op jit(solution)/shard_map/ppermute | solution.py:343
  236.6 72.0 %collective-permute-start.36 = (bf16[1568,256]{1,0:T(8,128)(2,1)S(1)}, bf16[1568,256]{1,0:T(8,128)(2,1)S(1)}, u32[]{:S(2)}, u32[]{:S(2)}) collective-permute-start(bf16[1568,256]{1,0:T(8,128)(2,1)S(1)} %copy-done.11), channel_id=1, source_target_pairs={{2,0},{3,1},{4,6},{5,7},{10,8},{11,9},{12,14},{13,15},{18,16},{19,... | collective-permute-start | bytes 2408456 | tf_op jit(solution)/shard_map/ppermute | solution.py:343
  237.9 96.5 %collective-permute-start.19 = (bf16[1568,384]{1,0:T(8,128)(2,1)S(1)}, bf16[1568,384]{1,0:T(8,128)(2,1)S(1)}, u32[]{:S(2)}, u32[]{:S(2)}) collective-permute-start(bf16[1568,384]{1,0:T(8,128)(2,1)S(1)} %collective-permute-done.18.refs_2_), channel_id=1, source_target_pairs={{2,0},{3,1},{4,6},{5,7},{10,8},{11,9},{12,14},{13,15},{18,16},{19,... | collective-permute-start | bytes 3612680 | tf_op jit(solution)/shard_map/ppermute | solution.py:343
  249.2 89.0 %collective-permute-start.34 = (bf16[32,32,512]{2,1,0:T(8,128)(2,1)S(1)}, bf16[32,32,512]{2,1,0:T(8,128)(2,1)S(1)}, u32[]{:S(2)}, u32[]{:S(2)}) collective-permute-start(bf16[32,32,512]{2,1,0:T(8,128)(2,1)S(1)} %get-tuple-element.50), channel_id=1, source_target_pairs={{0,1},{1,0},{2,3},{3,2},{4,5},{5,4},{6,7},{7,6},{8,9},{9,8},{10,11... | collective-permute-start | bytes 3145736 | tf_op jit(solution)/shard_map/ppermute | solution.py:343
  291.5 60.1 %collective-permute-start.13 = (bf16[1568,256]{1,0:T(8,128)(2,1)S(1)}, bf16[1568,256]{1,0:T(8,128)(2,1)S(1)}, u32[]{:S(2)}, u32[]{:S(2)}) collective-permute-start(bf16[1568,256]{1,0:T(8,128)(2,1)S(1)} %copy-done.1), channel_id=1, source_target_pairs={{2,0},{3,1},{4,6},{5,7},{10,8},{11,9},{12,14},{13,15},{18,16},{19,... | collective-permute-start | bytes 2408456 | tf_op jit(solution)/shard_map/ppermute | solution.py:343
  299.6 54.6 %collective-permute-start.46 = (bf16[32,32,384]{2,1,0:T(8,128)(2,1)S(1)}, bf16[32,32,384]{2,1,0:T(8,128)(2,1)S(1)}, u32[]{:S(2)}, u32[]{:S(2)}) collective-permute-start(bf16[32,32,384]{2,1,0:T(8,128)(2,1)S(1)} %get-tuple-element.59), channel_id=1, source_target_pairs={{0,1},{1,0},{2,3},{3,2},{4,5},{5,4},{6,7},{7,6},{8,9},{9,8},{10,11... | collective-permute-start | bytes 2359304 | tf_op jit(solution)/shard_map/ppermute | solution.py:343
  308.6 76.4 %collective-permute-start.24 = (bf16[32,32,512]{2,1,0:T(8,128)(2,1)}, bf16[32,32,512]{2,1,0:T(8,128)(2,1)}, u32[]{:S(2)}, u32[]{:S(2)}) collective-permute-start(bf16[32,32,512]{2,1,0:T(8,128)(2,1)} %correlate.24), channel_id=1, source_target_pairs={{0,1},{1,0},{2,3},{3,2},{4,5},{5,4},{6,7},{7,6},{8,9},{9,8},{10,11... | collective-permute-start | bytes 3145736 | tf_op jit(solution)/shard_map/ppermute | solution.py:343
  334.4 24.6 %collective-permute-start.45 = (bf16[32,32,256]{2,1,0:T(8,128)(2,1)S(1)}, bf16[32,32,256]{2,1,0:T(8,128)(2,1)S(1)}, u32[]{:S(2)}, u32[]{:S(2)}) collective-permute-start(bf16[32,32,256]{2,1,0:T(8,128)(2,1)S(1)} %get-tuple-element.58), channel_id=1, source_target_pairs={{0,1},{1,0},{2,3},{3,2},{4,5},{5,4},{6,7},{7,6},{8,9},{9,8},{10,11... | collective-permute-start | bytes 1572872 | tf_op jit(solution)/shard_map/ppermute | solution.py:343
  338.2 53.6 %collective-permute-start.20 = (bf16[32,32,384]{2,1,0:T(8,128)(2,1)}, bf16[32,32,384]{2,1,0:T(8,128)(2,1)}, u32[]{:S(2)}, u32[]{:S(2)}) collective-permute-start(bf16[32,32,384]{2,1,0:T(8,128)(2,1)} %correlate.23), channel_id=1, source_target_pairs={{0,1},{1,0},{2,3},{3,2},{4,5},{5,4},{6,7},{7,6},{8,9},{9,8},{10,11... | collective-permute-start | bytes 2359304 | tf_op jit(solution)/shard_map/ppermute | solution.py:343
  351.6 24.6 %collective-permute-start.44 = (bf16[32,32,128]{2,1,0:T(8,128)(2,1)S(1)}, bf16[32,32,128]{2,1,0:T(8,128)(2,1)S(1)}, u32[]{:S(2)}, u32[]{:S(2)}) collective-permute-start(bf16[32,32,128]{2,1,0:T(8,128)(2,1)S(1)} %get-tuple-element.57), channel_id=1, source_target_pairs={{0,1},{1,0},{2,3},{3,2},{4,5},{5,4},{6,7},{7,6},{8,9},{9,8},{10,11... | collective-permute-start | bytes 786440 | tf_op jit(solution)/shard_map/ppermute | solution.py:343
  354.3 39.7 %collective-permute-start.14 = (bf16[32,32,256]{2,1,0:T(8,128)(2,1)}, bf16[32,32,256]{2,1,0:T(8,128)(2,1)}, u32[]{:S(2)}, u32[]{:S(2)}) collective-permute-start(bf16[32,32,256]{2,1,0:T(8,128)(2,1)} %correlate.22), channel_id=1, source_target_pairs={{0,1},{1,0},{2,3},{3,2},{4,5},{5,4},{6,7},{7,6},{8,9},{9,8},{10,11... | collective-permute-start | bytes 1572872 | tf_op jit(solution)/shard_map/ppermute | solution.py:343
  359.1 36.9 %collective-permute-start.10 = (bf16[32,32,128]{2,1,0:T(8,128)(2,1)}, bf16[32,32,128]{2,1,0:T(8,128)(2,1)}, u32[]{:S(2)}, u32[]{:S(2)}) collective-permute-start(bf16[32,32,128]{2,1,0:T(8,128)(2,1)} %correlate.21), channel_id=1, source_target_pairs={{0,1},{1,0},{2,3},{3,2},{4,5},{5,4},{6,7},{7,6},{8,9},{9,8},{10,11... | collective-permute-start | bytes 786440 | tf_op jit(solution)/shard_map/ppermute | solution.py:343
  (39 other events, 360.5 us)

commit v3 on v2

--- a/solution.py
+++ b/solution.py
@@ -18,9 +18,9 @@
 VMEM_BYTES = 24 << 20
 NORMALIZE_BYTES = 50 << 20
 
-WIDTHS = (384, 512, 256, 128)
-EARLY = (0, 1, 2, 3)
-LATE = (1, 0, 2, 3)
+WIDTHS = (384, 384, 256, 128, 128)
+EARLY = (0, 1, 2, 3, 4)
+LATE = (0, 1, 2, 3, 4)
 SHARED = 2
 STEPS = (
     [(0, c) for c in LATE if c != SHARED]
@@ -28,7 +28,7 @@
     + [(2, c) for c in LATE]
     + [(3, c) for c in LATE]
 )
-STORED = {(1, 3): 4, (2, 1): 3, (2, 2): 1, (2, 3): 3, (3, 0): 1}
+STORED = {(1, 4): 5, (2, 0): 3, (2, 1): 1, (2, 2): 1, (2, 4): 3, (3, 0): 2, (3, 3): 1}
 
 
 def passed_along(array, axis, by):
@@ -204,7 +204,7 @@
     return 2 * there + side
 
 
-def correlate_kernel(rows, two, aliased, scale, me_ref, *refs):
+def correlate_kernel(tile, rows, two, aliased, scale, me_ref, *refs):
     refs = list(refs)
     hankels = [refs.pop(0) for _ in range(rows)]
     first = refs.pop(0)
@@ -215,7 +215,7 @@
     out_ref = refs.pop(0)
     depth, width = first.shape
     step = pl.program_id(0)
-    each = hankels[0].shape[0] // ROWS
+    each = hankels[0].shape[0] // tile
 
     @pl.when(step == 0)
     def _():
@@ -234,7 +234,7 @@
             pltpu.sync_copy(first, held.at[pl.ds(0, depth)])
 
     def product(ref, at):
-        lagged = ref[pl.ds(pl.multiple_of(at * ROWS, ROWS), ROWS), :]
+        lagged = ref[pl.ds(pl.multiple_of(at * tile, tile), tile), :]
         return jnp.dot(lagged, held[...], preferred_element_type=jnp.float32) * scale
 
     if rows == 1:
@@ -251,12 +251,12 @@
         out_ref[...] = product(hankels[0], step - each).reshape(out_ref.shape)
 
 
-def correlate(hankels, operands, me, place, scale, out, channels, sent=False):
+def correlate(hankels, operands, me, place, scale, out, channels, tile, sent=False):
     lanes, span = hankels[0].shape
     sources = lanes // LAGS
     depth, width = operands[0].shape
-    group = ROWS // LAGS
-    each = lanes // ROWS
+    group = tile // LAGS
+    each = lanes // tile
     rows = len(hankels)
     skip = (rows - 1) * each
     resident = pl.BlockSpec(memory_space=pltpu.VMEM)
@@ -288,7 +288,7 @@
     if sent:
         out_shape, out_specs = [sent_shape], [sent_spec]
     return pl.pallas_call(
-        functools.partial(correlate_kernel, rows, len(operands) == 2, bool(aliases), scale),
+        functools.partial(correlate_kernel, tile, rows, len(operands) == 2, bool(aliases), scale),
         out_shape=out_shape,
         grid_spec=pltpu.PrefetchScalarGridSpec(
             num_scalar_prefetch=1,
@@ -417,6 +417,7 @@
     ]
     out = None
     waiting = []
+    tiles = [ROWS // 2] * (line - 1) + [ROWS]
 
     def place(slot, c, partner):
         return lambda me: (origin(slot, me) ^ partner) * channels + offsets[c]
@@ -424,7 +425,7 @@
     def add(slot, c, partner, chunk, hankels):
         nonlocal out
         out, *sent = correlate(
-            hankels, chunk, here, place(slot, c, partner), scale, out, total
+            hankels, chunk, here, place(slot, c, partner), scale, out, total, tiles[slot]
         )
         return sent
 
@@ -439,7 +440,15 @@
             (made,) = add(slot, c, 0, chunk, [own_rows, partner_rows])
         else:
             (made,) = correlate(
-                [partner_rows], chunk, here, place(slot, c, 0), scale, out, total, sent=True
+                [partner_rows],
+                chunk,
+                here,
+                place(slot, c, 0),
+                scale,
+                out,
+                total,
+                tiles[slot],
+                sent=True,
             )
             add(slot, c, 0, chunk, [own_rows])
         waiting.append((hop(made, across), here, place(slot, c, 1)))

time: 399 us -> 457 us (1.15)
  Pallas kernels: 126 us -> 153 us
  starting transfers between devices: 65.4 us -> 82.7 us
  waiting for transfers between devices: 194 us -> 209 us
    pallas_call x21 -> x26, Pallas kernels: 87 us -> 114 us  [correlate(): pl.pallas_call(functools.partial(correlate_kernel, tile, rows, len(operan...]
    ppermute x41 -> x50, waiting for transfers between devices: 185 us -> 208 us  [hop(): return lax.ppermute(array, 'src', pairs)]
    ppermute x41 -> x50, starting transfers between devices: 54.8 us -> 70.4 us  [hop(): return lax.ppermute(array, 'src', pairs)]
    ppermute x6, waiting for transfers between devices: 9.08 us -> 0.91 us  [passed_along(): return lax.ppermute(array, axis, pairs)]
    pallas_call x15 -> x19, Pallas kernels: 23.5 us -> 23.9 us  [store(): pl.pallas_call(store_kernel, out_shape=jax.ShapeDtypeStruct(out.shape, ou...]
  transfers between devices with their start and end apart: 47 -> 56, of which waited for: 18 -> 15; matrix products, arithmetic and copies ran while one was open for 1% -> 1% of each run, Pallas kernels for 29% -> 31%
where the time goes in v3:
time: 457 us; the launch traced here: 456 us
  waiting for transfers between devices  209 us (46%)
  Pallas kernels  153 us (33%)
  starting transfers between devices  82.7 us (18%)
  local copies, waits for them, and re-layouts  6.41 us (1%)
  other arithmetic  4.74 us (1%)
    ppermute x50, waiting for transfers between devices, hop(): return lax.ppermute(array, 'src', pairs)  208 us
    pallas_call x26, Pallas kernels, correlate(): pl.pallas_call(functools.partial(correlate_kernel, tile, rows, len(operan...  114 us
    ppermute x50, starting transfers between devices, hop(): return lax.ppermute(array, 'src', pairs)  70.4 us
    pallas_call x19, Pallas kernels, store(): pl.pallas_call(store_kernel, out_shape=jax.ShapeDtypeStruct(out.shape, ou...  23.9 us
    ppermute x6, starting transfers between devices, passed_along(): return lax.ppermute(array, axis, pairs)  12.3 us
  transfers between devices with their start and end apart: 56, of which 15 were waited for; matrix products, arithmetic and copies ran while one was open for 1% of the time, Pallas kernels for 31%

profile of v3, /device:TPU:0, one launch (start us, length us, event | category | flops | bytes accessed | tf_op | source)
XLA Modules:
  0.0 455.6 jit_solution(17427697436245048908)
XLA Ops:
  7.8 5.2 %normalize.3 = (bf16[1568,384]{1,0:T(8,128)(2,1)S(1)}, bf16[1568,384]{1,0:T(8,128)(2,1)}, bf16[1568,256]{1,0:T(8,128)(2,1)S(1)}, bf16[1568,128]{1,0:T(8,128)(2,1)S(1)}, bf16[1568,128]{1,0:T(8,128)(2,1)S(1)}) custom-call(bf16[1536,1280]{1,0:T(8,128)(2,1)} %strain_ref.1, s32[1,1280]{1,0:T(1,128)S(1)} %get-tuple-element.79.refs_0_, ...), custom_call_target="tpu_custom_call" | custom-call | flops 1027604480 | bytes 7864320 | tf_op jit(solution)/shard_map/normalize/pallas_call | solution.py:92
  13.0 4.9 %select.3 = (bf16[128,1536]{1,0:T(8,128)(2,1)S(1)}, bf16[128,1536]{1,0:T(8,128)(2,1)S(1)}) custom-call(s32[1]{0:T(128)} %bitcast.me_ref, s32[256,1]{1,0:T(8,128)S(1)} %copy.43.index_ref, bf16[1568,384]{1,0:T(8,128)(2,1)S(1)} %get-tuple-element.40.refs_0_.refs_2_, bf16[1568,384]{1,0:T(8,128)(2,1)} %get-tuple-element.41.refs_1_.refs_2_, ...), custom_call_target="tpu_custom_call" | custom-call | flops 1006632960 | bytes 3932160 | tf_op jit(solution)/shard_map/select/pallas_call | solution.py:145
  17.9 3.0 collective-permute-start.2
  22.5 7.2 %collective-permute-done.2 = bf16[128,1536]{1,0:T(8,128)(2,1)S(1)} collective-permute-done((bf16[128,1536]{1,0:T(8,128)(2,1)S(1)}, bf16[128,1536]{1,0:T(8,128)(2,1)S(1)}, u32[]{:S(2)}, u32[]{:S(2)}) %collective-permute-start.2) | collective-permute-done | bytes 393248 | tf_op jit(solution)/shard_map/ppermute | solution.py:343
  43.8 24.3 %collective-permute-done.7.refs_2_ = bf16[1568,128]{1,0:T(8,128)(2,1)S(1)} collective-permute-done((bf16[1568,128]{1,0:T(8,128)(2,1)S(1)}, bf16[1568,128]{1,0:T(8,128)(2,1)S(1)}, u32[]{:S(2)}, u32[]{:S(2)}) %collective-permute-start.7) | collective-permute-done | bytes 401440 | tf_op jit(solution)/shard_map/ppermute | solution.py:343
  83.6 9.6 %collective-permute-start.19 = (bf16[1568,384]{1,0:T(8,128)(2,1)}, bf16[1568,384]{1,0:T(8,128)(2,1)}, u32[]{:S(2)}, u32[]{:S(2)}) collective-permute-start(bf16[1568,384]{1,0:T(8,128)(2,1)} %get-tuple-element.41.refs_1_.refs_2_), channel_id=1, source_target_pairs={{0,2},{1,3},{2,0},{3,1},{4,6},{5,7},{6,4},{7,5},{8,10},{9,11},{10,... | collective-permute-start | bytes 3612680 | tf_op jit(solution)/shard_map/ppermute | solution.py:343
  98.4 6.3 %correlate.32 = (f32[1,32,32,10240]{3,2,1,0:T(8,128)}, bf16[32,32,384]{2,1,0:T(8,128)(2,1)S(1)}) custom-call(s32[1]{0:T(128)} %bitcast.me_ref, bf16[1024,1664]{1,0:T(8,128)(2,1)S(1)} %hankel.3.refs_0_, bf16[1024,1664]{1,0:T(8,128)(2,1)S(1)} %hankel.2.refs_0_.refs_1_, ...), custom_call_target="tpu_custom_call", output_to_operand_aliasing={{0}: (4, {})} | custom-call | flops 2617245696 | bytes 2777088 | tf_op jit(solution)/shard_map/correlate/pallas_call | solution.py:290
  105.5 7.3 %correlate.33 = (f32[1,32,32,10240]{3,2,1,0:T(8,128)}, bf16[32,32,384]{2,1,0:T(8,128)(2,1)S(1)}) custom-call(s32[1]{0:T(128)} %bitcast.me_ref, bf16[1024,1664]{1,0:T(8,128)(2,1)S(1)} %hankel.3.refs_0_, bf16[1024,1664]{1,0:T(8,128)(2,1)S(1)} %hankel.2.refs_0_.refs_1_, ...), custom_call_target="tpu_custom_call", output_to_operand_aliasing={{0}: (4, {})} | custom-call | flops 2617245696 | bytes 2777088 | tf_op jit(solution)/shard_map/correlate/pallas_call | solution.py:290
  112.8 4.3 correlate.34
  117.1 4.8 %correlate.35 = (f32[1,32,32,10240]{3,2,1,0:T(8,128)}, bf16[32,32,128]{2,1,0:T(8,128)(2,1)}) custom-call(s32[1]{0:T(128)} %bitcast.me_ref, bf16[1024,1664]{1,0:T(8,128)(2,1)S(1)} %hankel.3.refs_0_, bf16[1024,1664]{1,0:T(8,128)(2,1)S(1)} %hankel.2.refs_0_.refs_1_, ...), custom_call_target="tpu_custom_call", output_to_operand_aliasing={{0}: (4, {})} | custom-call | flops 872415232 | bytes 925696 | tf_op jit(solution)/shard_map/correlate/pallas_call | solution.py:290
  130.2 4.1 collective-permute-start.34
  139.5 6.3 %correlate.37 = (f32[1,32,32,10240]{3,2,1,0:T(8,128)}, bf16[32,32,384]{2,1,0:T(8,128)(2,1)S(1)}) custom-call(s32[1]{0:T(128)} %bitcast.me_ref, bf16[1024,1664]{1,0:T(8,128)(2,1)S(1)} %hankel.3.refs_0_, bf16[1024,1664]{1,0:T(8,128)(2,1)S(1)} %hankel.2.refs_0_.refs_1_, bf16[1568,384]{1,0:T(8,128)(2,1)S(1)} %normalize.4.refs_2_, ...), custom_call_target="tpu_custom_call", output_to_operand_aliasing={{0}: (4, {})} | custom-call | flops 2617245696 | bytes 2777088 | tf_op jit(solution)/shard_map/correlate/pallas_call | solution.py:290
  150.0 7.3 %correlate.38 = (f32[1,32,32,10240]{3,2,1,0:T(8,128)}, bf16[32,32,384]{2,1,0:T(8,128)(2,1)S(1)}) custom-call(s32[1]{0:T(128)} %bitcast.me_ref, bf16[1024,1664]{1,0:T(8,128)(2,1)S(1)} %hankel.3.refs_0_, bf16[1024,1664]{1,0:T(8,128)(2,1)S(1)} %hankel.2.refs_0_.refs_1_, ...), custom_call_target="tpu_custom_call", output_to_operand_aliasing={{0}: (4, {})} | custom-call | flops 2617245696 | bytes 2777088 | tf_op jit(solution)/shard_map/correlate/pallas_call | solution.py:290
  158.3 4.6 correlate.39
  162.8 4.8 %correlate.40 = (f32[1,32,32,10240]{3,2,1,0:T(8,128)}, bf16[32,32,128]{2,1,0:T(8,128)(2,1)}) custom-call(s32[1]{0:T(128)} %bitcast.me_ref, bf16[1024,1664]{1,0:T(8,128)(2,1)S(1)} %hankel.3.refs_0_, bf16[1024,1664]{1,0:T(8,128)(2,1)S(1)} %hankel.2.refs_0_.refs_1_, bf16[1568,128]{1,0:T(8,128)(2,1)S(1)} %copy-done.28, ...), custom_call_target="tpu_custom_call", output_to_operand_aliasing={{0}: (4, {})} | custom-call | flops 872415232 | bytes 925696 | tf_op jit(solution)/shard_map/correlate/pallas_call | solution.py:290
  167.6 41.8 %collective-permute-done.13.refs_1_ = bf16[1568,128]{1,0:T(8,128)(2,1)S(1)} collective-permute-done((bf16[1568,128]{1,0:T(8,128)(2,1)S(1)}, bf16[1568,128]{1,0:T(8,128)(2,1)S(1)}, u32[]{:S(2)}, u32[]{:S(2)}) %collective-permute-start.13) | collective-permute-done | bytes 401440 | tf_op jit(solution)/shard_map/ppermute | solution.py:343
  211.1 6.9 %collective-permute-done.9.refs_1_ = bf16[1568,128]{1,0:T(8,128)(2,1)S(1)} collective-permute-done((bf16[1568,128]{1,0:T(8,128)(2,1)S(1)}, bf16[1568,128]{1,0:T(8,128)(2,1)S(1)}, u32[]{:S(2)}, u32[]{:S(2)}) %collective-permute-start.9) | collective-permute-done | bytes 401440 | tf_op jit(solution)/shard_map/ppermute | solution.py:343
  218.5 4.8 %correlate.41 = (f32[1,32,32,10240]{3,2,1,0:T(8,128)}, bf16[32,32,128]{2,1,0:T(8,128)(2,1)}) custom-call(s32[1]{0:T(128)} %bitcast.me_ref, bf16[1024,1664]{1,0:T(8,128)(2,1)S(1)} %hankel.3.refs_0_, bf16[1024,1664]{1,0:T(8,128)(2,1)S(1)} %hankel.2.refs_0_.refs_1_, bf16[1568,128]{1,0:T(8,128)(2,1)S(1)} %copy-done.30, ...), custom_call_target="tpu_custom_call", output_to_operand_aliasing={{0}: (4, {})} | custom-call | flops 872415232 | bytes 925696 | tf_op jit(solution)/shard_map/correlate/pallas_call | solution.py:290
  229.0 3.1 collective-permute-done.46.got_ref
  234.2 13.0 %collective-permute-done.50.got_ref = bf16[32,32,256]{2,1,0:T(8,128)(2,1)S(1)} collective-permute-done((bf16[32,32,256]{2,1,0:T(8,128)(2,1)}, bf16[32,32,256]{2,1,0:T(8,128)(2,1)S(1)}, u32[]{:S(2)}, u32[]{:S(2)}) %collective-permute-start.50) | collective-permute-done | bytes 524320 | tf_op jit(solution)/shard_map/ppermute | solution.py:343
  249.3 13.3 %collective-permute-done.38.got_ref = bf16[32,32,384]{2,1,0:T(8,128)(2,1)S(1)} collective-permute-done((bf16[32,32,384]{2,1,0:T(8,128)(2,1)}, bf16[32,32,384]{2,1,0:T(8,128)(2,1)S(1)}, u32[]{:S(2)}, u32[]{:S(2)}) %collective-permute-start.38) | collective-permute-done | bytes 786464 | tf_op jit(solution)/shard_map/ppermute | solution.py:343
  272.4 6.3 %correlate.42 = (f32[1,32,32,10240]{3,2,1,0:T(8,128)}, bf16[32,32,384]{2,1,0:T(8,128)(2,1)S(1)}) custom-call(s32[1]{0:T(128)} %bitcast.me_ref, bf16[1024,1664]{1,0:T(8,128)(2,1)S(1)} %hankel.3.refs_0_, bf16[1024,1664]{1,0:T(8,128)(2,1)S(1)} %hankel.2.refs_0_.refs_1_, ...), custom_call_target="tpu_custom_call", output_to_operand_aliasing={{0}: (5, {})} | custom-call | flops 2617245696 | bytes 2777088 | tf_op jit(solution)/shard_map/correlate/pallas_call | solution.py:290
  288.4 7.3 %correlate.43 = (f32[1,32,32,10240]{3,2,1,0:T(8,128)}, bf16[32,32,384]{2,1,0:T(8,128)(2,1)S(1)}) custom-call(s32[1]{0:T(128)} %bitcast.me_ref, bf16[1024,1664]{1,0:T(8,128)(2,1)S(1)} %hankel.3.refs_0_, bf16[1024,1664]{1,0:T(8,128)(2,1)S(1)} %hankel.2.refs_0_.refs_1_, ...), custom_call_target="tpu_custom_call", output_to_operand_aliasing={{0}: (5, {})} | custom-call | flops 2617245696 | bytes 2777088 | tf_op jit(solution)/shard_map/correlate/pallas_call | solution.py:290
  296.5 59.2 %collective-permute-done.45.refs_2_ = bf16[1568,256]{1,0:T(8,128)(2,1)} collective-permute-done((bf16[1568,256]{1,0:T(8,128)(2,1)}, bf16[1568,256]{1,0:T(8,128)(2,1)}, u32[]{:S(2)}, u32[]{:S(2)}) %collective-permute-start.45) | collective-permute-done | bytes 802848 | tf_op jit(solution)/shard_map/ppermute | solution.py:343
  356.2 5.6 %correlate.44 = (f32[1,32,32,10240]{3,2,1,0:T(8,128)}, bf16[32,32,256]{2,1,0:T(8,128)(2,1)S(1)}) custom-call(s32[1]{0:T(128)} %bitcast.me_ref, bf16[1024,1664]{1,0:T(8,128)(2,1)S(1)} %hankel.3.refs_0_, bf16[1024,1664]{1,0:T(8,128)(2,1)S(1)} %hankel.2.refs_0_.refs_1_, ...), custom_call_target="tpu_custom_call", output_to_operand_aliasing={{0}: (5, {})} | custom-call | flops 1744830464 | bytes 1851392 | tf_op jit(solution)/shard_map/correlate/pallas_call | solution.py:290
  363.4 4.2 correlate.30
  368.1 4.2 correlate.29
  375.4 4.4 correlate.45
  380.4 4.4 correlate.46
  397.9 28.8 %collective-permute-done.53.got_ref = bf16[32,32,128]{2,1,0:T(8,128)(2,1)S(1)} collective-permute-done((bf16[32,32,128]{2,1,0:T(8,128)(2,1)S(1)}, bf16[32,32,128]{2,1,0:T(8,128)(2,1)S(1)}, u32[]{:S(2)}, u32[]{:S(2)}) %collective-permute-start.53) | collective-permute-done | bytes 262176 | tf_op jit(solution)/shard_map/ppermute | solution.py:343
  428.0 4.3 correlate.47.kept_ref
  436.9 4.4 correlate.48.refs_3_
  (225 shorter events, 134.9 us)
Async XLA Ops:
  36.3 39.7 %collective-permute-start.37 = (bf16[1568,256]{1,0:T(8,128)(2,1)S(1)}, bf16[1568,256]{1,0:T(8,128)(2,1)S(1)}, u32[]{:S(2)}, u32[]{:S(2)}) collective-permute-start(bf16[1568,256]{1,0:T(8,128)(2,1)S(1)} %get-tuple-element.42.refs_2_.refs_1_), channel_id=1, source_target_pairs={{0,1},{1,0},{2,3},{3,2},{4,5},{5,4},{6,7},{7,6},{8,9},{9,8},{10,11... | collective-permute-start | bytes 2408456 | tf_op jit(solution)/shard_map/ppermute | solution.py:343
  37.9 40.9 %collective-permute-start.15 = (bf16[1568,256]{1,0:T(8,128)(2,1)S(1)}, bf16[1568,256]{1,0:T(8,128)(2,1)S(1)}, u32[]{:S(2)}, u32[]{:S(2)}) collective-permute-start(bf16[1568,256]{1,0:T(8,128)(2,1)S(1)} %get-tuple-element.42.refs_2_.refs_1_), channel_id=1, source_target_pairs={{0,2},{1,3},{2,0},{3,1},{4,6},{5,7},{6,4},{7,5},{8,10},{9,11},{10,... | collective-permute-start | bytes 2408456 | tf_op jit(solution)/shard_map/ppermute | solution.py:343
  38.5 29.6 %collective-permute-start.7 = (bf16[1568,128]{1,0:T(8,128)(2,1)S(1)}, bf16[1568,128]{1,0:T(8,128)(2,1)S(1)}, u32[]{:S(2)}, u32[]{:S(2)}) collective-permute-start(bf16[1568,128]{1,0:T(8,128)(2,1)S(1)} %get-tuple-element.44.refs_4_.refs_2_), channel_id=1, source_target_pairs={{0,2},{1,3},{2,0},{3,1},{4,6},{5,7},{6,4},{7,5},{8,10},{9,11},{10,... | collective-permute-start | bytes 1204232 | tf_op jit(solution)/shard_map/ppermute | solution.py:343
  42.4 28.1 %collective-permute-start.31 = (bf16[1568,128]{1,0:T(8,128)(2,1)S(1)}, bf16[1568,128]{1,0:T(8,128)(2,1)S(1)}, u32[]{:S(2)}, u32[]{:S(2)}) collective-permute-start(bf16[1568,128]{1,0:T(8,128)(2,1)S(1)} %get-tuple-element.43.refs_3_.refs_2_), channel_id=1, source_target_pairs={{2,4},{3,5},{4,2},{5,3},{10,12},{11,13},{12,10},{13,11},{18,20},{1... | collective-permute-start | bytes 1204232 | tf_op jit(solution)/shard_map/ppermute | solution.py:343
  43.1 29.0 %collective-permute-start.29 = (bf16[1568,128]{1,0:T(8,128)(2,1)S(1)}, bf16[1568,128]{1,0:T(8,128)(2,1)S(1)}, u32[]{:S(2)}, u32[]{:S(2)}) collective-permute-start(bf16[1568,128]{1,0:T(8,128)(2,1)S(1)} %get-tuple-element.44.refs_4_.refs_2_), channel_id=1, source_target_pairs={{2,4},{3,5},{4,2},{5,3},{10,12},{11,13},{12,10},{13,11},{18,20},{1... | collective-permute-start | bytes 1204232 | tf_op jit(solution)/shard_map/ppermute | solution.py:343
  76.0 46.4 %collective-permute-start.23 = (bf16[1536,384]{1,0:T(8,128)(2,1)S(1)}, bf16[1536,384]{1,0:T(8,128)(2,1)S(1)}, u32[]{:S(2)}, u32[]{:S(2)}) collective-permute-start(bf16[1536,384]{1,0:T(8,128)(2,1)S(1)} %slice_select_fusion), channel_id=1, source_target_pairs={{0,2},{1,3},{2,0},{3,1},{4,6},{5,7},{6,4},{7,5},{8,10},{9,11},{10,... | collective-permute-start | bytes 3538952 | tf_op jit(solution)/shard_map/ppermute | solution.py:343
  78.8 45.2 %collective-permute-start.33 = (bf16[1536,384]{1,0:T(8,128)(2,1)S(1)}, bf16[1536,384]{1,0:T(8,128)(2,1)S(1)}, u32[]{:S(2)}, u32[]{:S(2)}) collective-permute-start(bf16[1536,384]{1,0:T(8,128)(2,1)S(1)} %slice_select_fusion), channel_id=1, source_target_pairs={{2,4},{3,5},{4,2},{5,3},{10,12},{11,13},{12,10},{13,11},{18,20},{1... | collective-permute-start | bytes 3538952 | tf_op jit(solution)/shard_map/ppermute | solution.py:343
  83.6 63.8 %collective-permute-start.19 = (bf16[1568,384]{1,0:T(8,128)(2,1)}, bf16[1568,384]{1,0:T(8,128)(2,1)}, u32[]{:S(2)}, u32[]{:S(2)}) collective-permute-start(bf16[1568,384]{1,0:T(8,128)(2,1)} %get-tuple-element.41.refs_1_.refs_2_), channel_id=1, source_target_pairs={{0,2},{1,3},{2,0},{3,1},{4,6},{5,7},{6,4},{7,5},{8,10},{9,11},{10,... | collective-permute-start | bytes 3612680 | tf_op jit(solution)/shard_map/ppermute | solution.py:343
  94.0 54.7 %collective-permute-start.47 = (bf16[1568,384]{1,0:T(8,128)(2,1)}, bf16[1568,384]{1,0:T(8,128)(2,1)}, u32[]{:S(2)}, u32[]{:S(2)}) collective-permute-start(bf16[1568,384]{1,0:T(8,128)(2,1)} %get-tuple-element.41.refs_1_.refs_2_), channel_id=1, source_target_pairs={{2,4},{3,5},{4,2},{5,3},{10,12},{11,13},{12,10},{13,11},{18,20},{1... | collective-permute-start | bytes 3612680 | tf_op jit(solution)/shard_map/ppermute | solution.py:343
  136.1 87.2 %collective-permute-start.42 = (bf16[32,32,384]{2,1,0:T(8,128)(2,1)}, bf16[32,32,384]{2,1,0:T(8,128)(2,1)S(1)}, u32[]{:S(2)}, u32[]{:S(2)}) collective-permute-start(bf16[32,32,384]{2,1,0:T(8,128)(2,1)} %copy-done.35), channel_id=1, source_target_pairs={{0,1},{1,0},{2,3},{3,2},{4,5},{5,4},{6,7},{7,6},{8,9},{9,8},{10,11... | collective-permute-start | bytes 2359304 | tf_op jit(solution)/shard_map/ppermute | solution.py:343
  136.9 88.0 %collective-permute-start.41 = (bf16[32,32,384]{2,1,0:T(8,128)(2,1)}, bf16[32,32,384]{2,1,0:T(8,128)(2,1)S(1)}, u32[]{:S(2)}, u32[]{:S(2)}) collective-permute-start(bf16[32,32,384]{2,1,0:T(8,128)(2,1)} %copy-done.36), channel_id=1, source_target_pairs={{0,1},{1,0},{2,3},{3,2},{4,5},{5,4},{6,7},{7,6},{8,9},{9,8},{10,11... | collective-permute-start | bytes 2359304 | tf_op jit(solution)/shard_map/ppermute | solution.py:343
  146.6 86.5 %collective-permute-start.16 = (bf16[1568,256]{1,0:T(8,128)(2,1)S(1)}, bf16[1568,256]{1,0:T(8,128)(2,1)S(1)}, u32[]{:S(2)}, u32[]{:S(2)}) collective-permute-start(bf16[1568,256]{1,0:T(8,128)(2,1)S(1)} %collective-permute-done.15.refs_2_), channel_id=1, source_target_pairs={{2,4},{3,5},{4,2},{5,3},{10,12},{11,13},{12,10},{13,11},{18,20},{1... | collective-permute-start | bytes 2408456 | tf_op jit(solution)/shard_map/ppermute | solution.py:343
  147.4 62.0 %collective-permute-start.13 = (bf16[1568,128]{1,0:T(8,128)(2,1)S(1)}, bf16[1568,128]{1,0:T(8,128)(2,1)S(1)}, u32[]{:S(2)}, u32[]{:S(2)}) collective-permute-start(bf16[1568,128]{1,0:T(8,128)(2,1)S(1)} %collective-permute-done.12.refs_2_), channel_id=1, source_target_pairs={{2,0},{3,1},{4,6},{5,7},{10,8},{11,9},{12,14},{13,15},{18,16},{19,... | collective-permute-start | bytes 1204232 | tf_op jit(solution)/shard_map/ppermute | solution.py:343
  148.7 69.3 %collective-permute-start.9 = (bf16[1568,128]{1,0:T(8,128)(2,1)S(1)}, bf16[1568,128]{1,0:T(8,128)(2,1)S(1)}, u32[]{:S(2)}, u32[]{:S(2)}) collective-permute-start(bf16[1568,128]{1,0:T(8,128)(2,1)S(1)} %collective-permute-done.8.refs_2_), channel_id=1, source_target_pairs={{2,0},{3,1},{4,6},{5,7},{10,8},{11,9},{12,14},{13,15},{18,16},{19,... | collective-permute-start | bytes 1204232 | tf_op jit(solution)/shard_map/ppermute | solution.py:343
  209.4 53.6 %collective-permute-start.26 = (bf16[1568,384]{1,0:T(8,128)(2,1)S(1)}, bf16[1568,384]{1,0:T(8,128)(2,1)}, u32[]{:S(2)}, u32[]{:S(2)}) collective-permute-start(bf16[1568,384]{1,0:T(8,128)(2,1)S(1)} %normalize.4.refs_2_), channel_id=1, source_target_pairs={{2,4},{3,5},{4,2},{5,3},{10,12},{11,13},{12,10},{13,11},{18,20},{1... | collective-permute-start | bytes 3612680 | tf_op jit(solution)/shard_map/ppermute | solution.py:343
  224.9 39.4 %collective-permute-start.20 = (bf16[1568,384]{1,0:T(8,128)(2,1)}, bf16[1568,384]{1,0:T(8,128)(2,1)}, u32[]{:S(2)}, u32[]{:S(2)}) collective-permute-start(bf16[1568,384]{1,0:T(8,128)(2,1)} %collective-permute-done.19.refs_2_), channel_id=1, source_target_pairs={{2,4},{3,5},{4,2},{5,3},{10,12},{11,13},{12,10},{13,11},{18,20},{1... | collective-permute-start | bytes 3612680 | tf_op jit(solution)/shard_map/ppermute | solution.py:343
  227.7 37.9 %collective-permute-start.36 = (bf16[1568,384]{1,0:T(8,128)(2,1)S(1)}, bf16[1568,384]{1,0:T(8,128)(2,1)S(1)}, u32[]{:S(2)}, u32[]{:S(2)}) collective-permute-start(bf16[1568,384]{1,0:T(8,128)(2,1)S(1)} %normalize.5.refs_3_), channel_id=1, source_target_pairs={{2,0},{3,1},{4,6},{5,7},{10,8},{11,9},{12,14},{13,15},{18,16},{19,... | collective-permute-start | bytes 3612680 | tf_op jit(solution)/shard_map/ppermute | solution.py:343
  233.2 29.4 %collective-permute-start.38 = (bf16[32,32,384]{2,1,0:T(8,128)(2,1)}, bf16[32,32,384]{2,1,0:T(8,128)(2,1)S(1)}, u32[]{:S(2)}, u32[]{:S(2)}) collective-permute-start(bf16[32,32,384]{2,1,0:T(8,128)(2,1)} %copy-done.38), channel_id=1, source_target_pairs={{0,1},{1,0},{2,3},{3,2},{4,5},{5,4},{6,7},{7,6},{8,9},{9,8},{10,11... | collective-permute-start | bytes 2359304 | tf_op jit(solution)/shard_map/ppermute | solution.py:343
  248.0 38.9 %collective-permute-start.48 = (bf16[1568,384]{1,0:T(8,128)(2,1)}, bf16[1568,384]{1,0:T(8,128)(2,1)}, u32[]{:S(2)}, u32[]{:S(2)}) collective-permute-start(bf16[1568,384]{1,0:T(8,128)(2,1)} %collective-permute-done.47.refs_3_), channel_id=1, source_target_pairs={{2,0},{3,1},{4,6},{5,7},{10,8},{11,9},{12,14},{13,15},{18,16},{19,... | collective-permute-start | bytes 3612680 | tf_op jit(solution)/shard_map/ppermute | solution.py:343
  263.0 98.8 %collective-permute-start.27 = (bf16[1568,384]{1,0:T(8,128)(2,1)}, bf16[1568,384]{1,0:T(8,128)(2,1)}, u32[]{:S(2)}, u32[]{:S(2)}) collective-permute-start(bf16[1568,384]{1,0:T(8,128)(2,1)} %collective-permute-done.26.refs_2_), channel_id=1, source_target_pairs={{2,0},{3,1},{4,6},{5,7},{10,8},{11,9},{12,14},{13,15},{18,16},{19,... | collective-permute-start | bytes 3612680 | tf_op jit(solution)/shard_map/ppermute | solution.py:343
  264.3 103.3 %collective-permute-start.21 = (bf16[1568,384]{1,0:T(8,128)(2,1)}, bf16[1568,384]{1,0:T(8,128)(2,1)}, u32[]{:S(2)}, u32[]{:S(2)}) collective-permute-start(bf16[1568,384]{1,0:T(8,128)(2,1)} %collective-permute-done.20.refs_2_), channel_id=1, source_target_pairs={{2,0},{3,1},{4,6},{5,7},{10,8},{11,9},{12,14},{13,15},{18,16},{19,... | collective-permute-start | bytes 3612680 | tf_op jit(solution)/shard_map/ppermute | solution.py:343
  265.6 90.1 %collective-permute-start.45 = (bf16[1568,256]{1,0:T(8,128)(2,1)}, bf16[1568,256]{1,0:T(8,128)(2,1)}, u32[]{:S(2)}, u32[]{:S(2)}) collective-permute-start(bf16[1568,256]{1,0:T(8,128)(2,1)} %collective-permute-done.44.refs_3_), channel_id=1, source_target_pairs={{2,0},{3,1},{4,6},{5,7},{10,8},{11,9},{12,14},{13,15},{18,16},{19,... | collective-permute-start | bytes 2408456 | tf_op jit(solution)/shard_map/ppermute | solution.py:343
  281.0 91.3 %collective-permute-start.43 = (bf16[32,32,384]{2,1,0:T(8,128)(2,1)S(1)}, bf16[32,32,384]{2,1,0:T(8,128)(2,1)S(1)}, u32[]{:S(2)}, u32[]{:S(2)}) collective-permute-start(bf16[32,32,384]{2,1,0:T(8,128)(2,1)S(1)} %get-tuple-element.61), channel_id=1, source_target_pairs={{0,1},{1,0},{2,3},{3,2},{4,5},{5,4},{6,7},{7,6},{8,9},{9,8},{10,11... | collective-permute-start | bytes 2359304 | tf_op jit(solution)/shard_map/ppermute | solution.py:343
  286.9 92.9 %collective-permute-start.17 = (bf16[1568,256]{1,0:T(8,128)(2,1)S(1)}, bf16[1568,256]{1,0:T(8,128)(2,1)S(1)}, u32[]{:S(2)}, u32[]{:S(2)}) collective-permute-start(bf16[1568,256]{1,0:T(8,128)(2,1)S(1)} %copy-done.1), channel_id=1, source_target_pairs={{2,0},{3,1},{4,6},{5,7},{10,8},{11,9},{12,14},{13,15},{18,16},{19,... | collective-permute-start | bytes 2408456 | tf_op jit(solution)/shard_map/ppermute | solution.py:343
  355.7 34.3 %collective-permute-start.55 = (bf16[32,32,384]{2,1,0:T(8,128)(2,1)S(1)}, bf16[32,32,384]{2,1,0:T(8,128)(2,1)S(1)}, u32[]{:S(2)}, u32[]{:S(2)}) collective-permute-start(bf16[32,32,384]{2,1,0:T(8,128)(2,1)S(1)} %get-tuple-element.73), channel_id=1, source_target_pairs={{0,1},{1,0},{2,3},{3,2},{4,5},{5,4},{6,7},{7,6},{8,9},{9,8},{10,11... | collective-permute-start | bytes 2359304 | tf_op jit(solution)/shard_map/ppermute | solution.py:343
  361.9 25.5 %collective-permute-start.54 = (bf16[32,32,256]{2,1,0:T(8,128)(2,1)S(1)}, bf16[32,32,256]{2,1,0:T(8,128)(2,1)S(1)}, u32[]{:S(2)}, u32[]{:S(2)}) collective-permute-start(bf16[32,32,256]{2,1,0:T(8,128)(2,1)S(1)} %get-tuple-element.72), channel_id=1, source_target_pairs={{0,1},{1,0},{2,3},{3,2},{4,5},{5,4},{6,7},{7,6},{8,9},{9,8},{10,11... | collective-permute-start | bytes 1572872 | tf_op jit(solution)/shard_map/ppermute | solution.py:343
  367.6 67.1 %collective-permute-start.28 = (bf16[32,32,384]{2,1,0:T(8,128)(2,1)}, bf16[32,32,384]{2,1,0:T(8,128)(2,1)}, u32[]{:S(2)}, u32[]{:S(2)}) collective-permute-start(bf16[32,32,384]{2,1,0:T(8,128)(2,1)} %correlate.30), channel_id=1, source_target_pairs={{0,1},{1,0},{2,3},{3,2},{4,5},{5,4},{6,7},{7,6},{8,9},{9,8},{10,11... | collective-permute-start | bytes 2359304 | tf_op jit(solution)/shard_map/ppermute | solution.py:343
  372.3 73.4 %collective-permute-start.22 = (bf16[32,32,384]{2,1,0:T(8,128)(2,1)}, bf16[32,32,384]{2,1,0:T(8,128)(2,1)}, u32[]{:S(2)}, u32[]{:S(2)}) collective-permute-start(bf16[32,32,384]{2,1,0:T(8,128)(2,1)} %correlate.29), channel_id=1, source_target_pairs={{0,1},{1,0},{2,3},{3,2},{4,5},{5,4},{6,7},{7,6},{8,9},{9,8},{10,11... | collective-permute-start | bytes 2359304 | tf_op jit(solution)/shard_map/ppermute | solution.py:343
  379.8 46.9 %collective-permute-start.53 = (bf16[32,32,128]{2,1,0:T(8,128)(2,1)S(1)}, bf16[32,32,128]{2,1,0:T(8,128)(2,1)S(1)}, u32[]{:S(2)}, u32[]{:S(2)}) collective-permute-start(bf16[32,32,128]{2,1,0:T(8,128)(2,1)S(1)} %get-tuple-element.71), channel_id=1, source_target_pairs={{0,1},{1,0},{2,3},{3,2},{4,5},{5,4},{6,7},{7,6},{8,9},{9,8},{10,11... | collective-permute-start | bytes 786440 | tf_op jit(solution)/shard_map/ppermute | solution.py:343
  387.4 45.0 %collective-permute-start.52 = (bf16[32,32,128]{2,1,0:T(8,128)(2,1)S(1)}, bf16[32,32,128]{2,1,0:T(8,128)(2,1)S(1)}, u32[]{:S(2)}, u32[]{:S(2)}) collective-permute-start(bf16[32,32,128]{2,1,0:T(8,128)(2,1)S(1)} %get-tuple-element.70), channel_id=1, source_target_pairs={{0,1},{1,0},{2,3},{3,2},{4,5},{5,4},{6,7},{7,6},{8,9},{9,8},{10,11... | collective-permute-start | bytes 786440 | tf_op jit(solution)/shard_map/ppermute | solution.py:343
  390.0 60.2 %collective-permute-start.18 = (bf16[32,32,256]{2,1,0:T(8,128)(2,1)}, bf16[32,32,256]{2,1,0:T(8,128)(2,1)}, u32[]{:S(2)}, u32[]{:S(2)}) collective-permute-start(bf16[32,32,256]{2,1,0:T(8,128)(2,1)} %correlate.28), channel_id=1, source_target_pairs={{0,1},{1,0},{2,3},{3,2},{4,5},{5,4},{6,7},{7,6},{8,9},{9,8},{10,11... | collective-permute-start | bytes 1572872 | tf_op jit(solution)/shard_map/ppermute | solution.py:343
  426.7 25.4 %collective-permute-start.14 = (bf16[32,32,128]{2,1,0:T(8,128)(2,1)}, bf16[32,32,128]{2,1,0:T(8,128)(2,1)}, u32[]{:S(2)}, u32[]{:S(2)}) collective-permute-start(bf16[32,32,128]{2,1,0:T(8,128)(2,1)} %correlate.27), channel_id=1, source_target_pairs={{0,1},{1,0},{2,3},{3,2},{4,5},{5,4},{6,7},{7,6},{8,9},{9,8},{10,11... | collective-permute-start | bytes 786440 | tf_op jit(solution)/shard_map/ppermute | solution.py:343
  (64 other events, 883.3 us)

commit v4 on v2

--- a/solution.py
+++ b/solution.py
@@ -107,6 +107,40 @@
         ),
         name="normalize",
     )(strain, *masks, lead, trail)
+
+
+def mask_kernel(strain_ref, mask_ref, out_ref, held, alive, arrived):
+    columns = pl.ds(0, out_ref.shape[1])
+    copies = [
+        pltpu.make_async_copy(strain_ref.at[:, columns], held, arrived.at[0]),
+        pltpu.make_async_copy(mask_ref.at[:, columns], alive, arrived.at[1]),
+    ]
+    for copy in copies:
+        copy.start()
+    for copy in copies:
+        copy.wait()
+    keep = jnp.broadcast_to(alive[...] > 0, held.shape)
+    out_ref[...] = jnp.where(keep, held[...].astype(jnp.float32), 0.0).astype(jnp.bfloat16)
+
+
+def mask_first(strain, mask, width):
+    samples = strain.shape[0]
+    return pl.pallas_call(
+        mask_kernel,
+        out_shape=jax.ShapeDtypeStruct((samples, width), jnp.bfloat16),
+        in_specs=[pl.BlockSpec(memory_space=pltpu.HBM)] * 2,
+        out_specs=pl.BlockSpec(memory_space=pltpu.VMEM),
+        scratch_shapes=[
+            pltpu.VMEM((samples, width), jnp.bfloat16),
+            pltpu.VMEM((1, width), jnp.int32),
+            pltpu.SemaphoreType.DMA((2,)),
+        ],
+        compiler_params=pltpu.CompilerParams(vmem_limit_bytes=NORMALIZE_BYTES),
+        cost_estimate=pl.CostEstimate(
+            flops=samples * width, bytes_accessed=4 * samples * width, transcendentals=0
+        ),
+        name="mask",
+    )(strain, mask)
 
 
 def select_kernel(own, me_ref, index_ref, *refs):
@@ -370,9 +404,7 @@
         lead = passed_along(rows(samples - HALF, samples), "win", 1)
         return lead, trail
 
-    raw = jnp.where(
-        dead_mask[:, : WIDTHS[0]] > 0, strain[:, : WIDTHS[0]], jnp.zeros((), strain.dtype)
-    )
+    raw = mask_first(strain, dead_mask, WIDTHS[0])
     raw_out = hop(raw, outer)
     raw_in = hop(raw, inner)
     lead, trail = around(lambda a, b: masked(strain[a:b]))

time: 399 us -> 400 us (level); the launches traced: 398 us -> 394 us
    unnamed x48 -> x54, local copies, waits for them, and re-layouts: 5.96 us -> 8.64 us
  transfers between devices with their start and end apart: 47 -> 47, of which waited for: 18 -> 18; matrix products, arithmetic and copies ran while one was open for 1% -> 0% of each run, Pallas kernels for 29% -> 29%
where the time goes in v4:
time: 400 us; the launch traced here: 394 us
  waiting for transfers between devices  194 us (48%)
  Pallas kernels  123 us (31%)
  starting transfers between devices  64.3 us (16%)
  local copies, waits for them, and re-layouts  9.47 us (2%)
    ppermute x41, waiting for transfers between devices, hop(): return lax.ppermute(array, 'src', pairs)  186 us
    pallas_call x21, Pallas kernels, correlate(): pl.pallas_call(functools.partial(correlate_kernel, rows, len(operands) ==...  84.6 us
    ppermute x41, starting transfers between devices, hop(): return lax.ppermute(array, 'src', pairs)  52.4 us
    pallas_call x15, Pallas kernels, store(): pl.pallas_call(store_kernel, out_shape=jax.ShapeDtypeStruct(out.shape, ou...  23.6 us
    ppermute x6, starting transfers between devices, passed_along(): return lax.ppermute(array, axis, pairs)  11.9 us
    unnamed x54, local copies, waits for them, and re-layouts  8.64 us
    pallas_call x3, Pallas kernels, normalize_chunks(): pl.pallas_call(functools.partial(normalize_kernel, widths, len(masks)), o...  8.19 us
  transfers between devices with their start and end apart: 47, of which 18 were waited for; matrix products, arithmetic and copies ran while one was open for 0% of the time, Pallas kernels for 29%

profile of v4, /device:TPU:0, one launch (start us, length us, event | category | flops | bytes accessed | tf_op | source)
XLA Modules:
  0.0 394.0 jit_solution(4758571516895111098)
XLA Ops:
  3.9 3.0 collective-permute-start
  7.8 5.0 %normalize.3 = (bf16[1568,384]{1,0:T(8,128)(2,1)S(1)}, bf16[1568,512]{1,0:T(8,128)(2,1)}, bf16[1568,256]{1,0:T(8,128)(2,1)S(1)}, bf16[1568,128]{1,0:T(8,128)(2,1)S(1)}) custom-call(bf16[1536,1280]{1,0:T(8,128)(2,1)} %strain_ref.3, s32[1,1280]{1,0:T(1,128)S(1)} %get-tuple-element.65.refs_0_, bf16[32,1280]{1,0:T(8,128)(2,1)S(1)} %collective-permute-done.refs_1_, ...), custom_call_target="tpu_custom_call" | custom-call | flops 1027604480 | bytes 7864320 | tf_op jit(solution)/shard_map/normalize/pallas_call | solution.py:92
  16.9 3.0 collective-permute-start.2
  20.0 8.8 %collective-permute-done.2 = bf16[128,1536]{1,0:T(8,128)(2,1)S(1)} collective-permute-done((bf16[128,1536]{1,0:T(8,128)(2,1)S(1)}, bf16[128,1536]{1,0:T(8,128)(2,1)S(1)}, u32[]{:S(2)}, u32[]{:S(2)}) %collective-permute-start.2) | collective-permute-done | bytes 393248 | tf_op jit(solution)/shard_map/ppermute | solution.py:377
  44.3 22.7 %collective-permute-done.7.refs_2_ = bf16[1568,128]{1,0:T(8,128)(2,1)S(1)} collective-permute-done((bf16[1568,128]{1,0:T(8,128)(2,1)S(1)}, bf16[1568,128]{1,0:T(8,128)(2,1)S(1)}, u32[]{:S(2)}, u32[]{:S(2)}) %collective-permute-start.7) | collective-permute-done | bytes 401440 | tf_op jit(solution)/shard_map/ppermute | solution.py:377
  82.4 35.1 %collective-permute-done.26.refs_2_ = bf16[1568,128]{1,0:T(8,128)(2,1)S(1)} collective-permute-done((bf16[1568,128]{1,0:T(8,128)(2,1)}, bf16[1568,128]{1,0:T(8,128)(2,1)S(1)}, u32[]{:S(2)}, u32[]{:S(2)}) %collective-permute-start.26) | collective-permute-done | bytes 401440 | tf_op jit(solution)/shard_map/ppermute | solution.py:377
  119.0 6.0 %correlate.26 = (f32[1,32,32,10240]{3,2,1,0:T(8,128)}, bf16[32,32,512]{2,1,0:T(8,128)(2,1)}) custom-call(s32[1]{0:T(128)} %bitcast.me_ref, bf16[1024,1664]{1,0:T(8,128)(2,1)S(1)} %hankel.3.refs_0_, bf16[1024,1664]{1,0:T(8,128)(2,1)S(1)} %hankel.2.refs_0_.refs_1_, bf16[1568,512]{1,0:T(8,128)(2,1)S(1)} %copy-done.1, ...), custom_call_target="tpu_custom_call", output_to_operand_aliasing={{0}: (4, {})} | custom-call | flops 3489660928 | bytes 3702784 | tf_op jit(solution)/shard_map/correlate/pallas_call | solution.py:324
  124.9 5.8 %correlate.27 = (f32[1,32,32,10240]{3,2,1,0:T(8,128)}, bf16[32,32,384]{2,1,0:T(8,128)(2,1)}) custom-call(s32[1]{0:T(128)} %bitcast.me_ref, bf16[1024,1664]{1,0:T(8,128)(2,1)S(1)} %hankel.3.refs_0_, bf16[1024,1664]{1,0:T(8,128)(2,1)S(1)} %hankel.2.refs_0_.refs_1_, ...), custom_call_target="tpu_custom_call", output_to_operand_aliasing={{0}: (4, {})} | custom-call | flops 2617245696 | bytes 2777088 | tf_op jit(solution)/shard_map/correlate/pallas_call | solution.py:324
  130.7 3.5 correlate.28
  134.9 6.3 %collective-permute-done.31.got_ref = bf16[32,32,128]{2,1,0:T(8,128)(2,1)S(1)} collective-permute-done((bf16[32,32,128]{2,1,0:T(8,128)(2,1)S(1)}, bf16[32,32,128]{2,1,0:T(8,128)(2,1)S(1)}, u32[]{:S(2)}, u32[]{:S(2)}) %collective-permute-start.31) | collective-permute-done | bytes 262176 | tf_op jit(solution)/shard_map/ppermute | solution.py:377
  148.5 3.7 collective-permute-start.38
  159.5 4.5 %collective-permute-done.39.refs_1_ = bf16[64,384]{1,0:T(8,128)(2,1)S(1)} collective-permute-done((bf16[64,384]{1,0:T(8,128)(2,1)S(1)}, bf16[64,384]{1,0:T(8,128)(2,1)S(1)}, u32[]{:S(2)}, u32[]{:S(2)}) %collective-permute-start.39) | collective-permute-done | bytes 49184 | tf_op jit(solution)/shard_map/ppermute | solution.py:37
  171.4 5.6 %correlate.30 = (f32[1,32,32,10240]{3,2,1,0:T(8,128)}, bf16[32,32,384]{2,1,0:T(8,128)(2,1)S(1)}) custom-call(s32[1]{0:T(128)} %bitcast.me_ref, bf16[1024,1664]{1,0:T(8,128)(2,1)S(1)} %hankel.3.refs_0_, bf16[1024,1664]{1,0:T(8,128)(2,1)S(1)} %hankel.2.refs_0_.refs_1_, bf16[1568,384]{1,0:T(8,128)(2,1)S(1)} %normalize.4.refs_2_, ...), custom_call_target="tpu_custom_call", output_to_operand_aliasing={{0}: (4, {})} | custom-call | flops 2617245696 | bytes 2777088 | tf_op jit(solution)/shard_map/correlate/pallas_call | solution.py:324
  179.0 7.3 %correlate.31 = (f32[1,32,32,10240]{3,2,1,0:T(8,128)}, bf16[32,32,512]{2,1,0:T(8,128)(2,1)}) custom-call(s32[1]{0:T(128)} %bitcast.me_ref, bf16[1024,1664]{1,0:T(8,128)(2,1)S(1)} %hankel.3.refs_0_, bf16[1024,1664]{1,0:T(8,128)(2,1)S(1)} %hankel.2.refs_0_.refs_1_, bf16[1568,512]{1,0:T(8,128)(2,1)} %collective-permute-done.21.refs_2_, ...), custom_call_target="tpu_custom_call", output_to_operand_aliasing={{0}: (4, {})} | custom-call | flops 3489660928 | bytes 3702784 | tf_op jit(solution)/shard_map/correlate/pallas_call | solution.py:324
  187.0 3.8 correlate.32
  192.2 3.5 correlate.33
  195.6 9.7 %collective-permute-done.30.got_ref = bf16[32,32,384]{2,1,0:T(8,128)(2,1)S(1)} collective-permute-done((bf16[32,32,384]{2,1,0:T(8,128)(2,1)S(1)}, bf16[32,32,384]{2,1,0:T(8,128)(2,1)S(1)}, u32[]{:S(2)}, u32[]{:S(2)}) %collective-permute-start.30) | collective-permute-done | bytes 786464 | tf_op jit(solution)/shard_map/ppermute | solution.py:377
  208.6 13.6 %collective-permute-done.41.got_ref = bf16[32,32,128]{2,1,0:T(8,128)(2,1)S(1)} collective-permute-done((bf16[32,32,128]{2,1,0:T(8,128)(2,1)S(1)}, bf16[32,32,128]{2,1,0:T(8,128)(2,1)S(1)}, u32[]{:S(2)}, u32[]{:S(2)}) %collective-permute-start.41) | collective-permute-done | bytes 262176 | tf_op jit(solution)/shard_map/ppermute | solution.py:377
  236.5 7.0 %correlate.34 = (f32[1,32,32,10240]{3,2,1,0:T(8,128)}, bf16[32,32,512]{2,1,0:T(8,128)(2,1)S(1)}) custom-call(s32[1]{0:T(128)} %bitcast.me_ref, bf16[1024,1664]{1,0:T(8,128)(2,1)S(1)} %hankel.3.refs_0_, bf16[1024,1664]{1,0:T(8,128)(2,1)S(1)} %hankel.2.refs_0_.refs_1_, ...), custom_call_target="tpu_custom_call", output_to_operand_aliasing={{0}: (5, {})} | custom-call | flops 3489660928 | bytes 3702784 | tf_op jit(solution)/shard_map/correlate/pallas_call | solution.py:324
  243.5 4.0 %collective-permute-done.43.got_ref = bf16[32,32,512]{2,1,0:T(8,128)(2,1)} collective-permute-done((bf16[32,32,512]{2,1,0:T(8,128)(2,1)}, bf16[32,32,512]{2,1,0:T(8,128)(2,1)}, u32[]{:S(2)}, u32[]{:S(2)}) %collective-permute-start.43) | collective-permute-done | bytes 1048608 | tf_op jit(solution)/shard_map/ppermute | solution.py:377
  252.8 37.5 %collective-permute-done.40.refs_2_ = bf16[1568,384]{1,0:T(8,128)(2,1)} collective-permute-done((bf16[1568,384]{1,0:T(8,128)(2,1)}, bf16[1568,384]{1,0:T(8,128)(2,1)}, u32[]{:S(2)}, u32[]{:S(2)}) %collective-permute-start.40) | collective-permute-done | bytes 1204256 | tf_op jit(solution)/shard_map/ppermute | solution.py:377
  291.8 6.6 %correlate.35 = (f32[1,32,32,10240]{3,2,1,0:T(8,128)}, bf16[32,32,384]{2,1,0:T(8,128)(2,1)S(1)}) custom-call(s32[1]{0:T(128)} %bitcast.me_ref, bf16[1024,1664]{1,0:T(8,128)(2,1)S(1)} %hankel.3.refs_0_, bf16[1024,1664]{1,0:T(8,128)(2,1)S(1)} %hankel.2.refs_0_.refs_1_, ...), custom_call_target="tpu_custom_call", output_to_operand_aliasing={{0}: (5, {})} | custom-call | flops 2617245696 | bytes 2777088 | tf_op jit(solution)/shard_map/correlate/pallas_call | solution.py:324
  299.3 4.5 %correlate.24 = bf16[32,32,512]{2,1,0:T(8,128)(2,1)} custom-call(s32[1]{0:T(128)} %bitcast.me_ref, bf16[1024,1664]{1,0:T(8,128)(2,1)S(1)} %hankel.2.refs_0_.refs_1_, bf16[1568,512]{1,0:T(8,128)(2,1)} %collective-permute-done.23.refs_1_, bf16[1568,512]{1,0:T(8,128)(2,1)} %collective-permute-done.22.refs_2_), custom_call_target="tpu_custom_call" | custom-call | flops 1744830464 | bytes 3702784 | tf_op jit(solution)/shard_map/correlate/pallas_call | solution.py:324
  303.8 3.6 collective-permute-done.36.refs_2_
  308.3 3.6 correlate.36
  311.8 21.3 %collective-permute-done.19.refs_1_ = bf16[1568,384]{1,0:T(8,128)(2,1)S(1)} collective-permute-done((bf16[1568,384]{1,0:T(8,128)(2,1)S(1)}, bf16[1568,384]{1,0:T(8,128)(2,1)S(1)}, u32[]{:S(2)}, u32[]{:S(2)}) %collective-permute-start.19) | collective-permute-done | bytes 1204256 | tf_op jit(solution)/shard_map/ppermute | solution.py:377
  334.1 3.2 correlate.23
  339.8 3.6 correlate.37
  343.3 7.0 %collective-permute-done.13.refs_1_ = bf16[1568,256]{1,0:T(8,128)(2,1)S(1)} collective-permute-done((bf16[1568,256]{1,0:T(8,128)(2,1)S(1)}, bf16[1568,256]{1,0:T(8,128)(2,1)S(1)}, u32[]{:S(2)}, u32[]{:S(2)}) %collective-permute-start.13) | collective-permute-done | bytes 802848 | tf_op jit(solution)/shard_map/ppermute | solution.py:377
  359.8 12.8 %collective-permute-done.44.got_ref = bf16[32,32,128]{2,1,0:T(8,128)(2,1)S(1)} collective-permute-done((bf16[32,32,128]{2,1,0:T(8,128)(2,1)S(1)}, bf16[32,32,128]{2,1,0:T(8,128)(2,1)S(1)}, u32[]{:S(2)}, u32[]{:S(2)}) %collective-permute-start.44) | collective-permute-done | bytes 262176 | tf_op jit(solution)/shard_map/ppermute | solution.py:377
  373.4 4.6 %correlate.38.refs_3_ = f32[1,32,32,10240]{3,2,1,0:T(8,128)} custom-call(s32[1]{0:T(128)} %bitcast.me_ref, bf16[1024,1664]{1,0:T(8,128)(2,1)S(1)} %hankel.3.refs_0_, bf16[1568,512]{1,0:T(8,128)(2,1)} %collective-permute-done.23.refs_1_, bf16[1568,512]{1,0:T(8,128)(2,1)} %collective-permute-done.22.refs_2_, ...), custom_call_target="tpu_custom_call", output_to_operand_aliasing={{}: (4, {})} | custom-call | flops 1744830464 | bytes 3702784 | tf_op jit(solution)/shard_map/correlate/pallas_call | solution.py:324
  378.1 3.3 correlate.39.kept_ref
  (171 shorter events, 120.2 us)
Async XLA Ops:
  35.4 39.3 %collective-permute-start.29 = (bf16[1568,256]{1,0:T(8,128)(2,1)S(1)}, bf16[1568,256]{1,0:T(8,128)(2,1)S(1)}, u32[]{:S(2)}, u32[]{:S(2)}) collective-permute-start(bf16[1568,256]{1,0:T(8,128)(2,1)S(1)} %get-tuple-element.35.refs_2_.refs_1_), channel_id=1, source_target_pairs={{0,1},{1,0},{2,3},{3,2},{4,5},{5,4},{6,7},{7,6},{8,9},{9,8},{10,11... | collective-permute-start | bytes 2408456 | tf_op jit(solution)/shard_map/ppermute | solution.py:377
  36.9 42.7 %collective-permute-start.11 = (bf16[1568,256]{1,0:T(8,128)(2,1)S(1)}, bf16[1568,256]{1,0:T(8,128)(2,1)S(1)}, u32[]{:S(2)}, u32[]{:S(2)}) collective-permute-start(bf16[1568,256]{1,0:T(8,128)(2,1)S(1)} %get-tuple-element.35.refs_2_.refs_1_), channel_id=1, source_target_pairs={{0,2},{1,3},{2,0},{3,1},{4,6},{5,7},{6,4},{7,5},{8,10},{9,11},{10,... | collective-permute-start | bytes 2408456 | tf_op jit(solution)/shard_map/ppermute | solution.py:377
  37.6 29.4 %collective-permute-start.7 = (bf16[1568,128]{1,0:T(8,128)(2,1)S(1)}, bf16[1568,128]{1,0:T(8,128)(2,1)S(1)}, u32[]{:S(2)}, u32[]{:S(2)}) collective-permute-start(bf16[1568,128]{1,0:T(8,128)(2,1)S(1)} %get-tuple-element.36.refs_3_.refs_2_), channel_id=1, source_target_pairs={{0,2},{1,3},{2,0},{3,1},{4,6},{5,7},{6,4},{7,5},{8,10},{9,11},{10,... | collective-permute-start | bytes 1204232 | tf_op jit(solution)/shard_map/ppermute | solution.py:377
  41.3 40.4 %collective-permute-start.35 = (bf16[1568,256]{1,0:T(8,128)(2,1)S(1)}, bf16[1568,256]{1,0:T(8,128)(2,1)}, u32[]{:S(2)}, u32[]{:S(2)}) collective-permute-start(bf16[1568,256]{1,0:T(8,128)(2,1)S(1)} %get-tuple-element.35.refs_2_.refs_1_), channel_id=1, source_target_pairs={{2,4},{3,5},{4,2},{5,3},{10,12},{11,13},{12,10},{13,11},{18,20},{1... | collective-permute-start | bytes 2408456 | tf_op jit(solution)/shard_map/ppermute | solution.py:377
  42.8 27.9 %collective-permute-start.25 = (bf16[1568,128]{1,0:T(8,128)(2,1)S(1)}, bf16[1568,128]{1,0:T(8,128)(2,1)}, u32[]{:S(2)}, u32[]{:S(2)}) collective-permute-start(bf16[1568,128]{1,0:T(8,128)(2,1)S(1)} %get-tuple-element.36.refs_3_.refs_2_), channel_id=1, source_target_pairs={{2,4},{3,5},{4,2},{5,3},{10,12},{11,13},{12,10},{13,11},{18,20},{1... | collective-permute-start | bytes 1204232 | tf_op jit(solution)/shard_map/ppermute | solution.py:377
  70.7 73.8 %collective-permute-start.21 = (bf16[1568,512]{1,0:T(8,128)(2,1)}, bf16[1568,512]{1,0:T(8,128)(2,1)}, u32[]{:S(2)}, u32[]{:S(2)}) collective-permute-start(bf16[1568,512]{1,0:T(8,128)(2,1)} %get-tuple-element.34.refs_1_.refs_2_), channel_id=1, source_target_pairs={{0,2},{1,3},{2,0},{3,1},{4,6},{5,7},{6,4},{7,5},{8,10},{9,11},{10,... | collective-permute-start | bytes 4816904 | tf_op jit(solution)/shard_map/ppermute | solution.py:377
  72.1 45.4 %collective-permute-start.26 = (bf16[1568,128]{1,0:T(8,128)(2,1)}, bf16[1568,128]{1,0:T(8,128)(2,1)S(1)}, u32[]{:S(2)}, u32[]{:S(2)}) collective-permute-start(bf16[1568,128]{1,0:T(8,128)(2,1)} %collective-permute-done.25.refs_3_), channel_id=1, source_target_pairs={{2,0},{3,1},{4,6},{5,7},{10,8},{11,9},{12,14},{13,15},{18,16},{19,... | collective-permute-start | bytes 1204232 | tf_op jit(solution)/shard_map/ppermute | solution.py:377
  74.7 67.8 %collective-permute-start.15 = (bf16[1536,384]{1,0:T(8,128)(2,1)S(1)}, bf16[1536,384]{1,0:T(8,128)(2,1)S(1)}, u32[]{:S(2)}, u32[]{:S(2)}) collective-permute-start(bf16[1536,384]{1,0:T(8,128)(2,1)S(1)} %mask.1), channel_id=1, source_target_pairs={{0,2},{1,3},{2,0},{3,1},{4,6},{5,7},{6,4},{7,5},{8,10},{9,11},{10,... | collective-permute-start | bytes 3538952 | tf_op jit(solution)/shard_map/ppermute | solution.py:377
  79.6 66.7 %collective-permute-start.37 = (bf16[1536,384]{1,0:T(8,128)(2,1)S(1)}, bf16[1536,384]{1,0:T(8,128)(2,1)S(1)}, u32[]{:S(2)}, u32[]{:S(2)}) collective-permute-start(bf16[1536,384]{1,0:T(8,128)(2,1)S(1)} %mask.1), channel_id=1, source_target_pairs={{2,4},{3,5},{4,2},{5,3},{10,12},{11,13},{12,10},{13,11},{18,20},{1... | collective-permute-start | bytes 3538952 | tf_op jit(solution)/shard_map/ppermute | solution.py:377
  81.6 96.1 %collective-permute-start.27 = (bf16[1568,512]{1,0:T(8,128)(2,1)S(1)}, bf16[1568,512]{1,0:T(8,128)(2,1)S(1)}, u32[]{:S(2)}, u32[]{:S(2)}) collective-permute-start(bf16[1568,512]{1,0:T(8,128)(2,1)S(1)} %copy-done.1), channel_id=1, source_target_pairs={{2,4},{3,5},{4,2},{5,3},{10,12},{11,13},{12,10},{13,11},{18,20},{1... | collective-permute-start | bytes 4816904 | tf_op jit(solution)/shard_map/ppermute | solution.py:377
  141.9 35.2 %collective-permute-start.32 = (bf16[32,32,384]{2,1,0:T(8,128)(2,1)}, bf16[32,32,384]{2,1,0:T(8,128)(2,1)}, u32[]{:S(2)}, u32[]{:S(2)}) collective-permute-start(bf16[32,32,384]{2,1,0:T(8,128)(2,1)} %get-tuple-element.44), channel_id=1, source_target_pairs={{0,1},{1,0},{2,3},{3,2},{4,5},{5,4},{6,7},{7,6},{8,9},{9,8},{10,11... | collective-permute-start | bytes 2359304 | tf_op jit(solution)/shard_map/ppermute | solution.py:377
  142.4 24.0 %collective-permute-start.9 = (bf16[1568,128]{1,0:T(8,128)(2,1)S(1)}, bf16[1568,128]{1,0:T(8,128)(2,1)S(1)}, u32[]{:S(2)}, u32[]{:S(2)}) collective-permute-start(bf16[1568,128]{1,0:T(8,128)(2,1)S(1)} %collective-permute-done.8.refs_2_), channel_id=1, source_target_pairs={{2,0},{3,1},{4,6},{5,7},{10,8},{11,9},{12,14},{13,15},{18,16},{19,... | collective-permute-start | bytes 1204232 | tf_op jit(solution)/shard_map/ppermute | solution.py:377
  144.5 62.8 %collective-permute-start.22 = (bf16[1568,512]{1,0:T(8,128)(2,1)}, bf16[1568,512]{1,0:T(8,128)(2,1)}, u32[]{:S(2)}, u32[]{:S(2)}) collective-permute-start(bf16[1568,512]{1,0:T(8,128)(2,1)} %collective-permute-done.21.refs_2_), channel_id=1, source_target_pairs={{2,4},{3,5},{4,2},{5,3},{10,12},{11,13},{12,10},{13,11},{18,20},{1... | collective-permute-start | bytes 4816904 | tf_op jit(solution)/shard_map/ppermute | solution.py:377
  164.0 26.8 %collective-permute-start.33 = (bf16[32,32,512]{2,1,0:T(8,128)(2,1)}, bf16[32,32,512]{2,1,0:T(8,128)(2,1)}, u32[]{:S(2)}, u32[]{:S(2)}) collective-permute-start(bf16[32,32,512]{2,1,0:T(8,128)(2,1)} %get-tuple-element.45), channel_id=1, source_target_pairs={{0,1},{1,0},{2,3},{3,2},{4,5},{5,4},{6,7},{7,6},{8,9},{9,8},{10,11... | collective-permute-start | bytes 3145736 | tf_op jit(solution)/shard_map/ppermute | solution.py:377
  177.0 28.3 %collective-permute-start.30 = (bf16[32,32,384]{2,1,0:T(8,128)(2,1)S(1)}, bf16[32,32,384]{2,1,0:T(8,128)(2,1)S(1)}, u32[]{:S(2)}, u32[]{:S(2)}) collective-permute-start(bf16[32,32,384]{2,1,0:T(8,128)(2,1)S(1)} %get-tuple-element.42), channel_id=1, source_target_pairs={{0,1},{1,0},{2,3},{3,2},{4,5},{5,4},{6,7},{7,6},{8,9},{9,8},{10,11... | collective-permute-start | bytes 2359304 | tf_op jit(solution)/shard_map/ppermute | solution.py:377
  177.7 57.5 %collective-permute-start.28 = (bf16[1568,512]{1,0:T(8,128)(2,1)S(1)}, bf16[1568,512]{1,0:T(8,128)(2,1)}, u32[]{:S(2)}, u32[]{:S(2)}) collective-permute-start(bf16[1568,512]{1,0:T(8,128)(2,1)S(1)} %collective-permute-done.27.refs_3_), channel_id=1, source_target_pairs={{2,0},{3,1},{4,6},{5,7},{10,8},{11,9},{12,14},{13,15},{18,16},{19,... | collective-permute-start | bytes 4816904 | tf_op jit(solution)/shard_map/ppermute | solution.py:377
  186.3 47.6 %collective-permute-start.18 = (bf16[1568,384]{1,0:T(8,128)(2,1)S(1)}, bf16[1568,384]{1,0:T(8,128)(2,1)S(1)}, u32[]{:S(2)}, u32[]{:S(2)}) collective-permute-start(bf16[1568,384]{1,0:T(8,128)(2,1)S(1)} %normalize.4.refs_2_), channel_id=1, source_target_pairs={{2,4},{3,5},{4,2},{5,3},{10,12},{11,13},{12,10},{13,11},{18,20},{1... | collective-permute-start | bytes 3612680 | tf_op jit(solution)/shard_map/ppermute | solution.py:377
  190.8 34.6 %collective-permute-start.42 = (bf16[32,32,256]{2,1,0:T(8,128)(2,1)}, bf16[32,32,256]{2,1,0:T(8,128)(2,1)S(1)}, u32[]{:S(2)}, u32[]{:S(2)}) collective-permute-start(bf16[32,32,256]{2,1,0:T(8,128)(2,1)} %get-tuple-element.52), channel_id=1, source_target_pairs={{0,1},{1,0},{2,3},{3,2},{4,5},{5,4},{6,7},{7,6},{8,9},{9,8},{10,11... | collective-permute-start | bytes 1572872 | tf_op jit(solution)/shard_map/ppermute | solution.py:377
  207.3 91.1 %collective-permute-start.23 = (bf16[1568,512]{1,0:T(8,128)(2,1)}, bf16[1568,512]{1,0:T(8,128)(2,1)}, u32[]{:S(2)}, u32[]{:S(2)}) collective-permute-start(bf16[1568,512]{1,0:T(8,128)(2,1)} %collective-permute-done.22.refs_2_), channel_id=1, source_target_pairs={{2,0},{3,1},{4,6},{5,7},{10,8},{11,9},{12,14},{13,15},{18,16},{19,... | collective-permute-start | bytes 4816904 | tf_op jit(solution)/shard_map/ppermute | solution.py:377
  222.2 25.3 %collective-permute-start.43 = (bf16[32,32,512]{2,1,0:T(8,128)(2,1)}, bf16[32,32,512]{2,1,0:T(8,128)(2,1)}, u32[]{:S(2)}, u32[]{:S(2)}) collective-permute-start(bf16[32,32,512]{2,1,0:T(8,128)(2,1)} %get-tuple-element.53), channel_id=1, source_target_pairs={{0,1},{1,0},{2,3},{3,2},{4,5},{5,4},{6,7},{7,6},{8,9},{9,8},{10,11... | collective-permute-start | bytes 3145736 | tf_op jit(solution)/shard_map/ppermute | solution.py:377
  225.4 64.9 %collective-permute-start.40 = (bf16[1568,384]{1,0:T(8,128)(2,1)}, bf16[1568,384]{1,0:T(8,128)(2,1)}, u32[]{:S(2)}, u32[]{:S(2)}) collective-permute-start(bf16[1568,384]{1,0:T(8,128)(2,1)} %normalize.5.refs_3_), channel_id=1, source_target_pairs={{2,0},{3,1},{4,6},{5,7},{10,8},{11,9},{12,14},{13,15},{18,16},{19,... | collective-permute-start | bytes 3612680 | tf_op jit(solution)/shard_map/ppermute | solution.py:377
  233.9 73.5 %collective-permute-start.36 = (bf16[1568,256]{1,0:T(8,128)(2,1)}, bf16[1568,256]{1,0:T(8,128)(2,1)S(1)}, u32[]{:S(2)}, u32[]{:S(2)}) collective-permute-start(bf16[1568,256]{1,0:T(8,128)(2,1)} %collective-permute-done.35.refs_3_), channel_id=1, source_target_pairs={{2,0},{3,1},{4,6},{5,7},{10,8},{11,9},{12,14},{13,15},{18,16},{19,... | collective-permute-start | bytes 2408456 | tf_op jit(solution)/shard_map/ppermute | solution.py:377
  235.2 98.0 %collective-permute-start.19 = (bf16[1568,384]{1,0:T(8,128)(2,1)S(1)}, bf16[1568,384]{1,0:T(8,128)(2,1)S(1)}, u32[]{:S(2)}, u32[]{:S(2)}) collective-permute-start(bf16[1568,384]{1,0:T(8,128)(2,1)S(1)} %collective-permute-done.18.refs_2_), channel_id=1, source_target_pairs={{2,0},{3,1},{4,6},{5,7},{10,8},{11,9},{12,14},{13,15},{18,16},{19,... | collective-permute-start | bytes 3612680 | tf_op jit(solution)/shard_map/ppermute | solution.py:377
  247.4 89.8 %collective-permute-start.34 = (bf16[32,32,512]{2,1,0:T(8,128)(2,1)S(1)}, bf16[32,32,512]{2,1,0:T(8,128)(2,1)S(1)}, u32[]{:S(2)}, u32[]{:S(2)}) collective-permute-start(bf16[32,32,512]{2,1,0:T(8,128)(2,1)S(1)} %get-tuple-element.50), channel_id=1, source_target_pairs={{0,1},{1,0},{2,3},{3,2},{4,5},{5,4},{6,7},{7,6},{8,9},{9,8},{10,11... | collective-permute-start | bytes 3145736 | tf_op jit(solution)/shard_map/ppermute | solution.py:377
  290.2 60.1 %collective-permute-start.13 = (bf16[1568,256]{1,0:T(8,128)(2,1)S(1)}, bf16[1568,256]{1,0:T(8,128)(2,1)S(1)}, u32[]{:S(2)}, u32[]{:S(2)}) collective-permute-start(bf16[1568,256]{1,0:T(8,128)(2,1)S(1)} %copy-done.3), channel_id=1, source_target_pairs={{2,0},{3,1},{4,6},{5,7},{10,8},{11,9},{12,14},{13,15},{18,16},{19,... | collective-permute-start | bytes 2408456 | tf_op jit(solution)/shard_map/ppermute | solution.py:377
  298.4 55.1 %collective-permute-start.46 = (bf16[32,32,384]{2,1,0:T(8,128)(2,1)S(1)}, bf16[32,32,384]{2,1,0:T(8,128)(2,1)S(1)}, u32[]{:S(2)}, u32[]{:S(2)}) collective-permute-start(bf16[32,32,384]{2,1,0:T(8,128)(2,1)S(1)} %get-tuple-element.59), channel_id=1, source_target_pairs={{0,1},{1,0},{2,3},{3,2},{4,5},{5,4},{6,7},{7,6},{8,9},{9,8},{10,11... | collective-permute-start | bytes 2359304 | tf_op jit(solution)/shard_map/ppermute | solution.py:377
  307.3 74.0 %collective-permute-start.24 = (bf16[32,32,512]{2,1,0:T(8,128)(2,1)}, bf16[32,32,512]{2,1,0:T(8,128)(2,1)}, u32[]{:S(2)}, u32[]{:S(2)}) collective-permute-start(bf16[32,32,512]{2,1,0:T(8,128)(2,1)} %correlate.24), channel_id=1, source_target_pairs={{0,1},{1,0},{2,3},{3,2},{4,5},{5,4},{6,7},{7,6},{8,9},{9,8},{10,11... | collective-permute-start | bytes 3145736 | tf_op jit(solution)/shard_map/ppermute | solution.py:377
  333.1 24.7 %collective-permute-start.45 = (bf16[32,32,256]{2,1,0:T(8,128)(2,1)S(1)}, bf16[32,32,256]{2,1,0:T(8,128)(2,1)S(1)}, u32[]{:S(2)}, u32[]{:S(2)}) collective-permute-start(bf16[32,32,256]{2,1,0:T(8,128)(2,1)S(1)} %get-tuple-element.58), channel_id=1, source_target_pairs={{0,1},{1,0},{2,3},{3,2},{4,5},{5,4},{6,7},{7,6},{8,9},{9,8},{10,11... | collective-permute-start | bytes 1572872 | tf_op jit(solution)/shard_map/ppermute | solution.py:377
  337.3 50.9 %collective-permute-start.20 = (bf16[32,32,384]{2,1,0:T(8,128)(2,1)}, bf16[32,32,384]{2,1,0:T(8,128)(2,1)}, u32[]{:S(2)}, u32[]{:S(2)}) collective-permute-start(bf16[32,32,384]{2,1,0:T(8,128)(2,1)} %correlate.23), channel_id=1, source_target_pairs={{0,1},{1,0},{2,3},{3,2},{4,5},{5,4},{6,7},{7,6},{8,9},{9,8},{10,11... | collective-permute-start | bytes 2359304 | tf_op jit(solution)/shard_map/ppermute | solution.py:377
  350.4 22.3 %collective-permute-start.44 = (bf16[32,32,128]{2,1,0:T(8,128)(2,1)S(1)}, bf16[32,32,128]{2,1,0:T(8,128)(2,1)S(1)}, u32[]{:S(2)}, u32[]{:S(2)}) collective-permute-start(bf16[32,32,128]{2,1,0:T(8,128)(2,1)S(1)} %get-tuple-element.57), channel_id=1, source_target_pairs={{0,1},{1,0},{2,3},{3,2},{4,5},{5,4},{6,7},{7,6},{8,9},{9,8},{10,11... | collective-permute-start | bytes 786440 | tf_op jit(solution)/shard_map/ppermute | solution.py:377
  353.4 36.9 %collective-permute-start.14 = (bf16[32,32,256]{2,1,0:T(8,128)(2,1)}, bf16[32,32,256]{2,1,0:T(8,128)(2,1)}, u32[]{:S(2)}, u32[]{:S(2)}) collective-permute-start(bf16[32,32,256]{2,1,0:T(8,128)(2,1)} %correlate.22), channel_id=1, source_target_pairs={{0,1},{1,0},{2,3},{3,2},{4,5},{5,4},{6,7},{7,6},{8,9},{9,8},{10,11... | collective-permute-start | bytes 1572872 | tf_op jit(solution)/shard_map/ppermute | solution.py:377
  357.8 34.5 %collective-permute-start.10 = (bf16[32,32,128]{2,1,0:T(8,128)(2,1)}, bf16[32,32,128]{2,1,0:T(8,128)(2,1)}, u32[]{:S(2)}, u32[]{:S(2)}) collective-permute-start(bf16[32,32,128]{2,1,0:T(8,128)(2,1)} %correlate.21), channel_id=1, source_target_pairs={{0,1},{1,0},{2,3},{3,2},{4,5},{5,4},{6,7},{7,6},{8,9},{9,8},{10,11... | collective-permute-start | bytes 786440 | tf_op jit(solution)/shard_map/ppermute | solution.py:377
  (42 other events, 414.0 us)
